TPU v7x, 256 devices: a whole 4x4x8 slice. The times are simulated.
256 devices in a mesh: ctx: 64 (over y, x, z_lo), dp: 4 (over z_hi, core).
Axes of the slice: x: 4, y: 4, z: 8 (z_hi: 2, z_lo: 4; z = z_hi * 4 + z_lo), core: 2. Of those that a mesh axis runs over, the one named last changes fastest.
Arguments:
- query: bfloat16 [4, 8192, 512], P('dp', 'ctx'), may hold values from -6 to 6
- key_input: bfloat16 [4, 8192, 512], P('dp', 'ctx'), may hold values from -6 to 6
- value_input: bfloat16 [4, 8192, 512], P('dp', 'ctx'), may hold values from -6 to 6
- filter_taps: float32 [8192, 512], P('ctx'), may hold values from -6 to 6
- grad_output: bfloat16 [4, 8192, 512], P('dp', 'ctx'), may hold values from -6 to 6
Outputs:
- output: bfloat16 [4, 8192, 512], P('dp', 'ctx')
- grad_query: bfloat16 [4, 8192, 512], P('dp', 'ctx')
- grad_key: bfloat16 [4, 8192, 512], P('dp', 'ctx')
- grad_value: bfloat16 [4, 8192, 512], P('dp', 'ctx')
- grad_filter: float32 [8192, 512], P('ctx')
All inputs are finite; a program needn't handle non-finite values.
Results may differ from a plain program's by a relative error of at most 0.0058.
Values may be sent and summed in bfloat16 or wider, within the bound.
No kernel may reach another device: no remote copies, remote signals or barrier semaphores. Data moves between devices by JAX's collectives and lax.ppermute only.
A program may use at most 64 MiB of HBM per device.

v0:
```python
import functools

import jax
import jax.numpy as jnp
import ml_dtypes
import numpy as np
from jax import lax
from jax.experimental import pallas as pl
from jax.experimental.pallas import tpu as pltpu
from jax.sharding import PartitionSpec as P

BF16 = jnp.bfloat16
F32 = jnp.float32

BLOCKS = 64
LANES = 128
ROWS = 128
HALF = 64
SEQS = 4
C = 512
OWNERS = 256
OWNED = C // OWNERS
KINDS = 3
CHUNK = KINDS * OWNED
GROUP = 16
TILE = GROUP * SEQS * CHUNK


def two_terms(table):
    high = table.astype(ml_dtypes.bfloat16)
    low = (table - high.astype(np.float64)).astype(ml_dtypes.bfloat16)
    return high, low


def tables():
    k1 = np.arange(HALF)[:, None] + 0.5
    angle1 = 2.0 * np.pi * k1 * np.arange(BLOCKS)[None, :] / ROWS
    first = np.concatenate([np.cos(angle1), -np.sin(angle1)], axis=0)
    first_high, first_low = two_terms(first)
    first_signal = np.concatenate([first_high, first_low], axis=1)
    first_filter = np.concatenate([first_high, first_low, first_high, first_high], axis=1)
    angle_t = 2.0 * np.pi * k1 * np.arange(LANES)[None, :] / (ROWS * LANES)
    twist = np.concatenate([np.cos(angle_t), -np.sin(angle_t)], axis=0).astype(np.float32)
    index = np.arange(LANES)
    angle2 = 2.0 * np.pi * ((index[:, None] * index[None, :]) % LANES) / LANES
    cos2, sin2 = np.cos(angle2), np.sin(angle2)
    second = np.block([[cos2, -sin2], [sin2, cos2]])
    second_back = np.block([[cos2, sin2], [-sin2, cos2]])
    last = np.concatenate([np.cos(angle1.T), -np.sin(angle1.T)], axis=1) * (2.0 / (ROWS * LANES))
    last_high, last_low = two_terms(last)
    last_stack = np.concatenate([last_high, last_high, last_low], axis=1)
    row = np.arange(CHUNK * HALF)
    pick = np.zeros((CHUNK * HALF, KINDS * LANES))
    pick[row, (row % CHUNK // OWNED) * LANES + OWNED * (row // CHUNK) + row % OWNED] = 1.0
    line = np.arange(TILE)
    block = line // (SEQS * CHUNK)
    seq = line % (SEQS * CHUNK) // CHUNK
    kind = line % CHUNK // OWNED
    own = line % OWNED
    order = np.zeros((TILE, TILE))
    order[((kind * OWNED + own) * SEQS + seq) * GROUP + block, line] = 1.0
    return (
        pick.astype(ml_dtypes.bfloat16),
        order.astype(ml_dtypes.bfloat16),
        np.ascontiguousarray(order.T).astype(ml_dtypes.bfloat16),
        first_signal,
        first_filter,
        twist,
        np.stack(two_terms(second)),
        np.stack(two_terms(second_back)),
        last_stack,
    )


def mm(a, b, dims=((1,), (0,))):
    return lax.dot_general(a, b, (dims, ((), ())), preferred_element_type=F32)


def pack_kernel(q_ref, k_ref, v_ref, f_ref, g_ref, pick_ref, out_ref):
    term = lax.axis_index("dp")
    product = (k_ref[0].astype(F32) * v_ref[0].astype(F32)).astype(BF16)
    grad_mix = (g_ref[0].astype(F32) * q_ref[0].astype(F32)).astype(BF16)
    taps = f_ref[...]
    high = taps.astype(BF16).astype(F32)
    rest = taps - high
    middle = rest.astype(BF16).astype(F32)
    part = jnp.where(term == 0, high, jnp.where(term == 1, middle, rest - middle)).astype(BF16)
    pick = pick_ref[...]
    for b in range(C // LANES):
        cols = slice(b * LANES, (b + 1) * LANES)
        data = jnp.concatenate([product[:, cols], grad_mix[:, cols], part[:, cols]], axis=1)
        rows = mm(pick, data, ((1,), (1,)))
        out_ref[b * CHUNK * HALF : (b + 1) * CHUNK * HALF, :] = rows.astype(BF16)


def unpack_kernel(q_ref, k_ref, v_ref, g_ref, got_ref, pick_ref, o_ref, gq_ref, gk_ref, gv_ref, gf_ref):
    pick = pick_ref[...]
    for b in range(C // LANES):
        cols = slice(b * LANES, (b + 1) * LANES)
        got = got_ref[b * CHUNK * HALF : (b + 1) * CHUNK * HALF, :]
        data = mm(got, pick, ((0,), (0,)))
        mixed = data[:, :LANES]
        back = data[:, LANES : 2 * LANES]
        gf_ref[:, cols] = data[:, 2 * LANES :]
        o_ref[0, :, cols] = (q_ref[0, :, cols].astype(F32) * mixed).astype(BF16)
        gq_ref[0, :, cols] = (g_ref[0, :, cols].astype(F32) * mixed).astype(BF16)
        gk_ref[0, :, cols] = (back * v_ref[0, :, cols].astype(F32)).astype(BF16)
        gv_ref[0, :, cols] = (back * k_ref[0, :, cols].astype(F32)).astype(BF16)


def split(x):
    high = x.astype(BF16)
    low = (x - high.astype(F32)).astype(BF16)
    return high, low


def conv_kernel(
    got_ref,
    order_ref,
    back_ref,
    fs_ref,
    ff_ref,
    tw_ref,
    sec_ref,
    secb_ref,
    last_ref,
    out_ref,
    sig_ref,
    spec_ref,
    fin_ref,
):
    order = order_ref[...]
    n_sig = KINDS * OWNED * SEQS
    for h in range(2):
        lo = 2 * h * TILE
        data = jnp.concatenate([got_ref[lo : lo + TILE, :], got_ref[lo + TILE : lo + 2 * TILE, :]], axis=1)
        sorted_rows = mm(order, data).astype(BF16)
        for s in range(n_sig):
            for u in range(2):
                at = (2 * h + u) * GROUP
                sig_ref[at : at + GROUP, s * LANES : (s + 1) * LANES] = sorted_rows[
                    s * GROUP : (s + 1) * GROUP, u * LANES : (u + 1) * LANES
                ]

    def sig(s):
        return sig_ref[:, s * LANES : (s + 1) * LANES]

    wr = tw_ref[:HALF, :]
    wi = tw_ref[HALF:, :]

    def spectra(first):
        halves = []
        for u in range(2):
            ar = first[:HALF, u * LANES : (u + 1) * LANES]
            ai = first[HALF:, u * LANES : (u + 1) * LANES]
            halves.append(jnp.concatenate([ar * wr - ai * wi, ar * wi + ai * wr], axis=1))
        high, low = split(jnp.concatenate(halves, axis=0))
        return mm(high, sec_ref[0]) + mm(low, sec_ref[0]) + mm(high, sec_ref[1])

    for p in range(KINDS * OWNED * SEQS // 2 - OWNED * SEQS // 2):
        data = sig_ref[:, 2 * p * LANES : 2 * (p + 1) * LANES]
        first = mm(fs_ref[...], jnp.concatenate([data, data], axis=0))
        spec_ref[2 * p * HALF : 2 * (p + 1) * HALF, :] = spectra(first)

    base = 2 * OWNED * SEQS
    terms = [
        jnp.concatenate([sig(base + own * SEQS + term) for own in range(OWNED)], axis=1) for term in range(3)
    ]
    first = mm(ff_ref[...], jnp.concatenate([terms[0], terms[0], terms[1], terms[2]], axis=0))
    filter_spec = spectra(first)

    def inverse(pair):
        high, low = split(jnp.concatenate(pair, axis=0))
        full = mm(high, secb_ref[0]) + mm(low, secb_ref[0]) + mm(high, secb_ref[1])
        cols = []
        for u in range(2):
            br = full[u * HALF : (u + 1) * HALF, :LANES]
            bi = full[u * HALF : (u + 1) * HALF, LANES:]
            cols.append(jnp.concatenate([br * wr + bi * wi, bi * wr - br * wi], axis=0))
        high, low = split(jnp.concatenate(cols, axis=1))
        return mm(last_ref[...], jnp.concatenate([high, low, high], axis=0))

    def keep(s, values):
        values = values.astype(BF16)
        for b in range(BLOCKS // GROUP):
            fin_ref[b // 2, s * GROUP : (s + 1) * GROUP, (b % 2) * LANES : (b % 2 + 1) * LANES] = values[
                b * GROUP : (b + 1) * GROUP, :
            ]

    taps = []
    for own in range(OWNED):
        hr = filter_spec[own * HALF : (own + 1) * HALF, :LANES]
        hi = filter_spec[own * HALF : (own + 1) * HALF, LANES:]
        qr = jnp.zeros((HALF, LANES), F32)
        qi = jnp.zeros((HALF, LANES), F32)
        for half in range(SEQS // 2):
            mixed_pair, back_pair = [], []
            for u in range(2):
                s = own * SEQS + 2 * half + u
                pr = spec_ref[s * HALF : (s + 1) * HALF, :LANES]
                pi = spec_ref[s * HALF : (s + 1) * HALF, LANES:]
                z = OWNED * SEQS + s
                gr = spec_ref[z * HALF : (z + 1) * HALF, :LANES]
                gi = spec_ref[z * HALF : (z + 1) * HALF, LANES:]
                mixed_pair.append(jnp.concatenate([hr * pr - hi * pi, hr * pi + hi * pr], axis=1))
                back_pair.append(jnp.concatenate([gr * hr + gi * hi, gi * hr - gr * hi], axis=1))
                qr = qr + (gr * pr + gi * pi)
                qi = qi + (gi * pr - gr * pi)
            for kind, pair in ((0, mixed_pair), (1, back_pair)):
                res = inverse(pair)
                for u in range(2):
                    keep((kind * OWNED + own) * SEQS + 2 * half + u, res[:, u * LANES : (u + 1) * LANES])
        taps.append(jnp.concatenate([qr, qi], axis=1))
    res = inverse(taps)
    for own in range(OWNED):
        for d in range(SEQS):
            keep((2 * OWNED + own) * SEQS + d, res[:, own * LANES : (own + 1) * LANES])

    back = back_ref[...]
    for h in range(2):
        rows = mm(back, fin_ref[h]).astype(BF16)
        lo = 2 * h * TILE
        out_ref[lo : lo + TILE, :] = rows[:, :LANES]
        out_ref[lo + TILE : lo + 2 * TILE, :] = rows[:, LANES:]


def exchange(rows):
    parts = rows.reshape(OWNERS * KINDS, OWNED, LANES)
    parts = lax.all_to_all(parts, ("ctx", "dp"), split_axis=0, concat_axis=0, tiled=True)
    return parts.reshape(OWNERS * CHUNK, LANES)


def local(query, key_input, value_input, filter_taps, grad_output):
    pick, order, back, first_signal, first_filter, twist, second, second_back, last = tables()
    rows = jax.ShapeDtypeStruct((OWNERS * CHUNK, LANES), BF16)
    limit = pltpu.CompilerParams(vmem_limit_bytes=32 * 1024 * 1024)
    sent = pl.pallas_call(pack_kernel, out_shape=rows, compiler_params=limit, name="pack")(
        query, key_input, value_input, filter_taps, grad_output, pick
    )
    got = exchange(sent)
    results = pl.pallas_call(
        conv_kernel,
        out_shape=rows,
        scratch_shapes=[
            pltpu.VMEM((BLOCKS, KINDS * OWNED * SEQS * LANES), BF16),
            pltpu.VMEM((2 * OWNED * SEQS * HALF, 2 * LANES), F32),
            pltpu.VMEM((2, TILE, 2 * LANES), BF16),
        ],
        compiler_params=limit,
        name="conv",
    )(got, order, back, first_signal, first_filter, twist, second, second_back, last)
    returned = exchange(results)
    like = jax.ShapeDtypeStruct(query.shape, BF16)
    return pl.pallas_call(
        unpack_kernel,
        out_shape=(like, like, like, like, jax.ShapeDtypeStruct(filter_taps.shape, F32)),
        compiler_params=limit,
        name="unpack",
    )(query, key_input, value_input, grad_output, returned, pick)


def solution(mesh):
    shared = P("dp", "ctx", None)
    taps = P("ctx", None)
    return jax.shard_map(
        local,
        mesh=mesh,
        in_specs=(shared, shared, shared, taps, shared),
        out_specs=(shared, shared, shared, shared, taps),
        check_vma=False,
    )
```

profile of v0, /device:TPU:1, one launch (start us, length us, event | category | flops | bytes accessed | tf_op | source)
XLA Modules:
  0.0 71.0 jit_solution(17120773692019581602)
XLA Ops:
  0.6 0.0 copy-start
  0.6 1.0 %copy-done = bf16[384,384]{1,0:T(8,128)(2,1)S(1)} copy-done((bf16[384,384]{1,0:T(8,128)(2,1)S(1)}, bf16[384,384]{1,0:T(8,128)(2,1)}, u32[]{:S(2)}) %copy-start) | copy-done | bytes 294936
  1.6 0.9 %copy-done.2 = bf16[1,128,512]{2,1,0:T(8,128)(2,1)S(1)} copy-done((bf16[1,128,512]{2,1,0:T(8,128)(2,1)S(1)}, bf16[1,128,512]{2,1,0:T(8,128)(2,1)}, u32[]{:S(2)}) %copy-start.2) | copy-done | bytes 131096
  2.5 0.9 %copy-done.4 = bf16[1,128,512]{2,1,0:T(8,128)(2,1)S(1)} copy-done((bf16[1,128,512]{2,1,0:T(8,128)(2,1)S(1)}, bf16[1,128,512]{2,1,0:T(8,128)(2,1)}, u32[]{:S(2)}) %copy-start.4) | copy-done | bytes 131096
  3.4 0.9 %copy-done.6 = bf16[1,128,512]{2,1,0:T(8,128)(2,1)S(1)} copy-done((bf16[1,128,512]{2,1,0:T(8,128)(2,1)S(1)}, bf16[1,128,512]{2,1,0:T(8,128)(2,1)}, u32[]{:S(2)}) %copy-start.6) | copy-done | bytes 131096
  4.3 0.9 %copy-done.8 = bf16[1,128,512]{2,1,0:T(8,128)(2,1)S(1)} copy-done((bf16[1,128,512]{2,1,0:T(8,128)(2,1)S(1)}, bf16[1,128,512]{2,1,0:T(8,128)(2,1)}, u32[]{:S(2)}) %copy-start.8) | copy-done | bytes 131096
  5.2 0.9 %copy-done.12 = f32[128,512]{1,0:T(8,128)S(1)} copy-done((f32[128,512]{1,0:T(8,128)S(1)}, f32[128,512]{1,0:T(8,128)}, u32[]{:S(2)}) %copy-start.12) | copy-done | bytes 262168
  6.2 0.5 pack.1
  6.7 0.0 copy-start.10
  6.7 0.0 copy-start.11
  6.7 0.0 copy-start.15
  6.7 0.0 copy-start.16
  6.7 0.0 copy-start.17
  6.7 34.0 %all_to_all.10 = bf16[768,2,128]{2,1,0:T(2,128)(2,1)S(1)} all-to-all(bf16[768,2,128]{2,1,0:T(2,128)(2,1)S(1)} %bitcast.7), channel_id=1, replica_groups=mesh['ctx'=64,'dp'=4] {'ctx','dp'}, dimensions={0} | all-to-all | bytes 786432 | tf_op jit(solution)/shard_map/all_to_all | solution.py:229
  40.8 0.0 copy-done.13
  40.8 0.0 copy-done.14
  40.8 0.0 copy-done.18
  40.8 0.0 copy-done.10
  40.8 0.0 copy-done.11
  40.8 0.0 copy-done.15
  40.8 0.0 copy-done.16
  40.8 0.0 copy-done.17
  40.8 0.0 copy-start.9
  40.9 4.5 %conv.1 = bf16[1536,128]{1,0:T(8,128)(2,1)S(1)} custom-call(bf16[1536,128]{1,0:T(8,128)(2,1)S(1)} %bitcast.4, bf16[384,384]{1,0:T(8,128)(2,1)S(1)} %copy-done.11, bf16[384,384]{1,0:T(8,128)(2,1)S(1)} %copy-done.10, bf16[128,128]{1,0:T(8,128)(2,1)S(1)} %copy-done.18, bf16[128,256]{1,0:T(8,128)(2,1)S(1)} %copy-done.16, f32[128,128]{1,0:T(8,128)S(1)} %copy-done.15, ...), custom_call_target="tpu_custom_call" | custom-call | tf_op jit(solution)/shard_map/conv/pallas_call | solution.py:241
  45.4 0.0 copy-start.1
  45.4 0.0 copy-start.3
  45.4 0.0 copy-start.5
  45.4 0.0 copy-start.7
  45.4 24.2 %all_to_all.11 = bf16[768,2,128]{2,1,0:T(2,128)(2,1)S(1)} all-to-all(bf16[768,2,128]{2,1,0:T(2,128)(2,1)S(1)} %bitcast.5), channel_id=1, replica_groups=mesh['ctx'=64,'dp'=4] {'ctx','dp'}, dimensions={0} | all-to-all | bytes 786432 | tf_op jit(solution)/shard_map/all_to_all | solution.py:229
  69.6 0.0 copy-done.9
  69.6 0.0 copy-done.1
  69.6 1.3 %unpack.1 = (bf16[1,128,512]{2,1,0:T(8,128)(2,1)}, bf16[1,128,512]{2,1,0:T(8,128)(2,1)}, bf16[1,128,512]{2,1,0:T(8,128)(2,1)}, bf16[1,128,512]{2,1,0:T(8,128)(2,1)}, f32[128,512]{1,0:T(8,128)}) custom-call(bf16[1,128,512]{2,1,0:T(8,128)(2,1)S(1)} %copy-done.3, bf16[1,128,512]{2,1,0:T(8,128)(2,1)S(1)} %copy-done.5, bf16[1,128,512]{2,1,0:T(8,128)(2,1)S(1)} %copy-done.7, ...), custom_call_target="tpu_custom_call" | custom-call | tf_op jit(solution)/shard_map/unpack/pallas_call | solution.py:254
  (11 shorter events, 0.0 us)
Async XLA Ops:
  0.6 1.0 %copy-start = (bf16[384,384]{1,0:T(8,128)(2,1)S(1)}, bf16[384,384]{1,0:T(8,128)(2,1)}, u32[]{:S(2)}) copy-start(bf16[384,384]{1,0:T(8,128)(2,1)} %constant.18.clone.pick_ref) | copy-start | bytes 884740
  1.6 0.9 %copy-start.2 = (bf16[1,128,512]{2,1,0:T(8,128)(2,1)S(1)}, bf16[1,128,512]{2,1,0:T(8,128)(2,1)}, u32[]{:S(2)}) copy-start(bf16[1,128,512]{2,1,0:T(8,128)(2,1)} %q_ref.3) | copy-start | bytes 393220
  2.5 0.9 %copy-start.4 = (bf16[1,128,512]{2,1,0:T(8,128)(2,1)S(1)}, bf16[1,128,512]{2,1,0:T(8,128)(2,1)}, u32[]{:S(2)}) copy-start(bf16[1,128,512]{2,1,0:T(8,128)(2,1)} %k_ref.3) | copy-start | bytes 393220
  3.4 0.9 %copy-start.6 = (bf16[1,128,512]{2,1,0:T(8,128)(2,1)S(1)}, bf16[1,128,512]{2,1,0:T(8,128)(2,1)}, u32[]{:S(2)}) copy-start(bf16[1,128,512]{2,1,0:T(8,128)(2,1)} %v_ref.3) | copy-start | bytes 393220
  4.3 0.9 %copy-start.8 = (bf16[1,128,512]{2,1,0:T(8,128)(2,1)S(1)}, bf16[1,128,512]{2,1,0:T(8,128)(2,1)}, u32[]{:S(2)}) copy-start(bf16[1,128,512]{2,1,0:T(8,128)(2,1)} %g_ref.3) | copy-start | bytes 393220
  5.2 0.9 %copy-start.12 = (f32[128,512]{1,0:T(8,128)S(1)}, f32[128,512]{1,0:T(8,128)}, u32[]{:S(2)}) copy-start(f32[128,512]{1,0:T(8,128)} %f_ref.1) | copy-start | bytes 786436
  6.2 34.6 %copy-start.13 = (bf16[2,256,256]{2,1,0:T(8,128)(2,1)S(1)}, bf16[2,256,256]{2,1,0:T(8,128)(2,1)}, u32[]{:S(2)}) copy-start(bf16[2,256,256]{2,1,0:T(8,128)(2,1)} %constant.25.clone.secb_ref) | copy-start | bytes 786436
  6.2 34.6 %copy-start.14 = (bf16[2,256,256]{2,1,0:T(8,128)(2,1)S(1)}, bf16[2,256,256]{2,1,0:T(8,128)(2,1)}, u32[]{:S(2)}) copy-start(bf16[2,256,256]{2,1,0:T(8,128)(2,1)} %constant.24.clone.sec_ref) | copy-start | bytes 786436
  6.2 34.6 %copy-start.18 = (bf16[128,128]{1,0:T(8,128)(2,1)S(1)}, bf16[128,128]{1,0:T(8,128)(2,1)}, u32[]{:S(2)}) copy-start(bf16[128,128]{1,0:T(8,128)(2,1)} %constant.21.clone.fs_ref) | copy-start | bytes 98308
  6.7 34.1 %copy-start.10 = (bf16[384,384]{1,0:T(8,128)(2,1)S(1)}, bf16[384,384]{1,0:T(8,128)(2,1)}, u32[]{:S(2)}) copy-start(bf16[384,384]{1,0:T(8,128)(2,1)} %constant.20.clone.back_ref) | copy-start | bytes 884740
  6.7 34.1 %copy-start.11 = (bf16[384,384]{1,0:T(8,128)(2,1)S(1)}, bf16[384,384]{1,0:T(8,128)(2,1)}, u32[]{:S(2)}) copy-start(bf16[384,384]{1,0:T(8,128)(2,1)} %constant.19.clone.order_ref) | copy-start | bytes 884740
  6.7 34.1 %copy-start.15 = (f32[128,128]{1,0:T(8,128)S(1)}, f32[128,128]{1,0:T(8,128)}, u32[]{:S(2)}) copy-start(f32[128,128]{1,0:T(8,128)} %constant.23.clone.tw_ref) | copy-start | bytes 196612
  6.7 34.1 %copy-start.16 = (bf16[128,256]{1,0:T(8,128)(2,1)S(1)}, bf16[128,256]{1,0:T(8,128)(2,1)}, u32[]{:S(2)}) copy-start(bf16[128,256]{1,0:T(8,128)(2,1)} %constant.22.clone.ff_ref) | copy-start | bytes 196612
  6.7 34.1 %copy-start.17 = (bf16[64,384]{1,0:T(8,128)(2,1)S(1)}, bf16[64,384]{1,0:T(8,128)(2,1)}, u32[]{:S(2)}) copy-start(bf16[64,384]{1,0:T(8,128)(2,1)} %constant.26.clone.last_ref) | copy-start | bytes 147460
  40.8 28.8 %copy-start.9 = (bf16[1,128,512]{2,1,0:T(8,128)(2,1)S(1)}, bf16[1,128,512]{2,1,0:T(8,128)(2,1)}, u32[]{:S(2)}) copy-start(bf16[1,128,512]{2,1,0:T(8,128)(2,1)} %g_ref.3) | copy-start | bytes 393220
  45.4 24.2 %copy-start.1 = (bf16[384,384]{1,0:T(8,128)(2,1)S(1)}, bf16[384,384]{1,0:T(8,128)(2,1)}, u32[]{:S(2)}) copy-start(bf16[384,384]{1,0:T(8,128)(2,1)} %constant.18.clone.pick_ref) | copy-start | bytes 884740
  45.4 24.2 %copy-start.3 = (bf16[1,128,512]{2,1,0:T(8,128)(2,1)S(1)}, bf16[1,128,512]{2,1,0:T(8,128)(2,1)}, u32[]{:S(2)}) copy-start(bf16[1,128,512]{2,1,0:T(8,128)(2,1)} %q_ref.3) | copy-start | bytes 393220
  45.4 24.2 %copy-start.5 = (bf16[1,128,512]{2,1,0:T(8,128)(2,1)S(1)}, bf16[1,128,512]{2,1,0:T(8,128)(2,1)}, u32[]{:S(2)}) copy-start(bf16[1,128,512]{2,1,0:T(8,128)(2,1)} %k_ref.3) | copy-start | bytes 393220
  45.4 24.2 %copy-start.7 = (bf16[1,128,512]{2,1,0:T(8,128)(2,1)S(1)}, bf16[1,128,512]{2,1,0:T(8,128)(2,1)}, u32[]{:S(2)}) copy-start(bf16[1,128,512]{2,1,0:T(8,128)(2,1)} %v_ref.3) | copy-start | bytes 393220
where the time goes:
time: 71.2 us; the launch traced here: 71 us
  blocking collectives  58.2 us (82%)
  Pallas kernels  6.34 us (9%)
  local copies, waits for them, and re-layouts  5.6 us (8%)
  between operations  0.8 us (1%)
    all_to_all x2, blocking collectives, exchange(): lax.all_to_all(parts, ('ctx', 'dp'), split_axis=0, concat_axis=0, tiled=T...  58.2 us
    unnamed x38, local copies, waits for them, and re-layouts  5.6 us
    pallas_call x1, Pallas kernels, local(): pl.pallas_call(conv_kernel, out_shape=rows, scratch_shapes=[pltpu.VMEM((B...  4.51 us

commit v1 on v0

--- a/solution.py
+++ b/solution.py
@@ -1,5 +1,3 @@
-import functools
-
 import jax
 import jax.numpy as jnp
 import ml_dtypes
@@ -24,6 +22,7 @@
 CHUNK = KINDS * OWNED
 GROUP = 16
 TILE = GROUP * SEQS * CHUNK
+PACK_VMEM = (64 * 1024 - 1024) * 1024
 
 
 def two_terms(table):
@@ -76,36 +75,64 @@
     return lax.dot_general(a, b, (dims, ((), ())), preferred_element_type=F32)
 
 
-def pack_kernel(q_ref, k_ref, v_ref, f_ref, g_ref, pick_ref, out_ref):
+def pack_kernel(q_hbm, k_hbm, v_hbm, f_hbm, g_hbm, pick_hbm, out_hbm, in_ref, f_ref, pick_ref, out_ref, in_sems, pick_sem, out_sems):
+    def copies(b):
+        cols = slice(b * LANES, (b + 1) * LANES)
+        rows = (k_hbm, v_hbm, g_hbm, q_hbm)
+        found = [pltpu.make_async_copy(src.at[0, :, cols], in_ref.at[i, b], in_sems.at[i, b]) for i, src in enumerate(rows)]
+        return found + [pltpu.make_async_copy(f_hbm.at[:, cols], f_ref.at[b], in_sems.at[4, b])]
+
+    for copy in copies(0):
+        copy.start()
+    pick_copy = pltpu.make_async_copy(pick_hbm, pick_ref, pick_sem)
+    pick_copy.start()
+    for b in range(1, C // LANES):
+        for copy in copies(b):
+            copy.start()
     term = lax.axis_index("dp")
-    product = (k_ref[0].astype(F32) * v_ref[0].astype(F32)).astype(BF16)
-    grad_mix = (g_ref[0].astype(F32) * q_ref[0].astype(F32)).astype(BF16)
-    taps = f_ref[...]
-    high = taps.astype(BF16).astype(F32)
-    rest = taps - high
-    middle = rest.astype(BF16).astype(F32)
-    part = jnp.where(term == 0, high, jnp.where(term == 1, middle, rest - middle)).astype(BF16)
+    sends = []
+    for b in range(C // LANES):
+        for copy in copies(b):
+            copy.wait()
+        product = (in_ref[0, b].astype(F32) * in_ref[1, b].astype(F32)).astype(BF16)
+        grad_mix = (in_ref[2, b].astype(F32) * in_ref[3, b].astype(F32)).astype(BF16)
+        taps = f_ref[b]
+        high = taps.astype(BF16).astype(F32)
+        rest = taps - high
+        middle = rest.astype(BF16).astype(F32)
+        part = jnp.where(term == 0, high, jnp.where(term == 1, middle, rest - middle)).astype(BF16)
+        if b == 0:
+            pick_copy.wait()
+        rows = mm(pick_ref[...], jnp.concatenate([product, grad_mix, part], axis=1), ((1,), (1,)))
+        at = pl.ds(b * CHUNK * HALF, CHUNK * HALF)
+        out_ref[b] = rows.astype(BF16)
+        sends.append(pltpu.make_async_copy(out_ref.at[b], out_hbm.at[at, :], out_sems.at[b]))
+        sends[-1].start()
+    for copy in sends:
+        copy.wait()
+
+
+def unpack_kernel(q_ref, k_ref, v_ref, g_ref, got_ref, pick_ref, o_hbm, gq_hbm, gk_hbm, gv_hbm, gf_hbm, rows_ref, taps_ref, sems):
     pick = pick_ref[...]
-    for b in range(C // LANES):
-        cols = slice(b * LANES, (b + 1) * LANES)
-        data = jnp.concatenate([product[:, cols], grad_mix[:, cols], part[:, cols]], axis=1)
-        rows = mm(pick, data, ((1,), (1,)))
-        out_ref[b * CHUNK * HALF : (b + 1) * CHUNK * HALF, :] = rows.astype(BF16)
-
-
-def unpack_kernel(q_ref, k_ref, v_ref, g_ref, got_ref, pick_ref, o_ref, gq_ref, gk_ref, gv_ref, gf_ref):
-    pick = pick_ref[...]
+    copies = []
     for b in range(C // LANES):
         cols = slice(b * LANES, (b + 1) * LANES)
         got = got_ref[b * CHUNK * HALF : (b + 1) * CHUNK * HALF, :]
         data = mm(got, pick, ((0,), (0,)))
         mixed = data[:, :LANES]
         back = data[:, LANES : 2 * LANES]
-        gf_ref[:, cols] = data[:, 2 * LANES :]
-        o_ref[0, :, cols] = (q_ref[0, :, cols].astype(F32) * mixed).astype(BF16)
-        gq_ref[0, :, cols] = (g_ref[0, :, cols].astype(F32) * mixed).astype(BF16)
-        gk_ref[0, :, cols] = (back * v_ref[0, :, cols].astype(F32)).astype(BF16)
-        gv_ref[0, :, cols] = (back * k_ref[0, :, cols].astype(F32)).astype(BF16)
+        taps_ref[b] = data[:, 2 * LANES :]
+        rows_ref[0, b] = (q_ref[0, :, cols].astype(F32) * mixed).astype(BF16)
+        rows_ref[1, b] = (g_ref[0, :, cols].astype(F32) * mixed).astype(BF16)
+        rows_ref[2, b] = (back * v_ref[0, :, cols].astype(F32)).astype(BF16)
+        rows_ref[3, b] = (back * k_ref[0, :, cols].astype(F32)).astype(BF16)
+        for i, out in enumerate((o_hbm, gq_hbm, gk_hbm, gv_hbm)):
+            copies.append(pltpu.make_async_copy(rows_ref.at[i, b], out.at[0, :, cols], sems.at[i, b]))
+        copies.append(pltpu.make_async_copy(taps_ref.at[b], gf_hbm.at[:, cols], sems.at[4, b]))
+        for copy in copies[-5:]:
+            copy.start()
+    for copy in copies:
+        copy.wait()
 
 
 def split(x):
@@ -234,9 +261,25 @@
     pick, order, back, first_signal, first_filter, twist, second, second_back, last = tables()
     rows = jax.ShapeDtypeStruct((OWNERS * CHUNK, LANES), BF16)
     limit = pltpu.CompilerParams(vmem_limit_bytes=32 * 1024 * 1024)
-    sent = pl.pallas_call(pack_kernel, out_shape=rows, compiler_params=limit, name="pack")(
-        query, key_input, value_input, filter_taps, grad_output, pick
-    )
+    hbm = pl.BlockSpec(memory_space=pltpu.HBM)
+    blocks = C // LANES
+    sent = pl.pallas_call(
+        pack_kernel,
+        out_shape=rows,
+        in_specs=[hbm] * 6,
+        out_specs=hbm,
+        scratch_shapes=[
+            pltpu.VMEM((4, blocks, LANES, LANES), BF16),
+            pltpu.VMEM((blocks, LANES, LANES), F32),
+            pltpu.VMEM(pick.shape, BF16),
+            pltpu.VMEM((blocks, CHUNK * HALF, LANES), BF16),
+            pltpu.SemaphoreType.DMA((5, blocks)),
+            pltpu.SemaphoreType.DMA(()),
+            pltpu.SemaphoreType.DMA((blocks,)),
+        ],
+        compiler_params=pltpu.CompilerParams(vmem_limit_bytes=PACK_VMEM),
+        name="pack",
+    )(query, key_input, value_input, filter_taps, grad_output, pick)
     got = exchange(sent)
     results = pl.pallas_call(
         conv_kernel,
@@ -254,6 +297,12 @@
     return pl.pallas_call(
         unpack_kernel,
         out_shape=(like, like, like, like, jax.ShapeDtypeStruct(filter_taps.shape, F32)),
+        out_specs=[hbm] * 5,
+        scratch_shapes=[
+            pltpu.VMEM((4, C // LANES, LANES, LANES), BF16),
+            pltpu.VMEM((C // LANES, LANES, LANES), F32),
+            pltpu.SemaphoreType.DMA((5, C // LANES)),
+        ],
         compiler_params=limit,
         name="unpack",
     )(query, key_input, value_input, grad_output, returned, pick)

time: 71.2 us -> 68.7 us (0.965)
  local copies, waits for them, and re-layouts: 5.6 us -> 0.09 us
  Pallas kernels: 6.34 us -> 9.14 us
    unnamed x38 -> x26, local copies, waits for them, and re-layouts: 5.6 us -> 0.09 us
    pallas_call x1, Pallas kernels: 0.49 us -> 3.32 us  [local(): pl.pallas_call(pack_kernel, out_shape=rows, in_specs=[hbm] * 6, out_specs...]
where the time goes in v1:
time: 68.7 us; the launch traced here: 68.5 us
  blocking collectives  58.4 us (85%)
  Pallas kernels  9.14 us (13%)
  between operations  0.81 us (1%)
    all_to_all x2, blocking collectives, exchange(): lax.all_to_all(parts, ('ctx', 'dp'), split_axis=0, concat_axis=0, tiled=T...  58.4 us
    pallas_call x1, Pallas kernels, local(): pl.pallas_call(conv_kernel, out_shape=rows, scratch_shapes=[pltpu.VMEM((B...  4.51 us
    pallas_call x1, Pallas kernels, local(): pl.pallas_call(pack_kernel, out_shape=rows, in_specs=[hbm] * 6, out_specs...  3.32 us

profile of v1, /device:TPU:1, one launch (start us, length us, event | category | flops | bytes accessed | tf_op | source)
XLA Modules:
  0.0 68.5 jit_solution(17202422310927037228)
XLA Ops:
  0.6 0.0 copy-start.7
  0.6 0.0 copy-start.8
  0.7 0.0 copy-start.12
  0.7 3.3 %pack.1 = bf16[1536,128]{1,0:T(8,128)(2,1)} custom-call(bf16[1,128,512]{2,1,0:T(8,128)(2,1)} %q_ref.1, bf16[1,128,512]{2,1,0:T(8,128)(2,1)} %k_ref.1, bf16[1,128,512]{2,1,0:T(8,128)(2,1)} %v_ref.1, f32[128,512]{1,0:T(8,128)} %f_hbm.1, bf16[1,128,512]{2,1,0:T(8,128)(2,1)} %g_ref.1, bf16[384,384]{1,0:T(8,128)(2,1)} %constant.18.clone.pick_hbm.pick_ref), custom_call_target="tpu_custom_call" | custom-call | tf_op jit(solution)/shard_map/pack/pallas_call | solution.py:266
  4.0 0.0 copy-start.5
  4.0 0.0 copy-start.6
  4.0 0.0 copy-start.9
  4.0 0.0 copy-start.10
  4.0 0.0 copy-start.11
  4.1 34.3 %all_to_all.10 = bf16[768,2,128]{2,1,0:T(2,128)(2,1)S(1)} all-to-all(bf16[768,2,128]{2,1,0:T(2,128)(2,1)} %bitcast.7), channel_id=1, replica_groups=mesh['ctx'=64,'dp'=4] {'ctx','dp'}, dimensions={0} | all-to-all | bytes 786432 | tf_op jit(solution)/shard_map/all_to_all | solution.py:256
  38.3 0.0 copy-done.7
  38.3 0.0 copy-done.8
  38.3 0.0 copy-done.12
  38.3 0.0 copy-done.5
  38.3 0.0 copy-done.6
  38.3 0.0 copy-done.9
  38.4 0.0 copy-done.10
  38.4 0.0 copy-done.11
  38.4 0.0 copy-start.4
  38.4 4.5 %conv.1 = bf16[1536,128]{1,0:T(8,128)(2,1)S(1)} custom-call(bf16[1536,128]{1,0:T(8,128)(2,1)S(1)} %bitcast.4, bf16[384,384]{1,0:T(8,128)(2,1)S(1)} %copy-done.6, bf16[384,384]{1,0:T(8,128)(2,1)S(1)} %copy-done.5, bf16[128,128]{1,0:T(8,128)(2,1)S(1)} %copy-done.12, bf16[128,256]{1,0:T(8,128)(2,1)S(1)} %copy-done.10, f32[128,128]{1,0:T(8,128)S(1)} %copy-done.9, ...), custom_call_target="tpu_custom_call" | custom-call | tf_op jit(solution)/shard_map/conv/pallas_call | solution.py:284
  42.9 0.0 copy-start
  42.9 0.0 copy-start.1
  42.9 0.0 copy-start.2
  42.9 0.0 copy-start.3
  43.0 24.2 %all_to_all.11 = bf16[768,2,128]{2,1,0:T(2,128)(2,1)S(1)} all-to-all(bf16[768,2,128]{2,1,0:T(2,128)(2,1)S(1)} %bitcast.5), channel_id=1, replica_groups=mesh['ctx'=64,'dp'=4] {'ctx','dp'}, dimensions={0} | all-to-all | bytes 786432 | tf_op jit(solution)/shard_map/all_to_all | solution.py:256
  67.1 0.0 copy-done.4
  67.1 0.0 copy-done
  67.1 0.0 copy-done.1
  67.1 0.0 copy-done.2
  67.2 0.0 copy-done.3
  67.2 1.3 %unpack.1 = (bf16[1,128,512]{2,1,0:T(8,128)(2,1)}, bf16[1,128,512]{2,1,0:T(8,128)(2,1)}, bf16[1,128,512]{2,1,0:T(8,128)(2,1)}, bf16[1,128,512]{2,1,0:T(8,128)(2,1)}, f32[128,512]{1,0:T(8,128)}) custom-call(bf16[1,128,512]{2,1,0:T(8,128)(2,1)S(1)} %copy-done.1, bf16[1,128,512]{2,1,0:T(8,128)(2,1)S(1)} %copy-done.2, bf16[1,128,512]{2,1,0:T(8,128)(2,1)S(1)} %copy-done.3, ...), custom_call_target="tpu_custom_call" | custom-call | tf_op jit(solution)/shard_map/unpack/pallas_call | solution.py:297
Async XLA Ops:
  0.6 37.7 %copy-start.7 = (bf16[2,256,256]{2,1,0:T(8,128)(2,1)S(1)}, bf16[2,256,256]{2,1,0:T(8,128)(2,1)}, u32[]{:S(2)}) copy-start(bf16[2,256,256]{2,1,0:T(8,128)(2,1)} %constant.25.clone.secb_ref) | copy-start | bytes 786436
  0.6 37.7 %copy-start.8 = (bf16[2,256,256]{2,1,0:T(8,128)(2,1)S(1)}, bf16[2,256,256]{2,1,0:T(8,128)(2,1)}, u32[]{:S(2)}) copy-start(bf16[2,256,256]{2,1,0:T(8,128)(2,1)} %constant.24.clone.sec_ref) | copy-start | bytes 786436
  0.7 37.7 %copy-start.12 = (bf16[128,128]{1,0:T(8,128)(2,1)S(1)}, bf16[128,128]{1,0:T(8,128)(2,1)}, u32[]{:S(2)}) copy-start(bf16[128,128]{1,0:T(8,128)(2,1)} %constant.21.clone.fs_ref) | copy-start | bytes 98308
  4.0 34.3 %copy-start.5 = (bf16[384,384]{1,0:T(8,128)(2,1)S(1)}, bf16[384,384]{1,0:T(8,128)(2,1)}, u32[]{:S(2)}) copy-start(bf16[384,384]{1,0:T(8,128)(2,1)} %constant.20.clone.back_ref) | copy-start | bytes 884740
  4.0 34.3 %copy-start.6 = (bf16[384,384]{1,0:T(8,128)(2,1)S(1)}, bf16[384,384]{1,0:T(8,128)(2,1)}, u32[]{:S(2)}) copy-start(bf16[384,384]{1,0:T(8,128)(2,1)} %constant.19.clone.order_ref) | copy-start | bytes 884740
  4.0 34.3 %copy-start.9 = (f32[128,128]{1,0:T(8,128)S(1)}, f32[128,128]{1,0:T(8,128)}, u32[]{:S(2)}) copy-start(f32[128,128]{1,0:T(8,128)} %constant.23.clone.tw_ref) | copy-start | bytes 196612
  4.0 34.3 %copy-start.10 = (bf16[128,256]{1,0:T(8,128)(2,1)S(1)}, bf16[128,256]{1,0:T(8,128)(2,1)}, u32[]{:S(2)}) copy-start(bf16[128,256]{1,0:T(8,128)(2,1)} %constant.22.clone.ff_ref) | copy-start | bytes 196612
  4.0 34.3 %copy-start.11 = (bf16[64,384]{1,0:T(8,128)(2,1)S(1)}, bf16[64,384]{1,0:T(8,128)(2,1)}, u32[]{:S(2)}) copy-start(bf16[64,384]{1,0:T(8,128)(2,1)} %constant.26.clone.last_ref) | copy-start | bytes 147460
  38.4 28.8 %copy-start.4 = (bf16[1,128,512]{2,1,0:T(8,128)(2,1)S(1)}, bf16[1,128,512]{2,1,0:T(8,128)(2,1)}, u32[]{:S(2)}) copy-start(bf16[1,128,512]{2,1,0:T(8,128)(2,1)} %g_ref.1) | copy-start | bytes 393220
  42.9 24.2 %copy-start = (bf16[384,384]{1,0:T(8,128)(2,1)S(1)}, bf16[384,384]{1,0:T(8,128)(2,1)}, u32[]{:S(2)}) copy-start(bf16[384,384]{1,0:T(8,128)(2,1)} %constant.18.clone.pick_hbm.pick_ref) | copy-start | bytes 884740
  42.9 24.2 %copy-start.1 = (bf16[1,128,512]{2,1,0:T(8,128)(2,1)S(1)}, bf16[1,128,512]{2,1,0:T(8,128)(2,1)}, u32[]{:S(2)}) copy-start(bf16[1,128,512]{2,1,0:T(8,128)(2,1)} %q_ref.1) | copy-start | bytes 393220
  42.9 24.2 %copy-start.2 = (bf16[1,128,512]{2,1,0:T(8,128)(2,1)S(1)}, bf16[1,128,512]{2,1,0:T(8,128)(2,1)}, u32[]{:S(2)}) copy-start(bf16[1,128,512]{2,1,0:T(8,128)(2,1)} %k_ref.1) | copy-start | bytes 393220
  42.9 24.2 %copy-start.3 = (bf16[1,128,512]{2,1,0:T(8,128)(2,1)S(1)}, bf16[1,128,512]{2,1,0:T(8,128)(2,1)}, u32[]{:S(2)}) copy-start(bf16[1,128,512]{2,1,0:T(8,128)(2,1)} %v_ref.1) | copy-start | bytes 393220

commit v2 on v1

--- a/solution.py
+++ b/solution.py
@@ -22,7 +22,6 @@
 CHUNK = KINDS * OWNED
 GROUP = 16
 TILE = GROUP * SEQS * CHUNK
-PACK_VMEM = (64 * 1024 - 1024) * 1024
 
 
 def two_terms(table):
@@ -75,41 +74,26 @@
     return lax.dot_general(a, b, (dims, ((), ())), preferred_element_type=F32)
 
 
-def pack_kernel(q_hbm, k_hbm, v_hbm, f_hbm, g_hbm, pick_hbm, out_hbm, in_ref, f_ref, pick_ref, out_ref, in_sems, pick_sem, out_sems):
-    def copies(b):
+def pack_kernel(q_hbm, k_hbm, v_hbm, f_hbm, g_hbm, pick_hbm, out_ref, in_ref, f_ref, pick_ref, sems):
+    copies = [pltpu.make_async_copy(src.at[0], in_ref.at[i], sems.at[i]) for i, src in enumerate((k_hbm, v_hbm, g_hbm, q_hbm))]
+    copies.append(pltpu.make_async_copy(f_hbm, f_ref, sems.at[4]))
+    copies.append(pltpu.make_async_copy(pick_hbm, pick_ref, sems.at[5]))
+    for copy in copies:
+        copy.start()
+    term = lax.axis_index("dp")
+    for copy in copies:
+        copy.wait()
+    for b in range(C // LANES):
         cols = slice(b * LANES, (b + 1) * LANES)
-        rows = (k_hbm, v_hbm, g_hbm, q_hbm)
-        found = [pltpu.make_async_copy(src.at[0, :, cols], in_ref.at[i, b], in_sems.at[i, b]) for i, src in enumerate(rows)]
-        return found + [pltpu.make_async_copy(f_hbm.at[:, cols], f_ref.at[b], in_sems.at[4, b])]
-
-    for copy in copies(0):
-        copy.start()
-    pick_copy = pltpu.make_async_copy(pick_hbm, pick_ref, pick_sem)
-    pick_copy.start()
-    for b in range(1, C // LANES):
-        for copy in copies(b):
-            copy.start()
-    term = lax.axis_index("dp")
-    sends = []
-    for b in range(C // LANES):
-        for copy in copies(b):
-            copy.wait()
-        product = (in_ref[0, b].astype(F32) * in_ref[1, b].astype(F32)).astype(BF16)
-        grad_mix = (in_ref[2, b].astype(F32) * in_ref[3, b].astype(F32)).astype(BF16)
-        taps = f_ref[b]
+        product = (in_ref[0, :, cols].astype(F32) * in_ref[1, :, cols].astype(F32)).astype(BF16)
+        grad_mix = (in_ref[2, :, cols].astype(F32) * in_ref[3, :, cols].astype(F32)).astype(BF16)
+        taps = f_ref[:, cols]
         high = taps.astype(BF16).astype(F32)
         rest = taps - high
         middle = rest.astype(BF16).astype(F32)
         part = jnp.where(term == 0, high, jnp.where(term == 1, middle, rest - middle)).astype(BF16)
-        if b == 0:
-            pick_copy.wait()
         rows = mm(pick_ref[...], jnp.concatenate([product, grad_mix, part], axis=1), ((1,), (1,)))
-        at = pl.ds(b * CHUNK * HALF, CHUNK * HALF)
-        out_ref[b] = rows.astype(BF16)
-        sends.append(pltpu.make_async_copy(out_ref.at[b], out_hbm.at[at, :], out_sems.at[b]))
-        sends[-1].start()
-    for copy in sends:
-        copy.wait()
+        out_ref[b * CHUNK * HALF : (b + 1) * CHUNK * HALF, :] = rows.astype(BF16)
 
 
 def unpack_kernel(q_ref, k_ref, v_ref, g_ref, got_ref, pick_ref, o_hbm, gq_hbm, gk_hbm, gv_hbm, gf_hbm, rows_ref, taps_ref, sems):
@@ -262,24 +246,20 @@
     rows = jax.ShapeDtypeStruct((OWNERS * CHUNK, LANES), BF16)
     limit = pltpu.CompilerParams(vmem_limit_bytes=32 * 1024 * 1024)
     hbm = pl.BlockSpec(memory_space=pltpu.HBM)
-    blocks = C // LANES
+    inputs = (query, key_input, value_input, filter_taps, grad_output, jnp.asarray(pick))
     sent = pl.pallas_call(
         pack_kernel,
         out_shape=rows,
         in_specs=[hbm] * 6,
-        out_specs=hbm,
         scratch_shapes=[
-            pltpu.VMEM((4, blocks, LANES, LANES), BF16),
-            pltpu.VMEM((blocks, LANES, LANES), F32),
+            pltpu.VMEM((4,) + query.shape[1:], BF16),
+            pltpu.VMEM(filter_taps.shape, F32),
             pltpu.VMEM(pick.shape, BF16),
-            pltpu.VMEM((blocks, CHUNK * HALF, LANES), BF16),
-            pltpu.SemaphoreType.DMA((5, blocks)),
-            pltpu.SemaphoreType.DMA(()),
-            pltpu.SemaphoreType.DMA((blocks,)),
+            pltpu.SemaphoreType.DMA((6,)),
         ],
-        compiler_params=pltpu.CompilerParams(vmem_limit_bytes=PACK_VMEM),
+        compiler_params=limit,
         name="pack",
-    )(query, key_input, value_input, filter_taps, grad_output, pick)
+    )(*[pltpu.with_memory_space_constraint(x, pltpu.HBM) for x in inputs])
     got = exchange(sent)
     results = pl.pallas_call(
         conv_kernel,

time: 68.7 us -> 67 us (0.975)
  Pallas kernels: 9.14 us -> 7.71 us
    pallas_call x1, Pallas kernels: 3.32 us -> 1.89 us  [local(): pl.pallas_call(pack_kernel, out_shape=rows, in_specs=[hbm] * 6, scratch_s...]
where the time goes in v2:
time: 67 us; the launch traced here: 66.8 us
  blocking collectives  58.2 us (87%)
  Pallas kernels  7.71 us (12%)
  between operations  0.81 us (1%)
    all_to_all x2, blocking collectives, exchange(): lax.all_to_all(parts, ('ctx', 'dp'), split_axis=0, concat_axis=0, tiled=T...  58.2 us
    pallas_call x1, Pallas kernels, local(): pl.pallas_call(conv_kernel, out_shape=rows, scratch_shapes=[pltpu.VMEM((B...  4.51 us
    pallas_call x1, Pallas kernels, local(): pl.pallas_call(pack_kernel, out_shape=rows, in_specs=[hbm] * 6, scratch_s...  1.89 us

profile of v2, /device:TPU:1, one launch (start us, length us, event | category | flops | bytes accessed | tf_op | source)
XLA Modules:
  0.0 66.8 jit_solution(14799438818321027509)
XLA Ops:
  0.6 0.0 copy-start.7
  0.6 0.0 copy-start.8
  0.7 0.0 copy-start.12
  0.7 1.9 %pack.1 = bf16[1536,128]{1,0:T(8,128)(2,1)S(1)} custom-call(bf16[1,128,512]{2,1,0:T(8,128)(2,1)} %q_ref.1, bf16[1,128,512]{2,1,0:T(8,128)(2,1)} %k_ref.1, bf16[1,128,512]{2,1,0:T(8,128)(2,1)} %v_ref.1, f32[128,512]{1,0:T(8,128)} %f_hbm.1, bf16[1,128,512]{2,1,0:T(8,128)(2,1)} %g_ref.1, bf16[384,384]{1,0:T(8,128)(2,1)} %constant.18.clone.pick_hbm.pick_ref), custom_call_target="tpu_custom_call" | custom-call | tf_op jit(solution)/shard_map/pack/pallas_call | solution.py:250
  2.6 0.0 copy-start.5
  2.6 0.0 copy-start.6
  2.6 0.0 copy-start.9
  2.6 0.0 copy-start.10
  2.6 0.0 copy-start.11
  2.6 34.0 %all_to_all.10 = bf16[768,2,128]{2,1,0:T(2,128)(2,1)S(1)} all-to-all(bf16[768,2,128]{2,1,0:T(2,128)(2,1)S(1)} %bitcast.7), channel_id=1, replica_groups=mesh['ctx'=64,'dp'=4] {'ctx','dp'}, dimensions={0} | all-to-all | bytes 786432 | tf_op jit(solution)/shard_map/all_to_all | solution.py:240
  36.7 0.0 copy-done.7
  36.7 0.0 copy-done.8
  36.7 0.0 copy-done.12
  36.7 0.0 copy-done.5
  36.7 0.0 copy-done.6
  36.7 0.0 copy-done.9
  36.7 0.0 copy-done.10
  36.7 0.0 copy-done.11
  36.7 0.0 copy-start.4
  36.7 4.5 %conv.1 = bf16[1536,128]{1,0:T(8,128)(2,1)S(1)} custom-call(bf16[1536,128]{1,0:T(8,128)(2,1)S(1)} %bitcast.4, bf16[384,384]{1,0:T(8,128)(2,1)S(1)} %copy-done.6, bf16[384,384]{1,0:T(8,128)(2,1)S(1)} %copy-done.5, bf16[128,128]{1,0:T(8,128)(2,1)S(1)} %copy-done.12, bf16[128,256]{1,0:T(8,128)(2,1)S(1)} %copy-done.10, f32[128,128]{1,0:T(8,128)S(1)} %copy-done.9, ...), custom_call_target="tpu_custom_call" | custom-call | tf_op jit(solution)/shard_map/conv/pallas_call | solution.py:264
  41.3 0.0 copy-start
  41.3 0.0 copy-start.1
  41.3 0.0 copy-start.2
  41.3 0.0 copy-start.3
  41.3 24.2 %all_to_all.11 = bf16[768,2,128]{2,1,0:T(2,128)(2,1)S(1)} all-to-all(bf16[768,2,128]{2,1,0:T(2,128)(2,1)S(1)} %bitcast.5), channel_id=1, replica_groups=mesh['ctx'=64,'dp'=4] {'ctx','dp'}, dimensions={0} | all-to-all | bytes 786432 | tf_op jit(solution)/shard_map/all_to_all | solution.py:240
  65.5 0.0 copy-done.4
  65.5 0.0 copy-done
  65.5 0.0 copy-done.1
  65.5 0.0 copy-done.2
  65.5 0.0 copy-done.3
  65.5 1.3 %unpack.1 = (bf16[1,128,512]{2,1,0:T(8,128)(2,1)}, bf16[1,128,512]{2,1,0:T(8,128)(2,1)}, bf16[1,128,512]{2,1,0:T(8,128)(2,1)}, bf16[1,128,512]{2,1,0:T(8,128)(2,1)}, f32[128,512]{1,0:T(8,128)}) custom-call(bf16[1,128,512]{2,1,0:T(8,128)(2,1)S(1)} %copy-done.1, bf16[1,128,512]{2,1,0:T(8,128)(2,1)S(1)} %copy-done.2, bf16[1,128,512]{2,1,0:T(8,128)(2,1)S(1)} %copy-done.3, ...), custom_call_target="tpu_custom_call" | custom-call | tf_op jit(solution)/shard_map/unpack/pallas_call | solution.py:277
Async XLA Ops:
  0.6 36.0 %copy-start.7 = (bf16[2,256,256]{2,1,0:T(8,128)(2,1)S(1)}, bf16[2,256,256]{2,1,0:T(8,128)(2,1)}, u32[]{:S(2)}) copy-start(bf16[2,256,256]{2,1,0:T(8,128)(2,1)} %constant.25.clone.secb_ref) | copy-start | bytes 786436
  0.6 36.0 %copy-start.8 = (bf16[2,256,256]{2,1,0:T(8,128)(2,1)S(1)}, bf16[2,256,256]{2,1,0:T(8,128)(2,1)}, u32[]{:S(2)}) copy-start(bf16[2,256,256]{2,1,0:T(8,128)(2,1)} %constant.24.clone.sec_ref) | copy-start | bytes 786436
  0.7 36.0 %copy-start.12 = (bf16[128,128]{1,0:T(8,128)(2,1)S(1)}, bf16[128,128]{1,0:T(8,128)(2,1)}, u32[]{:S(2)}) copy-start(bf16[128,128]{1,0:T(8,128)(2,1)} %constant.21.clone.fs_ref) | copy-start | bytes 98308
  2.6 34.1 %copy-start.5 = (bf16[384,384]{1,0:T(8,128)(2,1)S(1)}, bf16[384,384]{1,0:T(8,128)(2,1)}, u32[]{:S(2)}) copy-start(bf16[384,384]{1,0:T(8,128)(2,1)} %constant.20.clone.back_ref) | copy-start | bytes 884740
  2.6 34.1 %copy-start.6 = (bf16[384,384]{1,0:T(8,128)(2,1)S(1)}, bf16[384,384]{1,0:T(8,128)(2,1)}, u32[]{:S(2)}) copy-start(bf16[384,384]{1,0:T(8,128)(2,1)} %constant.19.clone.order_ref) | copy-start | bytes 884740
  2.6 34.1 %copy-start.9 = (f32[128,128]{1,0:T(8,128)S(1)}, f32[128,128]{1,0:T(8,128)}, u32[]{:S(2)}) copy-start(f32[128,128]{1,0:T(8,128)} %constant.23.clone.tw_ref) | copy-start | bytes 196612
  2.6 34.1 %copy-start.10 = (bf16[128,256]{1,0:T(8,128)(2,1)S(1)}, bf16[128,256]{1,0:T(8,128)(2,1)}, u32[]{:S(2)}) copy-start(bf16[128,256]{1,0:T(8,128)(2,1)} %constant.22.clone.ff_ref) | copy-start | bytes 196612
  2.6 34.1 %copy-start.11 = (bf16[64,384]{1,0:T(8,128)(2,1)S(1)}, bf16[64,384]{1,0:T(8,128)(2,1)}, u32[]{:S(2)}) copy-start(bf16[64,384]{1,0:T(8,128)(2,1)} %constant.26.clone.last_ref) | copy-start | bytes 147460
  36.7 28.8 %copy-start.4 = (bf16[1,128,512]{2,1,0:T(8,128)(2,1)S(1)}, bf16[1,128,512]{2,1,0:T(8,128)(2,1)}, u32[]{:S(2)}) copy-start(bf16[1,128,512]{2,1,0:T(8,128)(2,1)} %g_ref.1) | copy-start | bytes 393220
  41.3 24.2 %copy-start = (bf16[384,384]{1,0:T(8,128)(2,1)S(1)}, bf16[384,384]{1,0:T(8,128)(2,1)}, u32[]{:S(2)}) copy-start(bf16[384,384]{1,0:T(8,128)(2,1)} %constant.18.clone.pick_hbm.pick_ref) | copy-start | bytes 884740
  41.3 24.2 %copy-start.1 = (bf16[1,128,512]{2,1,0:T(8,128)(2,1)S(1)}, bf16[1,128,512]{2,1,0:T(8,128)(2,1)}, u32[]{:S(2)}) copy-start(bf16[1,128,512]{2,1,0:T(8,128)(2,1)} %q_ref.1) | copy-start | bytes 393220
  41.3 24.2 %copy-start.2 = (bf16[1,128,512]{2,1,0:T(8,128)(2,1)S(1)}, bf16[1,128,512]{2,1,0:T(8,128)(2,1)}, u32[]{:S(2)}) copy-start(bf16[1,128,512]{2,1,0:T(8,128)(2,1)} %k_ref.1) | copy-start | bytes 393220
  41.3 24.2 %copy-start.3 = (bf16[1,128,512]{2,1,0:T(8,128)(2,1)S(1)}, bf16[1,128,512]{2,1,0:T(8,128)(2,1)}, u32[]{:S(2)}) copy-start(bf16[1,128,512]{2,1,0:T(8,128)(2,1)} %v_ref.1) | copy-start | bytes 393220

commit v3 on v2

--- a/solution.py
+++ b/solution.py
@@ -16,12 +16,16 @@
 HALF = 64
 SEQS = 4
 C = 512
-OWNERS = 256
-OWNED = C // OWNERS
-KINDS = 3
-CHUNK = KINDS * OWNED
+CORES = 2
+OWNERS = 128
+OWNED = C // CORES // OWNERS
+PARTS = 5
+CHUNK = PARTS * OWNED
 GROUP = 16
-TILE = GROUP * SEQS * CHUNK
+HALVES = 2
+SIGNALS = HALVES * CHUNK
+TILE = GROUP * SIGNALS
+SWAP = ((0, 1), (1, 0))
 
 
 def two_terms(table):
@@ -36,7 +40,7 @@
     first = np.concatenate([np.cos(angle1), -np.sin(angle1)], axis=0)
     first_high, first_low = two_terms(first)
     first_signal = np.concatenate([first_high, first_low], axis=1)
-    first_filter = np.concatenate([first_high, first_low, first_high, first_high], axis=1)
+    first_filter = np.concatenate([first_high, first_low, first_high], axis=1)
     angle_t = 2.0 * np.pi * k1 * np.arange(LANES)[None, :] / (ROWS * LANES)
     twist = np.concatenate([np.cos(angle_t), -np.sin(angle_t)], axis=0).astype(np.float32)
     index = np.arange(LANES)
@@ -47,18 +51,17 @@
     last = np.concatenate([np.cos(angle1.T), -np.sin(angle1.T)], axis=1) * (2.0 / (ROWS * LANES))
     last_high, last_low = two_terms(last)
     last_stack = np.concatenate([last_high, last_high, last_low], axis=1)
-    row = np.arange(CHUNK * HALF)
-    pick = np.zeros((CHUNK * HALF, KINDS * LANES))
-    pick[row, (row % CHUNK // OWNED) * LANES + OWNED * (row // CHUNK) + row % OWNED] = 1.0
     line = np.arange(TILE)
-    block = line // (SEQS * CHUNK)
-    seq = line % (SEQS * CHUNK) // CHUNK
-    kind = line % CHUNK // OWNED
+    block = line // SIGNALS
+    half = line % SIGNALS // CHUNK
+    part = line % CHUNK // OWNED
     own = line % OWNED
+    seq = half * CORES + part // 3
+    kind = part % 3
+    slot = np.where(kind == 2, 2 * OWNED * SEQS + own * HALVES + half, (kind * OWNED + own) * SEQS + seq)
     order = np.zeros((TILE, TILE))
-    order[((kind * OWNED + own) * SEQS + seq) * GROUP + block, line] = 1.0
+    order[slot * GROUP + block, line] = 1.0
     return (
-        pick.astype(ml_dtypes.bfloat16),
         order.astype(ml_dtypes.bfloat16),
         np.ascontiguousarray(order.T).astype(ml_dtypes.bfloat16),
         first_signal,
@@ -74,45 +77,63 @@
     return lax.dot_general(a, b, (dims, ((), ())), preferred_element_type=F32)
 
 
-def pack_kernel(q_hbm, k_hbm, v_hbm, f_hbm, g_hbm, pick_hbm, out_ref, in_ref, f_ref, pick_ref, sems):
+def columns(core, b):
+    return pl.ds(pl.multiple_of(core * (C // CORES) + b * LANES, LANES), LANES)
+
+
+def gate_kernel(q_hbm, k_hbm, v_hbm, g_hbm, out_ref, pick_ref, in_ref, sems):
     copies = [pltpu.make_async_copy(src.at[0], in_ref.at[i], sems.at[i]) for i, src in enumerate((k_hbm, v_hbm, g_hbm, q_hbm))]
-    copies.append(pltpu.make_async_copy(f_hbm, f_ref, sems.at[4]))
-    copies.append(pltpu.make_async_copy(pick_hbm, pick_ref, sems.at[5]))
     for copy in copies:
         copy.start()
-    term = lax.axis_index("dp")
-    for copy in copies:
-        copy.wait()
-    for b in range(C // LANES):
-        cols = slice(b * LANES, (b + 1) * LANES)
-        product = (in_ref[0, :, cols].astype(F32) * in_ref[1, :, cols].astype(F32)).astype(BF16)
-        grad_mix = (in_ref[2, :, cols].astype(F32) * in_ref[3, :, cols].astype(F32)).astype(BF16)
+    row = lax.broadcasted_iota(jnp.int32, (CHUNK * HALF, LANES), 0)
+    lane = lax.broadcasted_iota(jnp.int32, (CHUNK * HALF, LANES), 1)
+    first = (lane >> 1) * CHUNK + (lane & 1)
+    for part in range(PARTS):
+        chosen = jnp.where(row == first + OWNED * part, 1.0, 0.0)
+        pick_ref[:, part * LANES : (part + 1) * LANES] = chosen.astype(BF16)
+    for i in range(2):
+        copies[2 * i].wait()
+        copies[2 * i + 1].wait()
+        out_ref[i] = (in_ref[2 * i].astype(F32) * in_ref[2 * i + 1].astype(F32)).astype(BF16)
+
+
+def pack_kernel(own_ref, other_ref, f_ref, pick_ref, out_ref):
+    core = lax.axis_index("core")
+    term = lax.axis_index("zh")
+    for b in range(C // CORES // LANES):
+        cols = columns(core, b)
         taps = f_ref[:, cols]
         high = taps.astype(BF16).astype(F32)
-        rest = taps - high
-        middle = rest.astype(BF16).astype(F32)
-        part = jnp.where(term == 0, high, jnp.where(term == 1, middle, rest - middle)).astype(BF16)
-        rows = mm(pick_ref[...], jnp.concatenate([product, grad_mix, part], axis=1), ((1,), (1,)))
+        part = jnp.where(term == 0, high, taps - high).astype(BF16)
+        data = [own_ref[0, :, cols], own_ref[1, :, cols], part, other_ref[0, :, cols], other_ref[1, :, cols]]
+        rows = mm(pick_ref[...], jnp.concatenate(data, axis=1), ((1,), (1,)))
         out_ref[b * CHUNK * HALF : (b + 1) * CHUNK * HALF, :] = rows.astype(BF16)
 
 
-def unpack_kernel(q_ref, k_ref, v_ref, g_ref, got_ref, pick_ref, o_hbm, gq_hbm, gk_hbm, gv_hbm, gf_hbm, rows_ref, taps_ref, sems):
-    pick = pick_ref[...]
+def unpack_kernel(
+    q_ref, k_ref, v_ref, g_ref, own_ref, other_ref, pick_ref, o_hbm, gq_hbm, gk_hbm, gv_hbm, gf_hbm, rows_ref, taps_ref, sems
+):
+    core = lax.axis_index("core")
     copies = []
-    for b in range(C // LANES):
-        cols = slice(b * LANES, (b + 1) * LANES)
+    for i in range(C // LANES):
+        b = i // 2
+        cols = columns(core if i % 2 == 0 else 1 - core, b)
+        got_ref = own_ref if i % 2 == 0 else other_ref
         got = got_ref[b * CHUNK * HALF : (b + 1) * CHUNK * HALF, :]
-        data = mm(got, pick, ((0,), (0,)))
-        mixed = data[:, :LANES]
-        back = data[:, LANES : 2 * LANES]
-        taps_ref[b] = data[:, 2 * LANES :]
-        rows_ref[0, b] = (q_ref[0, :, cols].astype(F32) * mixed).astype(BF16)
-        rows_ref[1, b] = (g_ref[0, :, cols].astype(F32) * mixed).astype(BF16)
-        rows_ref[2, b] = (back * v_ref[0, :, cols].astype(F32)).astype(BF16)
-        rows_ref[3, b] = (back * k_ref[0, :, cols].astype(F32)).astype(BF16)
-        for i, out in enumerate((o_hbm, gq_hbm, gk_hbm, gv_hbm)):
-            copies.append(pltpu.make_async_copy(rows_ref.at[i, b], out.at[0, :, cols], sems.at[i, b]))
-        copies.append(pltpu.make_async_copy(taps_ref.at[b], gf_hbm.at[:, cols], sems.at[4, b]))
+        if i % 2 == 0:
+            data = mm(got, pick_ref[:, : 3 * LANES], ((0,), (0,)))
+            mixed, back, taps = data[:, :LANES], data[:, LANES : 2 * LANES], data[:, 2 * LANES :]
+        else:
+            data = mm(got, pick_ref[:, 2 * LANES :], ((0,), (0,)))
+            taps, mixed, back = data[:, :LANES], data[:, LANES : 2 * LANES], data[:, 2 * LANES :]
+        taps_ref[i] = taps
+        rows_ref[0, i] = (q_ref[0, :, cols].astype(F32) * mixed).astype(BF16)
+        rows_ref[1, i] = (g_ref[0, :, cols].astype(F32) * mixed).astype(BF16)
+        rows_ref[2, i] = (back * v_ref[0, :, cols].astype(F32)).astype(BF16)
+        rows_ref[3, i] = (back * k_ref[0, :, cols].astype(F32)).astype(BF16)
+        for j, out in enumerate((o_hbm, gq_hbm, gk_hbm, gv_hbm)):
+            copies.append(pltpu.make_async_copy(rows_ref.at[j, i], out.at[0, :, cols], sems.at[j, i]))
+        copies.append(pltpu.make_async_copy(taps_ref.at[i], gf_hbm.at[:, cols], sems.at[4, i]))
         for copy in copies[-5:]:
             copy.start()
     for copy in copies:
@@ -141,12 +162,11 @@
     fin_ref,
 ):
     order = order_ref[...]
-    n_sig = KINDS * OWNED * SEQS
     for h in range(2):
         lo = 2 * h * TILE
         data = jnp.concatenate([got_ref[lo : lo + TILE, :], got_ref[lo + TILE : lo + 2 * TILE, :]], axis=1)
         sorted_rows = mm(order, data).astype(BF16)
-        for s in range(n_sig):
+        for s in range(SIGNALS):
             for u in range(2):
                 at = (2 * h + u) * GROUP
                 sig_ref[at : at + GROUP, s * LANES : (s + 1) * LANES] = sorted_rows[
@@ -168,16 +188,16 @@
         high, low = split(jnp.concatenate(halves, axis=0))
         return mm(high, sec_ref[0]) + mm(low, sec_ref[0]) + mm(high, sec_ref[1])
 
-    for p in range(KINDS * OWNED * SEQS // 2 - OWNED * SEQS // 2):
+    for p in range(OWNED * SEQS):
         data = sig_ref[:, 2 * p * LANES : 2 * (p + 1) * LANES]
         first = mm(fs_ref[...], jnp.concatenate([data, data], axis=0))
         spec_ref[2 * p * HALF : 2 * (p + 1) * HALF, :] = spectra(first)
 
     base = 2 * OWNED * SEQS
     terms = [
-        jnp.concatenate([sig(base + own * SEQS + term) for own in range(OWNED)], axis=1) for term in range(3)
+        jnp.concatenate([sig(base + own * HALVES + term) for own in range(OWNED)], axis=1) for term in range(2)
     ]
-    first = mm(ff_ref[...], jnp.concatenate([terms[0], terms[0], terms[1], terms[2]], axis=0))
+    first = mm(ff_ref[...], jnp.concatenate([terms[0], terms[0], terms[1]], axis=0))
     filter_spec = spectra(first)
 
     def inverse(pair):
@@ -224,8 +244,8 @@
         taps.append(jnp.concatenate([qr, qi], axis=1))
     res = inverse(taps)
     for own in range(OWNED):
-        for d in range(SEQS):
-            keep((2 * OWNED + own) * SEQS + d, res[:, own * LANES : (own + 1) * LANES])
+        for half in range(HALVES):
+            keep(base + own * HALVES + half, res[:, own * LANES : (own + 1) * LANES])
 
     back = back_ref[...]
     for h in range(2):
@@ -236,36 +256,36 @@
 
 
 def exchange(rows):
-    parts = rows.reshape(OWNERS * KINDS, OWNED, LANES)
-    parts = lax.all_to_all(parts, ("ctx", "dp"), split_axis=0, concat_axis=0, tiled=True)
+    parts = rows.reshape(OWNERS * PARTS, OWNED, LANES)
+    parts = lax.all_to_all(parts, ("ctx", "zh"), split_axis=0, concat_axis=0, tiled=True)
     return parts.reshape(OWNERS * CHUNK, LANES)
 
 
 def local(query, key_input, value_input, filter_taps, grad_output):
-    pick, order, back, first_signal, first_filter, twist, second, second_back, last = tables()
+    order, back, first_signal, first_filter, twist, second, second_back, last = tables()
     rows = jax.ShapeDtypeStruct((OWNERS * CHUNK, LANES), BF16)
     limit = pltpu.CompilerParams(vmem_limit_bytes=32 * 1024 * 1024)
     hbm = pl.BlockSpec(memory_space=pltpu.HBM)
-    inputs = (query, key_input, value_input, filter_taps, grad_output, jnp.asarray(pick))
-    sent = pl.pallas_call(
-        pack_kernel,
-        out_shape=rows,
-        in_specs=[hbm] * 6,
-        scratch_shapes=[
-            pltpu.VMEM((4,) + query.shape[1:], BF16),
-            pltpu.VMEM(filter_taps.shape, F32),
-            pltpu.VMEM(pick.shape, BF16),
-            pltpu.SemaphoreType.DMA((6,)),
-        ],
+    inputs = (query, key_input, value_input, grad_output)
+    gated, pick = pl.pallas_call(
+        gate_kernel,
+        out_shape=(
+            jax.ShapeDtypeStruct((2,) + query.shape[1:], BF16),
+            jax.ShapeDtypeStruct((CHUNK * HALF, PARTS * LANES), BF16),
+        ),
+        in_specs=[hbm] * 4,
+        scratch_shapes=[pltpu.VMEM((4,) + query.shape[1:], BF16), pltpu.SemaphoreType.DMA((4,))],
         compiler_params=limit,
-        name="pack",
+        name="gate",
     )(*[pltpu.with_memory_space_constraint(x, pltpu.HBM) for x in inputs])
+    other = lax.ppermute(gated, "core", SWAP)
+    sent = pl.pallas_call(pack_kernel, out_shape=rows, compiler_params=limit, name="pack")(gated, other, filter_taps, pick)
     got = exchange(sent)
     results = pl.pallas_call(
         conv_kernel,
         out_shape=rows,
         scratch_shapes=[
-            pltpu.VMEM((BLOCKS, KINDS * OWNED * SEQS * LANES), BF16),
+            pltpu.VMEM((BLOCKS, SIGNALS * LANES), BF16),
             pltpu.VMEM((2 * OWNED * SEQS * HALF, 2 * LANES), F32),
             pltpu.VMEM((2, TILE, 2 * LANES), BF16),
         ],
@@ -273,6 +293,7 @@
         name="conv",
     )(got, order, back, first_signal, first_filter, twist, second, second_back, last)
     returned = exchange(results)
+    swapped = lax.ppermute(returned, "core", SWAP)
     like = jax.ShapeDtypeStruct(query.shape, BF16)
     return pl.pallas_call(
         unpack_kernel,
@@ -285,15 +306,16 @@
         ],
         compiler_params=limit,
         name="unpack",
-    )(query, key_input, value_input, grad_output, returned, pick)
+    )(query, key_input, value_input, grad_output, returned, swapped, pick)
 
 
 def solution(mesh):
-    shared = P("dp", "ctx", None)
+    split = jax.sharding.Mesh(mesh.devices.reshape(BLOCKS, HALVES, CORES), ("ctx", "zh", "core"))
+    shared = P(("zh", "core"), "ctx", None)
     taps = P("ctx", None)
     return jax.shard_map(
         local,
-        mesh=mesh,
+        mesh=split,
         in_specs=(shared, shared, shared, taps, shared),
         out_specs=(shared, shared, shared, shared, taps),
         check_vma=False,

time: 67 us -> 66.4 us (level)
  blocking collectives: 58.2 us -> 48 us
  starting transfers between devices: 0 us -> 7.14 us
  waiting for transfers between devices: 0 us -> 2.42 us
    all_to_all x2, blocking collectives: 58.2 us -> 48 us  [exchange(): lax.all_to_all(parts, ('ctx', 'zh'), split_axis=0, concat_axis=0, tiled=T...]
    ppermute x0 -> x2, starting transfers between devices: none -> 7.14 us  [the longest x1 3.82 us: local(): swapped = lax.ppermute(returned, 'core', SWAP)]
    ppermute x0 -> x2, waiting for transfers between devices: none -> 2.42 us  [the longest x1 1.26 us: local(): swapped = lax.ppermute(returned, 'core', SWAP)]
    pallas_call x1 -> x2, Pallas kernels: 1.89 us -> 1.81 us  [the longest x1 1.2 us: local(): pl.pallas_call(gate_kernel, out_shape=(jax.ShapeDtypeStruct((2,) + query....]
  transfers between devices with their start and end apart: 0 -> 2, of which waited for: 0 -> 2; matrix products, arithmetic and copies ran while one was open for 0% -> 0% of each run, Pallas kernels for 0% -> 0%
where the time goes in v3:
time: 66.4 us; the launch traced here: 66.2 us
  blocking collectives  48 us (72%)
  Pallas kernels  7.77 us (12%)
  starting transfers between devices  7.14 us (11%)
  waiting for transfers between devices  2.42 us (4%)
  between operations  0.79 us (1%)
    all_to_all x2, blocking collectives, exchange(): lax.all_to_all(parts, ('ctx', 'zh'), split_axis=0, concat_axis=0, tiled=T...  48 us
    pallas_call x1, Pallas kernels, local(): pl.pallas_call(conv_kernel, out_shape=rows, scratch_shapes=[pltpu.VMEM((B...  4.48 us
    ppermute x1, starting transfers between devices, local(): swapped = lax.ppermute(returned, 'core', SWAP)  3.82 us
    ppermute x1, starting transfers between devices, local(): other = lax.ppermute(gated, 'core', SWAP)  3.33 us
    pallas_call x1, Pallas kernels, local(): pl.pallas_call(unpack_kernel, out_shape=(like, like, like, like, jax.Shap...  1.48 us
  transfers between devices with their start and end apart: 2, of which 2 were waited for; matrix products, arithmetic and copies ran while one was open for 0% of the time, Pallas kernels for 0%

profile of v3, /device:TPU:1, one launch (start us, length us, event | category | flops | bytes accessed | tf_op | source)
XLA Modules:
  0.0 66.2 jit_solution(12655043259888319844)
XLA Ops:
  0.6 0.0 copy-start.6
  0.6 1.2 %gate.1 = (bf16[2,128,512]{2,1,0:T(8,128)(2,1)S(1)}, bf16[640,640]{1,0:T(8,128)(2,1)S(1)}) custom-call(bf16[1,128,512]{2,1,0:T(8,128)(2,1)} %q_ref.1, bf16[1,128,512]{2,1,0:T(8,128)(2,1)} %k_ref.1, bf16[1,128,512]{2,1,0:T(8,128)(2,1)} %v_ref.1, bf16[1,128,512]{2,1,0:T(8,128)(2,1)} %g_ref.1), custom_call_target="tpu_custom_call" | custom-call | tf_op jit(solution)/shard_map/gate/pallas_call | solution.py:270
  1.9 3.3 %collective-permute-start = (bf16[2,128,512]{2,1,0:T(8,128)(2,1)S(1)}, bf16[2,128,512]{2,1,0:T(8,128)(2,1)S(1)}, u32[]{:S(2)}, u32[]{:S(2)}) collective-permute-start(bf16[2,128,512]{2,1,0:T(8,128)(2,1)S(1)} %get-tuple-element.7.own_ref), channel_id=1, source_target_pairs={{0,1},{1,0},{2,3},{3,2},{4,5},{5,4},{6,7},{7,6},{8,9},{9,8},{10,11... | collective-permute-start | bytes 786440 | tf_op jit(solution)/shard_map/ppermute | solution.py:281
  5.2 1.2 %collective-permute-done.other_ref = bf16[2,128,512]{2,1,0:T(8,128)(2,1)S(1)} collective-permute-done((bf16[2,128,512]{2,1,0:T(8,128)(2,1)S(1)}, bf16[2,128,512]{2,1,0:T(8,128)(2,1)S(1)}, u32[]{:S(2)}, u32[]{:S(2)}) %collective-permute-start) | collective-permute-done | bytes 262176 | tf_op jit(solution)/shard_map/ppermute | solution.py:281
  6.3 0.0 copy-done.6
  6.4 0.0 copy-start.12
  6.4 0.6 pack.1
  7.0 0.0 copy-start.4
  7.0 0.0 copy-start.5
  7.0 0.0 copy-start.9
  7.0 0.0 copy-start.10
  7.0 28.4 %all_to_all.10 = bf16[640,2,128]{2,1,0:T(2,128)(2,1)S(1)} all-to-all(bf16[640,2,128]{2,1,0:T(2,128)(2,1)S(1)} %bitcast.8), channel_id=1, replica_groups=mesh['ctx'=64,'zh'=2,'core'=2] {'ctx','zh'}, dimensions={0} | all-to-all | bytes 655360 | tf_op jit(solution)/shard_map/all_to_all | solution.py:260
  35.4 0.0 copy-done.7
  35.4 0.0 copy-done.8
  35.4 0.0 copy-done.11
  35.4 0.0 copy-done.12
  35.4 0.0 copy-done.4
  35.4 0.0 copy-done.5
  35.4 0.0 copy-done.9
  35.4 0.0 copy-done.10
  35.4 4.5 %conv.1 = bf16[1280,128]{1,0:T(8,128)(2,1)S(1)} custom-call(bf16[1280,128]{1,0:T(8,128)(2,1)S(1)} %bitcast.4, bf16[320,320]{1,0:T(8,128)(2,1)S(1)} %copy-done.8, bf16[320,320]{1,0:T(8,128)(2,1)S(1)} %copy-done.7, bf16[128,128]{1,0:T(8,128)(2,1)S(1)} %copy-done.12, bf16[128,192]{1,0:T(8,128)(2,1)S(1)} %copy-done.10, f32[128,128]{1,0:T(8,128)S(1)} %copy-done.9, ...), custom_call_target="tpu_custom_call" | custom-call | tf_op jit(solution)/shard_map/conv/pallas_call | solution.py:284
  39.9 0.0 copy-start
  39.9 0.0 copy-start.1
  40.0 0.0 copy-start.2
  40.0 0.0 copy-start.3
  40.0 19.6 %all_to_all.11 = bf16[640,2,128]{2,1,0:T(2,128)(2,1)S(1)} all-to-all(bf16[640,2,128]{2,1,0:T(2,128)(2,1)S(1)} %bitcast.5), channel_id=1, replica_groups=mesh['ctx'=64,'zh'=2,'core'=2] {'ctx','zh'}, dimensions={0} | all-to-all | bytes 655360 | tf_op jit(solution)/shard_map/all_to_all | solution.py:260
  59.6 3.8 %collective-permute-start.1 = (bf16[1280,128]{1,0:T(8,128)(2,1)S(1)}, bf16[1280,128]{1,0:T(8,128)(2,1)S(1)}, u32[]{:S(2)}, u32[]{:S(2)}) collective-permute-start(bf16[1280,128]{1,0:T(8,128)(2,1)S(1)} %bitcast.6), channel_id=1, source_target_pairs={{0,1},{1,0},{2,3},{3,2},{4,5},{5,4},{6,7},{7,6},{8,9},{9,8},{10,11... | collective-permute-start | bytes 983048 | tf_op jit(solution)/shard_map/ppermute | solution.py:296
  63.4 1.3 %collective-permute-done.1.other_ref = bf16[1280,128]{1,0:T(8,128)(2,1)S(1)} collective-permute-done((bf16[1280,128]{1,0:T(8,128)(2,1)S(1)}, bf16[1280,128]{1,0:T(8,128)(2,1)S(1)}, u32[]{:S(2)}, u32[]{:S(2)}) %collective-permute-start.1) | collective-permute-done | bytes 327712 | tf_op jit(solution)/shard_map/ppermute | solution.py:296
  64.7 0.0 copy-done
  64.7 0.0 copy-done.1
  64.7 0.0 copy-done.2
  64.7 1.5 %unpack.1 = (bf16[1,128,512]{2,1,0:T(8,128)(2,1)}, bf16[1,128,512]{2,1,0:T(8,128)(2,1)}, bf16[1,128,512]{2,1,0:T(8,128)(2,1)}, bf16[1,128,512]{2,1,0:T(8,128)(2,1)}, f32[128,512]{1,0:T(8,128)}) custom-call(bf16[1,128,512]{2,1,0:T(8,128)(2,1)S(1)} %copy-done, bf16[1,128,512]{2,1,0:T(8,128)(2,1)S(1)} %copy-done.1, bf16[1,128,512]{2,1,0:T(8,128)(2,1)S(1)} %copy-done.2, ...), custom_call_target="tpu_custom_call" | custom-call | tf_op jit(solution)/shard_map/unpack/pallas_call | solution.py:298
  (4 shorter events, 0.0 us)
Async XLA Ops:
  0.6 5.7 %copy-start.6 = (f32[128,512]{1,0:T(8,128)S(1)}, f32[128,512]{1,0:T(8,128)}, u32[]{:S(2)}) copy-start(f32[128,512]{1,0:T(8,128)} %f_ref.1) | copy-start | bytes 786436
  1.9 4.5 %collective-permute-start = (bf16[2,128,512]{2,1,0:T(8,128)(2,1)S(1)}, bf16[2,128,512]{2,1,0:T(8,128)(2,1)S(1)}, u32[]{:S(2)}, u32[]{:S(2)}) collective-permute-start(bf16[2,128,512]{2,1,0:T(8,128)(2,1)S(1)} %get-tuple-element.7.own_ref), channel_id=1, source_target_pairs={{0,1},{1,0},{2,3},{3,2},{4,5},{5,4},{6,7},{7,6},{8,9},{9,8},{10,11... | collective-permute-start | bytes 786440 | tf_op jit(solution)/shard_map/ppermute | solution.py:281
  6.3 29.0 %copy-start.7 = (bf16[320,320]{1,0:T(8,128)(2,1)S(1)}, bf16[320,320]{1,0:T(8,128)(2,1)}, u32[]{:S(2)}) copy-start(bf16[320,320]{1,0:T(8,128)(2,1)} %constant.17.clone.back_ref) | copy-start | bytes 614404
  6.3 29.0 %copy-start.8 = (bf16[320,320]{1,0:T(8,128)(2,1)S(1)}, bf16[320,320]{1,0:T(8,128)(2,1)}, u32[]{:S(2)}) copy-start(bf16[320,320]{1,0:T(8,128)(2,1)} %constant.16.clone.order_ref) | copy-start | bytes 614404
  6.4 29.0 %copy-start.11 = (bf16[64,384]{1,0:T(8,128)(2,1)S(1)}, bf16[64,384]{1,0:T(8,128)(2,1)}, u32[]{:S(2)}) copy-start(bf16[64,384]{1,0:T(8,128)(2,1)} %constant.23.clone.last_ref) | copy-start | bytes 147460
  6.4 29.0 %copy-start.12 = (bf16[128,128]{1,0:T(8,128)(2,1)S(1)}, bf16[128,128]{1,0:T(8,128)(2,1)}, u32[]{:S(2)}) copy-start(bf16[128,128]{1,0:T(8,128)(2,1)} %constant.18.clone.fs_ref) | copy-start | bytes 98308
  7.0 28.4 %copy-start.4 = (bf16[2,256,256]{2,1,0:T(8,128)(2,1)S(1)}, bf16[2,256,256]{2,1,0:T(8,128)(2,1)}, u32[]{:S(2)}) copy-start(bf16[2,256,256]{2,1,0:T(8,128)(2,1)} %constant.22.clone.secb_ref) | copy-start | bytes 786436
  7.0 28.4 %copy-start.5 = (bf16[2,256,256]{2,1,0:T(8,128)(2,1)S(1)}, bf16[2,256,256]{2,1,0:T(8,128)(2,1)}, u32[]{:S(2)}) copy-start(bf16[2,256,256]{2,1,0:T(8,128)(2,1)} %constant.21.clone.sec_ref) | copy-start | bytes 786436
  7.0 28.4 %copy-start.9 = (f32[128,128]{1,0:T(8,128)S(1)}, f32[128,128]{1,0:T(8,128)}, u32[]{:S(2)}) copy-start(f32[128,128]{1,0:T(8,128)} %constant.20.clone.tw_ref) | copy-start | bytes 196612
  7.0 28.4 %copy-start.10 = (bf16[128,192]{1,0:T(8,128)(2,1)S(1)}, bf16[128,192]{1,0:T(8,128)(2,1)}, u32[]{:S(2)}) copy-start(bf16[128,192]{1,0:T(8,128)(2,1)} %constant.19.clone.ff_ref) | copy-start | bytes 147460
  39.9 24.7 %copy-start = (bf16[1,128,512]{2,1,0:T(8,128)(2,1)S(1)}, bf16[1,128,512]{2,1,0:T(8,128)(2,1)}, u32[]{:S(2)}) copy-start(bf16[1,128,512]{2,1,0:T(8,128)(2,1)} %q_ref.1) | copy-start | bytes 393220
  39.9 24.7 %copy-start.1 = (bf16[1,128,512]{2,1,0:T(8,128)(2,1)S(1)}, bf16[1,128,512]{2,1,0:T(8,128)(2,1)}, u32[]{:S(2)}) copy-start(bf16[1,128,512]{2,1,0:T(8,128)(2,1)} %k_ref.1) | copy-start | bytes 393220
  40.0 24.7 %copy-start.2 = (bf16[1,128,512]{2,1,0:T(8,128)(2,1)S(1)}, bf16[1,128,512]{2,1,0:T(8,128)(2,1)}, u32[]{:S(2)}) copy-start(bf16[1,128,512]{2,1,0:T(8,128)(2,1)} %v_ref.1) | copy-start | bytes 393220
  40.0 24.7 %copy-start.3 = (bf16[1,128,512]{2,1,0:T(8,128)(2,1)S(1)}, bf16[1,128,512]{2,1,0:T(8,128)(2,1)}, u32[]{:S(2)}) copy-start(bf16[1,128,512]{2,1,0:T(8,128)(2,1)} %g_ref.1) | copy-start | bytes 393220
  59.6 5.1 %collective-permute-start.1 = (bf16[1280,128]{1,0:T(8,128)(2,1)S(1)}, bf16[1280,128]{1,0:T(8,128)(2,1)S(1)}, u32[]{:S(2)}, u32[]{:S(2)}) collective-permute-start(bf16[1280,128]{1,0:T(8,128)(2,1)S(1)} %bitcast.6), channel_id=1, source_target_pairs={{0,1},{1,0},{2,3},{3,2},{4,5},{5,4},{6,7},{7,6},{8,9},{9,8},{10,11... | collective-permute-start | bytes 983048 | tf_op jit(solution)/shard_map/ppermute | solution.py:296

commit v4 on v2

v4 whole, which is shorter than its diff:
```python
import functools

import jax
import jax.numpy as jnp
import ml_dtypes
import numpy as np
from jax import lax
from jax.experimental import pallas as pl
from jax.experimental.pallas import tpu as pltpu
from jax.sharding import PartitionSpec as P

BF16 = jnp.bfloat16
F32 = jnp.float32

BLOCKS = 64
LANES = 128
ROWS = 128
HALF = 64
SEQS = 4
C = 512
CORES = 2
HALVES = 2
KINDS = 3
OWNERS = 256
OWNED = C // OWNERS
GROUP = 16
IN_ROWS = KINDS * OWNED
IN_TILE = GROUP * HALVES * IN_ROWS
PARTS = 5
OUT_ROWS = PARTS * OWNED
OUT_TILE = GROUP * HALVES * OUT_ROWS
TARGETS = OWNERS // CORES
SWAP = ((0, 1), (1, 0))


def two_terms(table):
    high = table.astype(ml_dtypes.bfloat16)
    low = (table - high.astype(np.float64)).astype(ml_dtypes.bfloat16)
    return high, low


def tables():
    k1 = np.arange(HALF)[:, None] + 0.5
    angle1 = 2.0 * np.pi * k1 * np.arange(BLOCKS)[None, :] / ROWS
    first = np.concatenate([np.cos(angle1), -np.sin(angle1)], axis=0)
    first_high, first_low = two_terms(first)
    first_signal = np.concatenate([first_high, first_low], axis=1)
    first_filter = np.concatenate([first_high, first_low, first_high, first_high], axis=1)
    angle_t = 2.0 * np.pi * k1 * np.arange(LANES)[None, :] / (ROWS * LANES)
    twist = np.concatenate([np.cos(angle_t), -np.sin(angle_t)], axis=0).astype(np.float32)
    index = np.arange(LANES)
    angle2 = 2.0 * np.pi * ((index[:, None] * index[None, :]) % LANES) / LANES
    cos2, sin2 = np.cos(angle2), np.sin(angle2)
    second = np.block([[cos2, -sin2], [sin2, cos2]])
    second_back = np.block([[cos2, sin2], [-sin2, cos2]])
    last = np.concatenate([np.cos(angle1.T), -np.sin(angle1.T)], axis=1) * (2.0 / (ROWS * LANES))
    last_high, last_low = two_terms(last)
    last_stack = np.concatenate([last_high, last_high, last_low], axis=1)
    row = np.arange(IN_ROWS * HALF)
    pick = np.zeros((IN_ROWS * HALF, KINDS * LANES))
    pick[row, (row % IN_ROWS // OWNED) * LANES + OWNED * (row // IN_ROWS) + row % OWNED] = 1.0
    line = np.arange(IN_TILE)
    slot = line % IN_ROWS * HALVES + line // IN_ROWS % HALVES
    order = np.zeros((IN_TILE, IN_TILE))
    order[slot * GROUP + line // (HALVES * IN_ROWS), line] = 1.0
    line = np.arange(OUT_TILE)
    half = line % (HALVES * OUT_ROWS) // OUT_ROWS
    part = line % OUT_ROWS // OWNED
    own = line % OWNED
    slot = np.where(
        part == 4, 2 * OWNED * SEQS + own * HALVES + half, (part % 2 * OWNED + own) * SEQS + half * CORES + part // 2
    )
    back = np.zeros((OUT_TILE, OUT_TILE))
    back[line, slot * GROUP + line // (HALVES * OUT_ROWS)] = 1.0
    row = np.arange(OUT_ROWS * HALF)
    own = OWNED * (row // OUT_ROWS) + row % OWNED
    part = row % OUT_ROWS // OWNED
    sort = np.zeros((CORES, OUT_ROWS * HALF, KINDS * LANES))
    for core in range(CORES):
        for kind, wanted in enumerate((2 * core, 2 * core + 1, 4)):
            sort[core, row[part == wanted], kind * LANES + own[part == wanted]] = 1.0
    high, low = two_terms(second)
    back_high, back_low = two_terms(second_back)
    return (
        pick.astype(ml_dtypes.bfloat16),
        sort.astype(ml_dtypes.bfloat16),
        order.astype(ml_dtypes.bfloat16),
        back.astype(ml_dtypes.bfloat16),
        first_signal,
        first_filter,
        twist,
        np.concatenate([high, high, low], axis=0),
        np.concatenate([back_high, back_high, back_low], axis=0),
        last_stack,
    )


def mm(a, b, dims=((1,), (0,))):
    return lax.dot_general(a, b, (dims, ((), ())), preferred_element_type=F32)


def pack_kernel(q_hbm, k_hbm, v_hbm, f_hbm, g_hbm, pick_hbm, out_ref, in_ref, f_ref, pick_ref, sems):
    copies = [pltpu.make_async_copy(src.at[0], in_ref.at[i], sems.at[i]) for i, src in enumerate((k_hbm, v_hbm, g_hbm, q_hbm))]
    copies.append(pltpu.make_async_copy(f_hbm, f_ref, sems.at[4]))
    copies.append(pltpu.make_async_copy(pick_hbm, pick_ref, sems.at[5]))
    for copy in copies:
        copy.start()
    term = lax.axis_index("core") * HALVES + lax.axis_index("zh")
    for copy in copies:
        copy.wait()
    for b in range(C // LANES):
        cols = slice(b * LANES, (b + 1) * LANES)
        product = (in_ref[0, :, cols].astype(F32) * in_ref[1, :, cols].astype(F32)).astype(BF16)
        grad_mix = (in_ref[2, :, cols].astype(F32) * in_ref[3, :, cols].astype(F32)).astype(BF16)
        taps = f_ref[:, cols]
        high = taps.astype(BF16).astype(F32)
        rest = taps - high
        middle = rest.astype(BF16).astype(F32)
        part = jnp.where(term == 0, high, jnp.where(term == 1, middle, rest - middle)).astype(BF16)
        rows = mm(pick_ref[...], jnp.concatenate([product, grad_mix, part], axis=1), ((1,), (1,)))
        out_ref[b * IN_ROWS * HALF : (b + 1) * IN_ROWS * HALF, :] = rows.astype(BF16)


def unpack_kernel(own, q_ref, k_ref, v_ref, g_ref, got_ref, sort_ref, *refs):
    o_hbm, gq_hbm, gk_hbm, gv_hbm, gf_hbm, rows_ref, taps_ref, sems = refs[-8:]
    core = lax.axis_index("core")
    owners = core if own else 1 - core
    copies = []
    for b in range(C // CORES // LANES):
        cols = pl.ds(pl.multiple_of(owners * (C // CORES) + b * LANES, LANES), LANES)
        got = got_ref[b * OUT_ROWS * HALF : (b + 1) * OUT_ROWS * HALF, :]
        data = mm(got, sort_ref[core], ((0,), (0,)))
        mixed, back = data[:, :LANES], data[:, LANES : 2 * LANES]
        taps_ref[b] = data[:, 2 * LANES :]
        rows_ref[0, b] = (q_ref[0, :, cols].astype(F32) * mixed).astype(BF16)
        rows_ref[1, b] = (g_ref[0, :, cols].astype(F32) * mixed).astype(BF16)
        rows_ref[2, b] = (back * v_ref[0, :, cols].astype(F32)).astype(BF16)
        rows_ref[3, b] = (back * k_ref[0, :, cols].astype(F32)).astype(BF16)
        for j, out in enumerate((o_hbm, gq_hbm, gk_hbm, gv_hbm)):
            copies.append(pltpu.make_async_copy(rows_ref.at[j, b], out.at[0, :, cols], sems.at[j, b]))
        copies.append(pltpu.make_async_copy(taps_ref.at[b], gf_hbm.at[:, cols], sems.at[4, b]))
        for copy in copies[-5:]:
            copy.start()
    for copy in copies:
        copy.wait()


def split(x):
    high = x.astype(BF16)
    low = (x - high.astype(F32)).astype(BF16)
    return high, low


def conv_kernel(
    got_ref,
    order_ref,
    back_ref,
    fs_ref,
    ff_ref,
    tw_ref,
    sec_ref,
    secb_ref,
    last_ref,
    out_ref,
    sig_ref,
    spec_ref,
    inv_ref,
    fin_ref,
):
    order = order_ref[...]
    for core in range(CORES):
        for h in range(2):
            lo = (2 * core + h) * 2 * IN_TILE
            data = jnp.concatenate([got_ref[lo : lo + IN_TILE, :], got_ref[lo + IN_TILE : lo + 2 * IN_TILE, :]], axis=1)
            sorted_rows = mm(order, data).astype(BF16)
            for kind in range(KINDS):
                for own in range(OWNED):
                    for half in range(HALVES):
                        seq = core * HALVES + half if kind == 2 else half * CORES + core
                        s = (kind * OWNED + own) * SEQS + seq
                        line = ((kind * OWNED + own) * HALVES + half) * GROUP
                        for u in range(2):
                            at = (2 * h + u) * GROUP
                            sig_ref[at : at + GROUP, s * LANES : (s + 1) * LANES] = sorted_rows[
                                line : line + GROUP, u * LANES : (u + 1) * LANES
                            ]

    def sig(s):
        return sig_ref[:, s * LANES : (s + 1) * LANES]

    wr = tw_ref[:HALF, :]
    wi = tw_ref[HALF:, :]

    def three(x):
        high, low = split(x)
        return jnp.concatenate([high, low, high], axis=1)

    def turned(first):
        halves = []
        for u in range(2):
            ar = first[:HALF, u * LANES : (u + 1) * LANES]
            ai = first[HALF:, u * LANES : (u + 1) * LANES]
            halves.append(jnp.concatenate([ar * wr - ai * wi, ar * wi + ai * wr], axis=1))
        return three(jnp.concatenate(halves, axis=0))

    base = 2 * OWNED * SEQS
    lines = []
    for p in range(OWNED * SEQS):
        data = sig_ref[:, 2 * p * LANES : 2 * (p + 1) * LANES]
        lines.append(turned(mm(fs_ref[...], jnp.concatenate([data, data], axis=0))))
    terms = [jnp.concatenate([sig(base + own * SEQS + term) for own in range(OWNED)], axis=1) for term in range(3)]
    lines.append(turned(mm(ff_ref[...], jnp.concatenate([terms[0], terms[0], terms[1], terms[2]], axis=0))))
    spec_ref[...] = mm(jnp.concatenate(lines, axis=0), sec_ref[...])

    def inverse(full):
        cols = []
        for u in range(2):
            br = full[u * HALF : (u + 1) * HALF, :LANES]
            bi = full[u * HALF : (u + 1) * HALF, LANES:]
            cols.append(jnp.concatenate([br * wr + bi * wi, bi * wr - br * wi], axis=0))
        high, low = split(jnp.concatenate(cols, axis=1))
        return mm(last_ref[...], jnp.concatenate([high, low, high], axis=0))

    def keep(s, values):
        values = values.astype(BF16)
        for b in range(BLOCKS // GROUP):
            fin_ref[b // 2, s * GROUP : (s + 1) * GROUP, (b % 2) * LANES : (b % 2 + 1) * LANES] = values[
                b * GROUP : (b + 1) * GROUP, :
            ]

    taps, lines, places = [], [], []
    for own in range(OWNED):
        at = (base + own) * HALF
        hr = spec_ref[at : at + HALF, :LANES]
        hi = spec_ref[at : at + HALF, LANES:]
        qr = jnp.zeros((HALF, LANES), F32)
        qi = jnp.zeros((HALF, LANES), F32)
        for half in range(HALVES):
            mixed_pair, back_pair = [], []
            for u in range(CORES):
                s = own * SEQS + half * CORES + u
                pr = spec_ref[s * HALF : (s + 1) * HALF, :LANES]
                pi = spec_ref[s * HALF : (s + 1) * HALF, LANES:]
                z = OWNED * SEQS + s
                gr = spec_ref[z * HALF : (z + 1) * HALF, :LANES]
                gi = spec_ref[z * HALF : (z + 1) * HALF, LANES:]
                mixed_pair.append(jnp.concatenate([hr * pr - hi * pi, hr * pi + hi * pr], axis=1))
                back_pair.append(jnp.concatenate([gr * hr + gi * hi, gi * hr - gr * hi], axis=1))
                qr = qr + (gr * pr + gi * pi)
                qi = qi + (gi * pr - gr * pi)
            for kind, pair in ((0, mixed_pair), (1, back_pair)):
                lines.append(three(jnp.concatenate(pair, axis=0)))
                s = (kind * OWNED + own) * SEQS + half * CORES
                places.append([(s,), (s + 1,)])
        taps.append(jnp.concatenate([qr, qi], axis=1))
    lines.append(three(jnp.concatenate(taps, axis=0)))
    places.append([[base + own * HALVES + half for half in range(HALVES)] for own in range(OWNED)])
    inv_ref[...] = mm(jnp.concatenate(lines, axis=0), secb_ref[...])
    for p, pair in enumerate(places):
        res = inverse(inv_ref[2 * p * HALF : 2 * (p + 1) * HALF, :])
        for u in range(2):
            for s in pair[u]:
                keep(s, res[:, u * LANES : (u + 1) * LANES])

    back = back_ref[...]
    for h in range(2):
        rows = mm(back, fin_ref[h]).astype(BF16)
        lo = 2 * h * OUT_TILE
        out_ref[lo : lo + OUT_TILE, :] = rows[:, :LANES]
        out_ref[lo + OUT_TILE : lo + 2 * OUT_TILE, :] = rows[:, LANES:]


def exchange(rows, axes):
    parts = rows.reshape(rows.shape[0] // OWNED, OWNED, LANES)
    parts = lax.all_to_all(parts, axes, split_axis=0, concat_axis=0, tiled=True)
    return parts.reshape(rows.shape)


def local(query, key_input, value_input, filter_taps, grad_output):
    pick, sort, order, back, first_signal, first_filter, twist, second, second_back, last = tables()
    limit = pltpu.CompilerParams(vmem_limit_bytes=32 * 1024 * 1024)
    hbm = pl.BlockSpec(memory_space=pltpu.HBM)
    inputs = (query, key_input, value_input, filter_taps, grad_output, jnp.asarray(pick))
    sent = pl.pallas_call(
        pack_kernel,
        out_shape=jax.ShapeDtypeStruct((OWNERS * IN_ROWS, LANES), BF16),
        in_specs=[hbm] * 6,
        scratch_shapes=[
            pltpu.VMEM((4,) + query.shape[1:], BF16),
            pltpu.VMEM(filter_taps.shape, F32),
            pltpu.VMEM(pick.shape, BF16),
            pltpu.SemaphoreType.DMA((6,)),
        ],
        compiler_params=limit,
        name="pack",
    )(*[pltpu.with_memory_space_constraint(x, pltpu.HBM) for x in inputs])
    got = exchange(sent, ("core", "ctx", "zh"))
    signals = (KINDS - 1) * OWNED * SEQS + OWNED
    results = pl.pallas_call(
        conv_kernel,
        out_shape=jax.ShapeDtypeStruct((TARGETS * OUT_ROWS, LANES), BF16),
        scratch_shapes=[
            pltpu.VMEM((BLOCKS, KINDS * OWNED * SEQS * LANES), BF16),
            pltpu.VMEM((signals * HALF, 2 * LANES), F32),
            pltpu.VMEM((signals * HALF, 2 * LANES), F32),
            pltpu.VMEM((2, OUT_TILE, 2 * LANES), BF16),
        ],
        compiler_params=limit,
        name="conv",
    )(got, order, back, first_signal, first_filter, twist, second, second_back, last)
    returned = exchange(results, ("ctx", "zh"))
    swapped = lax.ppermute(returned, "core", SWAP)
    like = jax.ShapeDtypeStruct(query.shape, BF16)
    unpack = functools.partial(
        pl.pallas_call,
        out_shape=(like, like, like, like, jax.ShapeDtypeStruct(filter_taps.shape, F32)),
        out_specs=[hbm] * 5,
        scratch_shapes=[
            pltpu.VMEM((4, C // CORES // LANES, LANES, LANES), BF16),
            pltpu.VMEM((C // CORES // LANES, LANES, LANES), F32),
            pltpu.SemaphoreType.DMA((5, C // CORES // LANES)),
        ],
        compiler_params=limit,
        cost_estimate=pl.CostEstimate(flops=10**9, bytes_accessed=2 * 10**6, transcendentals=0),
    )
    near = (query, key_input, value_input, grad_output)
    half = unpack(functools.partial(unpack_kernel, True), name="unpack_own")(*near, returned, sort)
    block = pl.BlockSpec(memory_space=pltpu.VMEM)
    return unpack(
        functools.partial(unpack_kernel, False),
        in_specs=[block] * 6 + [hbm] * 5,
        input_output_aliases={6 + i: i for i in range(5)},
        name="unpack_other",
    )(*near, swapped, sort, *half)


def solution(mesh):
    split = jax.sharding.Mesh(mesh.devices.reshape(BLOCKS, HALVES, CORES), ("ctx", "zh", "core"))
    shared = P(("zh", "core"), "ctx", None)
    taps = P("ctx", None)
    return jax.shard_map(
        local,
        mesh=split,
        in_specs=(shared, shared, shared, taps, shared),
        out_specs=(shared, shared, shared, shared, taps),
        check_vma=False,
    )
```

time: 67 us -> 64.9 us (0.969)
  blocking collectives: 58.2 us -> 53.9 us
  starting transfers between devices: 0 us -> 2.61 us
    all_to_all x2, blocking collectives: 58.2 us -> 53.9 us  [exchange(): parts = lax.all_to_all(parts, axes, split_axis=0, concat_axis=0, tiled=True)]
    ppermute x0 -> x1, starting transfers between devices: none -> 2.61 us  [local(): swapped = lax.ppermute(returned, 'core', SWAP)]
    pallas_call x3 -> x4, Pallas kernels: 7.71 us -> 7.28 us  [the longest x1 2.99 us: local(): pl.pallas_call(conv_kernel, out_shape=jax.ShapeDtypeStruct((TARGETS * OUT...]
  transfers between devices with their start and end apart: 0 -> 1, of which waited for: 0 -> 0; matrix products, arithmetic and copies ran while one was open for 0% -> 0% of each run, Pallas kernels for 0% -> 2%
where the time goes in v4:
time: 64.9 us; the launch traced here: 64.8 us
  blocking collectives  53.9 us (83%)
  Pallas kernels  7.28 us (11%)
  starting transfers between devices  2.61 us (4%)
  between operations  0.82 us (1%)
    all_to_all x2, blocking collectives, exchange(): parts = lax.all_to_all(parts, axes, split_axis=0, concat_axis=0, tiled=True)  53.9 us
    pallas_call x1, Pallas kernels, local(): pl.pallas_call(conv_kernel, out_shape=jax.ShapeDtypeStruct((TARGETS * OUT...  2.99 us
    ppermute x1, starting transfers between devices, local(): swapped = lax.ppermute(returned, 'core', SWAP)  2.61 us
    pallas_call x1, Pallas kernels, local(): pl.pallas_call(pack_kernel, out_shape=jax.ShapeDtypeStruct((OWNERS * IN_R...  1.94 us
  transfers between devices with their start and end apart: 1, of which 0 were waited for; matrix products, arithmetic and copies ran while one was open for 0% of the time, Pallas kernels for 2%

profile of v4, /device:TPU:1, one launch (start us, length us, event | category | flops | bytes accessed | tf_op | source)
XLA Modules:
  0.0 64.8 jit_solution(8156801343808060029)
XLA Ops:
  0.6 0.0 copy-start.2
  0.6 0.0 copy-start.7
  0.7 0.0 copy-start.8
  0.7 0.0 copy-start.9
  0.7 0.0 copy-start.10
  0.7 0.0 copy-start.11
  0.7 1.9 %pack.1 = bf16[1536,128]{1,0:T(8,128)(2,1)S(1)} custom-call(bf16[1,128,512]{2,1,0:T(8,128)(2,1)} %q_ref.3, bf16[1,128,512]{2,1,0:T(8,128)(2,1)} %k_ref.3, bf16[1,128,512]{2,1,0:T(8,128)(2,1)} %v_ref.3, f32[128,512]{1,0:T(8,128)} %f_hbm.1, bf16[1,128,512]{2,1,0:T(8,128)(2,1)} %g_ref.3, bf16[384,384]{1,0:T(8,128)(2,1)} %constant.20.clone.pick_hbm), custom_call_target="tpu_custom_call" | custom-call | tf_op jit(solution)/shard_map/pack/pallas_call | solution.py:284
  2.7 0.0 copy-start
  2.7 0.0 copy-start.1
  2.7 33.7 %all_to_all.10 = bf16[768,2,128]{2,1,0:T(2,128)(2,1)S(1)} all-to-all(bf16[768,2,128]{2,1,0:T(2,128)(2,1)S(1)} %bitcast.4), channel_id=1, replica_groups=mesh['ctx'=64,'zh'=2,'core'=2] {'core','ctx','zh'}, dimensions={0} | all-to-all | bytes 786432 | tf_op jit(solution)/shard_map/all_to_all | solution.py:275
  36.4 0.0 copy-done.2
  36.4 0.0 copy-done.7
  36.4 0.0 copy-done.8
  36.4 0.0 copy-done.9
  36.4 0.0 copy-done.10
  36.5 0.0 copy-done.11
  36.5 0.0 copy-done
  36.5 0.0 copy-done.1
  36.5 0.0 copy-start.12
  36.5 3.0 %conv.1 = bf16[1280,128]{1,0:T(8,128)(2,1)S(1)} custom-call(bf16[1536,128]{1,0:T(8,128)(2,1)S(1)} %bitcast.5, bf16[192,192]{1,0:T(8,128)(2,1)S(1)} %copy-done.7, bf16[320,320]{1,0:T(8,128)(2,1)S(1)} %copy-done.2, bf16[128,128]{1,0:T(8,128)(2,1)S(1)} %copy-done.11, bf16[128,256]{1,0:T(8,128)(2,1)S(1)} %copy-done.9, f32[128,128]{1,0:T(8,128)S(1)} %copy-done.8, ...), custom_call_target="tpu_custom_call" | custom-call | tf_op jit(solution)/shard_map/conv/pallas_call | solution.py:299
  39.5 0.0 copy-start.3
  39.5 0.0 copy-start.4
  39.5 0.0 copy-start.5
  39.5 0.0 copy-start.6
  39.5 20.2 %all_to_all.11 = bf16[640,2,128]{2,1,0:T(2,128)(2,1)S(1)} all-to-all(bf16[640,2,128]{2,1,0:T(2,128)(2,1)S(1)} %bitcast.6), channel_id=1, replica_groups=mesh['ctx'=64,'zh'=2,'core'=2] {'ctx','zh'}, dimensions={0} | all-to-all | bytes 655360 | tf_op jit(solution)/shard_map/all_to_all | solution.py:275
  59.7 2.6 %collective-permute-start = (bf16[1280,128]{1,0:T(8,128)(2,1)S(1)}, bf16[1280,128]{1,0:T(8,128)(2,1)S(1)}, u32[]{:S(2)}, u32[]{:S(2)}) collective-permute-start(bf16[1280,128]{1,0:T(8,128)(2,1)S(1)} %bitcast.7), channel_id=1, source_target_pairs={{0,1},{1,0},{2,3},{3,2},{4,5},{5,4},{6,7},{7,6},{8,9},{9,8},{10,11... | collective-permute-start | bytes 983048 | tf_op jit(solution)/shard_map/ppermute | solution.py:312
  62.3 0.0 copy-done.12
  62.3 0.0 copy-done.3
  62.4 0.0 copy-done.6
  62.4 1.2 %unpack_own.1 = (bf16[1,128,512]{2,1,0:T(8,128)(2,1)}, bf16[1,128,512]{2,1,0:T(8,128)(2,1)}, bf16[1,128,512]{2,1,0:T(8,128)(2,1)}, bf16[1,128,512]{2,1,0:T(8,128)(2,1)}, f32[128,512]{1,0:T(8,128)}) custom-call(bf16[1,128,512]{2,1,0:T(8,128)(2,1)S(1)} %copy-done.3, bf16[1,128,512]{2,1,0:T(8,128)(2,1)S(1)} %copy-done.4, bf16[1,128,512]{2,1,0:T(8,128)(2,1)S(1)} %copy-done.5, ...), custom_call_target="tpu_custom_call" | custom-call | flops 1000000000 | bytes 2000000 | tf_op jit(solution)/shard_map/unpack_own/pallas_call | solution.py:327
  63.5 0.0 collective-permute-done.got_ref
  63.6 1.2 %unpack_other.1 = (bf16[1,128,512]{2,1,0:T(8,128)(2,1)}, bf16[1,128,512]{2,1,0:T(8,128)(2,1)}, bf16[1,128,512]{2,1,0:T(8,128)(2,1)}, bf16[1,128,512]{2,1,0:T(8,128)(2,1)}, f32[128,512]{1,0:T(8,128)}) custom-call(bf16[1,128,512]{2,1,0:T(8,128)(2,1)S(1)} %copy-done.3, ...), custom_call_target="tpu_custom_call", output_to_operand_aliasing={{0}: (6, {}), {1}: (7, {}), {2}: (8, {}), {3}: (9, {}), {4}... | custom-call | flops 1000000000 | bytes 2000000 | tf_op jit(solution)/shard_map/unpack_other/pallas_call | solution.py:329
  (2 shorter events, 0.0 us)
Async XLA Ops:
  0.6 35.8 %copy-start.2 = (bf16[320,320]{1,0:T(8,128)(2,1)S(1)}, bf16[320,320]{1,0:T(8,128)(2,1)}, u32[]{:S(2)}) copy-start(bf16[320,320]{1,0:T(8,128)(2,1)} %constant.22.clone.back_ref) | copy-start | bytes 614404
  0.6 35.8 %copy-start.7 = (bf16[192,192]{1,0:T(8,128)(2,1)S(1)}, bf16[192,192]{1,0:T(8,128)(2,1)}, u32[]{:S(2)}) copy-start(bf16[192,192]{1,0:T(8,128)(2,1)} %constant.21.clone.order_ref) | copy-start | bytes 221188
  0.7 35.8 %copy-start.8 = (f32[128,128]{1,0:T(8,128)S(1)}, f32[128,128]{1,0:T(8,128)}, u32[]{:S(2)}) copy-start(f32[128,128]{1,0:T(8,128)} %constant.25.clone.tw_ref) | copy-start | bytes 196612
  0.7 35.8 %copy-start.9 = (bf16[128,256]{1,0:T(8,128)(2,1)S(1)}, bf16[128,256]{1,0:T(8,128)(2,1)}, u32[]{:S(2)}) copy-start(bf16[128,256]{1,0:T(8,128)(2,1)} %constant.24.clone.ff_ref) | copy-start | bytes 196612
  0.7 35.8 %copy-start.10 = (bf16[64,384]{1,0:T(8,128)(2,1)S(1)}, bf16[64,384]{1,0:T(8,128)(2,1)}, u32[]{:S(2)}) copy-start(bf16[64,384]{1,0:T(8,128)(2,1)} %constant.28.clone.last_ref) | copy-start | bytes 147460
  0.7 35.8 %copy-start.11 = (bf16[128,128]{1,0:T(8,128)(2,1)S(1)}, bf16[128,128]{1,0:T(8,128)(2,1)}, u32[]{:S(2)}) copy-start(bf16[128,128]{1,0:T(8,128)(2,1)} %constant.23.clone.fs_ref) | copy-start | bytes 98308
  2.7 33.8 %copy-start = (bf16[768,256]{1,0:T(8,128)(2,1)S(1)}, bf16[768,256]{1,0:T(8,128)(2,1)}, u32[]{:S(2)}) copy-start(bf16[768,256]{1,0:T(8,128)(2,1)} %constant.27.clone.secb_ref) | copy-start | bytes 1179652
  2.7 33.8 %copy-start.1 = (bf16[768,256]{1,0:T(8,128)(2,1)S(1)}, bf16[768,256]{1,0:T(8,128)(2,1)}, u32[]{:S(2)}) copy-start(bf16[768,256]{1,0:T(8,128)(2,1)} %constant.26.clone.sec_ref) | copy-start | bytes 1179652
  36.5 25.9 %copy-start.12 = (bf16[2,640,384]{2,1,0:T(8,128)(2,1)S(1)}, bf16[2,640,384]{2,1,0:T(8,128)(2,1)}, u32[]{:S(2)}) copy-start(bf16[2,640,384]{2,1,0:T(8,128)(2,1)} %constant.29.clone.sort_ref) | copy-start | bytes 2949124
  39.5 22.8 %copy-start.3 = (bf16[1,128,512]{2,1,0:T(8,128)(2,1)S(1)}, bf16[1,128,512]{2,1,0:T(8,128)(2,1)}, u32[]{:S(2)}) copy-start(bf16[1,128,512]{2,1,0:T(8,128)(2,1)} %q_ref.3) | copy-start | bytes 393220
  39.5 22.8 %copy-start.4 = (bf16[1,128,512]{2,1,0:T(8,128)(2,1)S(1)}, bf16[1,128,512]{2,1,0:T(8,128)(2,1)}, u32[]{:S(2)}) copy-start(bf16[1,128,512]{2,1,0:T(8,128)(2,1)} %k_ref.3) | copy-start | bytes 393220
  39.5 22.8 %copy-start.5 = (bf16[1,128,512]{2,1,0:T(8,128)(2,1)S(1)}, bf16[1,128,512]{2,1,0:T(8,128)(2,1)}, u32[]{:S(2)}) copy-start(bf16[1,128,512]{2,1,0:T(8,128)(2,1)} %v_ref.3) | copy-start | bytes 393220
  39.5 22.8 %copy-start.6 = (bf16[1,128,512]{2,1,0:T(8,128)(2,1)S(1)}, bf16[1,128,512]{2,1,0:T(8,128)(2,1)}, u32[]{:S(2)}) copy-start(bf16[1,128,512]{2,1,0:T(8,128)(2,1)} %g_ref.3) | copy-start | bytes 393220
  59.7 3.9 %collective-permute-start = (bf16[1280,128]{1,0:T(8,128)(2,1)S(1)}, bf16[1280,128]{1,0:T(8,128)(2,1)S(1)}, u32[]{:S(2)}, u32[]{:S(2)}) collective-permute-start(bf16[1280,128]{1,0:T(8,128)(2,1)S(1)} %bitcast.7), channel_id=1, source_target_pairs={{0,1},{1,0},{2,3},{3,2},{4,5},{5,4},{6,7},{7,6},{8,9},{9,8},{10,11... | collective-permute-start | bytes 983048 | tf_op jit(solution)/shard_map/ppermute | solution.py:312

commit v5 on v4

--- a/solution.py
+++ b/solution.py
@@ -21,15 +21,12 @@
 CORES = 2
 HALVES = 2
 KINDS = 3
-OWNERS = 256
-OWNED = C // OWNERS
+OWNERS = 128
+OWNED = C // CORES // OWNERS
 GROUP = 16
-IN_ROWS = KINDS * OWNED
-IN_TILE = GROUP * HALVES * IN_ROWS
 PARTS = 5
-OUT_ROWS = PARTS * OWNED
-OUT_TILE = GROUP * HALVES * OUT_ROWS
-TARGETS = OWNERS // CORES
+CHUNK = PARTS * OWNED
+TILE = GROUP * HALVES * CHUNK
 SWAP = ((0, 1), (1, 0))
 
 
@@ -45,7 +42,7 @@
     first = np.concatenate([np.cos(angle1), -np.sin(angle1)], axis=0)
     first_high, first_low = two_terms(first)
     first_signal = np.concatenate([first_high, first_low], axis=1)
-    first_filter = np.concatenate([first_high, first_low, first_high, first_high], axis=1)
+    first_filter = np.concatenate([first_high, first_low, first_high], axis=1)
     angle_t = 2.0 * np.pi * k1 * np.arange(LANES)[None, :] / (ROWS * LANES)
     twist = np.concatenate([np.cos(angle_t), -np.sin(angle_t)], axis=0).astype(np.float32)
     index = np.arange(LANES)
@@ -56,36 +53,28 @@
     last = np.concatenate([np.cos(angle1.T), -np.sin(angle1.T)], axis=1) * (2.0 / (ROWS * LANES))
     last_high, last_low = two_terms(last)
     last_stack = np.concatenate([last_high, last_high, last_low], axis=1)
-    row = np.arange(IN_ROWS * HALF)
-    pick = np.zeros((IN_ROWS * HALF, KINDS * LANES))
-    pick[row, (row % IN_ROWS // OWNED) * LANES + OWNED * (row // IN_ROWS) + row % OWNED] = 1.0
-    line = np.arange(IN_TILE)
-    slot = line % IN_ROWS * HALVES + line // IN_ROWS % HALVES
-    order = np.zeros((IN_TILE, IN_TILE))
-    order[slot * GROUP + line // (HALVES * IN_ROWS), line] = 1.0
-    line = np.arange(OUT_TILE)
-    half = line % (HALVES * OUT_ROWS) // OUT_ROWS
-    part = line % OUT_ROWS // OWNED
+    line = np.arange(TILE)
+    half = line % (HALVES * CHUNK) // CHUNK
+    part = line % CHUNK // OWNED
     own = line % OWNED
     slot = np.where(
         part == 4, 2 * OWNED * SEQS + own * HALVES + half, (part % 2 * OWNED + own) * SEQS + half * CORES + part // 2
     )
-    back = np.zeros((OUT_TILE, OUT_TILE))
-    back[line, slot * GROUP + line // (HALVES * OUT_ROWS)] = 1.0
-    row = np.arange(OUT_ROWS * HALF)
-    own = OWNED * (row // OUT_ROWS) + row % OWNED
-    part = row % OUT_ROWS // OWNED
-    sort = np.zeros((CORES, OUT_ROWS * HALF, KINDS * LANES))
-    for core in range(CORES):
-        for kind, wanted in enumerate((2 * core, 2 * core + 1, 4)):
-            sort[core, row[part == wanted], kind * LANES + own[part == wanted]] = 1.0
+    order = np.zeros((TILE, TILE))
+    order[slot * GROUP + line // (HALVES * CHUNK), line] = 1.0
+    row = np.arange(CHUNK * HALF)
+    own = OWNED * (row // CHUNK) + row % OWNED
+    part = row % CHUNK // OWNED
+    sort = np.zeros((CORES, CHUNK * HALF, KINDS * LANES))
+    for whose in range(CORES):
+        for kind, wanted in enumerate((2 * whose, 2 * whose + 1, 4)):
+            sort[whose, row[part == wanted], kind * LANES + own[part == wanted]] = 1.0
     high, low = two_terms(second)
     back_high, back_low = two_terms(second_back)
     return (
-        pick.astype(ml_dtypes.bfloat16),
         sort.astype(ml_dtypes.bfloat16),
         order.astype(ml_dtypes.bfloat16),
-        back.astype(ml_dtypes.bfloat16),
+        np.ascontiguousarray(order.T).astype(ml_dtypes.bfloat16),
         first_signal,
         first_filter,
         twist,
@@ -99,26 +88,39 @@
     return lax.dot_general(a, b, (dims, ((), ())), preferred_element_type=F32)
 
 
-def pack_kernel(q_hbm, k_hbm, v_hbm, f_hbm, g_hbm, pick_hbm, out_ref, in_ref, f_ref, pick_ref, sems):
+def columns(core, b):
+    return pl.ds(pl.multiple_of(core * (C // CORES) + b * LANES, LANES), LANES)
+
+
+def gate_kernel(q_hbm, k_hbm, v_hbm, g_hbm, out_ref, pick_ref, in_ref, sems):
     copies = [pltpu.make_async_copy(src.at[0], in_ref.at[i], sems.at[i]) for i, src in enumerate((k_hbm, v_hbm, g_hbm, q_hbm))]
-    copies.append(pltpu.make_async_copy(f_hbm, f_ref, sems.at[4]))
-    copies.append(pltpu.make_async_copy(pick_hbm, pick_ref, sems.at[5]))
     for copy in copies:
         copy.start()
-    term = lax.axis_index("core") * HALVES + lax.axis_index("zh")
-    for copy in copies:
-        copy.wait()
-    for b in range(C // LANES):
-        cols = slice(b * LANES, (b + 1) * LANES)
-        product = (in_ref[0, :, cols].astype(F32) * in_ref[1, :, cols].astype(F32)).astype(BF16)
-        grad_mix = (in_ref[2, :, cols].astype(F32) * in_ref[3, :, cols].astype(F32)).astype(BF16)
+    row = lax.broadcasted_iota(jnp.int32, (CHUNK * HALF, LANES), 0)
+    lane = lax.broadcasted_iota(jnp.int32, (CHUNK * HALF, LANES), 1)
+    first = (lane >> 1) * CHUNK + (lane & 1)
+    for part in range(PARTS):
+        chosen = jnp.where(row == first + OWNED * part, 1.0, 0.0)
+        pick_ref[:, part * LANES : (part + 1) * LANES] = chosen.astype(BF16)
+    for i in range(2):
+        copies[2 * i].wait()
+        copies[2 * i + 1].wait()
+        out_ref[i] = (in_ref[2 * i].astype(F32) * in_ref[2 * i + 1].astype(F32)).astype(BF16)
+
+
+def pack_kernel(gated_ref, q_ref, k_ref, v_ref, g_ref, f_ref, pick_ref, out_ref):
+    core = lax.axis_index("core")
+    term = lax.axis_index("zh")
+    for b in range(C // CORES // LANES):
+        cols = columns(core, b)
+        product = (k_ref[0, :, cols].astype(F32) * v_ref[0, :, cols].astype(F32)).astype(BF16)
+        grad_mix = (g_ref[0, :, cols].astype(F32) * q_ref[0, :, cols].astype(F32)).astype(BF16)
         taps = f_ref[:, cols]
         high = taps.astype(BF16).astype(F32)
-        rest = taps - high
-        middle = rest.astype(BF16).astype(F32)
-        part = jnp.where(term == 0, high, jnp.where(term == 1, middle, rest - middle)).astype(BF16)
-        rows = mm(pick_ref[...], jnp.concatenate([product, grad_mix, part], axis=1), ((1,), (1,)))
-        out_ref[b * IN_ROWS * HALF : (b + 1) * IN_ROWS * HALF, :] = rows.astype(BF16)
+        part = jnp.where(term == 0, high, taps - high).astype(BF16)
+        data = [gated_ref[0, :, cols], gated_ref[1, :, cols], product, grad_mix, part]
+        rows = mm(pick_ref[...], jnp.concatenate(data, axis=1), ((1,), (1,)))
+        out_ref[b * CHUNK * HALF : (b + 1) * CHUNK * HALF, :] = rows.astype(BF16)
 
 
 def unpack_kernel(own, q_ref, k_ref, v_ref, g_ref, got_ref, sort_ref, *refs):
@@ -127,9 +129,9 @@
     owners = core if own else 1 - core
     copies = []
     for b in range(C // CORES // LANES):
-        cols = pl.ds(pl.multiple_of(owners * (C // CORES) + b * LANES, LANES), LANES)
-        got = got_ref[b * OUT_ROWS * HALF : (b + 1) * OUT_ROWS * HALF, :]
-        data = mm(got, sort_ref[core], ((0,), (0,)))
+        cols = columns(owners, b)
+        got = got_ref[b * CHUNK * HALF : (b + 1) * CHUNK * HALF, :]
+        data = mm(got, sort_ref[0 if own else 1], ((0,), (0,)))
         mixed, back = data[:, :LANES], data[:, LANES : 2 * LANES]
         taps_ref[b] = data[:, 2 * LANES :]
         rows_ref[0, b] = (q_ref[0, :, cols].astype(F32) * mixed).astype(BF16)
@@ -168,22 +170,16 @@
     fin_ref,
 ):
     order = order_ref[...]
-    for core in range(CORES):
-        for h in range(2):
-            lo = (2 * core + h) * 2 * IN_TILE
-            data = jnp.concatenate([got_ref[lo : lo + IN_TILE, :], got_ref[lo + IN_TILE : lo + 2 * IN_TILE, :]], axis=1)
-            sorted_rows = mm(order, data).astype(BF16)
-            for kind in range(KINDS):
-                for own in range(OWNED):
-                    for half in range(HALVES):
-                        seq = core * HALVES + half if kind == 2 else half * CORES + core
-                        s = (kind * OWNED + own) * SEQS + seq
-                        line = ((kind * OWNED + own) * HALVES + half) * GROUP
-                        for u in range(2):
-                            at = (2 * h + u) * GROUP
-                            sig_ref[at : at + GROUP, s * LANES : (s + 1) * LANES] = sorted_rows[
-                                line : line + GROUP, u * LANES : (u + 1) * LANES
-                            ]
+    for h in range(2):
+        lo = 2 * h * TILE
+        data = jnp.concatenate([got_ref[lo : lo + TILE, :], got_ref[lo + TILE : lo + 2 * TILE, :]], axis=1)
+        sorted_rows = mm(order, data).astype(BF16)
+        for s in range(HALVES * CHUNK):
+            for u in range(2):
+                at = (2 * h + u) * GROUP
+                sig_ref[at : at + GROUP, s * LANES : (s + 1) * LANES] = sorted_rows[
+                    s * GROUP : (s + 1) * GROUP, u * LANES : (u + 1) * LANES
+                ]
 
     def sig(s):
         return sig_ref[:, s * LANES : (s + 1) * LANES]
@@ -208,8 +204,8 @@
     for p in range(OWNED * SEQS):
         data = sig_ref[:, 2 * p * LANES : 2 * (p + 1) * LANES]
         lines.append(turned(mm(fs_ref[...], jnp.concatenate([data, data], axis=0))))
-    terms = [jnp.concatenate([sig(base + own * SEQS + term) for own in range(OWNED)], axis=1) for term in range(3)]
-    lines.append(turned(mm(ff_ref[...], jnp.concatenate([terms[0], terms[0], terms[1], terms[2]], axis=0))))
+    terms = [jnp.concatenate([sig(base + own * HALVES + term) for own in range(OWNED)], axis=1) for term in range(2)]
+    lines.append(turned(mm(ff_ref[...], jnp.concatenate([terms[0], terms[0], terms[1]], axis=0))))
     spec_ref[...] = mm(jnp.concatenate(lines, axis=0), sec_ref[...])
 
     def inverse(full):
@@ -265,50 +261,52 @@
     back = back_ref[...]
     for h in range(2):
         rows = mm(back, fin_ref[h]).astype(BF16)
-        lo = 2 * h * OUT_TILE
-        out_ref[lo : lo + OUT_TILE, :] = rows[:, :LANES]
-        out_ref[lo + OUT_TILE : lo + 2 * OUT_TILE, :] = rows[:, LANES:]
-
-
-def exchange(rows, axes):
+        lo = 2 * h * TILE
+        out_ref[lo : lo + TILE, :] = rows[:, :LANES]
+        out_ref[lo + TILE : lo + 2 * TILE, :] = rows[:, LANES:]
+
+
+def exchange(rows):
     parts = rows.reshape(rows.shape[0] // OWNED, OWNED, LANES)
-    parts = lax.all_to_all(parts, axes, split_axis=0, concat_axis=0, tiled=True)
+    parts = lax.all_to_all(parts, ("ctx", "zh"), split_axis=0, concat_axis=0, tiled=True)
     return parts.reshape(rows.shape)
 
 
 def local(query, key_input, value_input, filter_taps, grad_output):
-    pick, sort, order, back, first_signal, first_filter, twist, second, second_back, last = tables()
+    sort, order, back, first_signal, first_filter, twist, second, second_back, last = tables()
     limit = pltpu.CompilerParams(vmem_limit_bytes=32 * 1024 * 1024)
     hbm = pl.BlockSpec(memory_space=pltpu.HBM)
-    inputs = (query, key_input, value_input, filter_taps, grad_output, jnp.asarray(pick))
-    sent = pl.pallas_call(
-        pack_kernel,
-        out_shape=jax.ShapeDtypeStruct((OWNERS * IN_ROWS, LANES), BF16),
-        in_specs=[hbm] * 6,
-        scratch_shapes=[
-            pltpu.VMEM((4,) + query.shape[1:], BF16),
-            pltpu.VMEM(filter_taps.shape, F32),
-            pltpu.VMEM(pick.shape, BF16),
-            pltpu.SemaphoreType.DMA((6,)),
-        ],
+    near = (query, key_input, value_input, grad_output)
+    other = [lax.ppermute(x, "core", SWAP) for x in near]
+    rows = jax.ShapeDtypeStruct((OWNERS * CHUNK, LANES), BF16)
+    gated, pick = pl.pallas_call(
+        gate_kernel,
+        out_shape=(
+            jax.ShapeDtypeStruct((2,) + query.shape[1:], BF16),
+            jax.ShapeDtypeStruct((CHUNK * HALF, PARTS * LANES), BF16),
+        ),
+        in_specs=[hbm] * 4,
+        scratch_shapes=[pltpu.VMEM((4,) + query.shape[1:], BF16), pltpu.SemaphoreType.DMA((4,))],
         compiler_params=limit,
-        name="pack",
-    )(*[pltpu.with_memory_space_constraint(x, pltpu.HBM) for x in inputs])
-    got = exchange(sent, ("core", "ctx", "zh"))
+        cost_estimate=pl.CostEstimate(flops=10**9, bytes_accessed=2 * 10**6, transcendentals=0),
+        name="gate",
+    )(*[pltpu.with_memory_space_constraint(x, pltpu.HBM) for x in near])
+    sent = pl.pallas_call(pack_kernel, out_shape=rows, compiler_params=limit, name="pack")(gated, *other, filter_taps, pick)
+    got = exchange(sent)
     signals = (KINDS - 1) * OWNED * SEQS + OWNED
     results = pl.pallas_call(
         conv_kernel,
-        out_shape=jax.ShapeDtypeStruct((TARGETS * OUT_ROWS, LANES), BF16),
+        out_shape=rows,
         scratch_shapes=[
-            pltpu.VMEM((BLOCKS, KINDS * OWNED * SEQS * LANES), BF16),
+            pltpu.VMEM((BLOCKS, HALVES * CHUNK * LANES), BF16),
             pltpu.VMEM((signals * HALF, 2 * LANES), F32),
             pltpu.VMEM((signals * HALF, 2 * LANES), F32),
-            pltpu.VMEM((2, OUT_TILE, 2 * LANES), BF16),
+            pltpu.VMEM((2, TILE, 2 * LANES), BF16),
         ],
         compiler_params=limit,
         name="conv",
     )(got, order, back, first_signal, first_filter, twist, second, second_back, last)
-    returned = exchange(results, ("ctx", "zh"))
+    returned = exchange(results)
     swapped = lax.ppermute(returned, "core", SWAP)
     like = jax.ShapeDtypeStruct(query.shape, BF16)
     unpack = functools.partial(
@@ -323,7 +321,6 @@
         compiler_params=limit,
         cost_estimate=pl.CostEstimate(flops=10**9, bytes_accessed=2 * 10**6, transcendentals=0),
     )
-    near = (query, key_input, value_input, grad_output)
     half = unpack(functools.partial(unpack_kernel, True), name="unpack_own")(*near, returned, sort)
     block = pl.BlockSpec(memory_space=pltpu.VMEM)
     return unpack(

time: 64.9 us -> 64.4 us (level)
  blocking collectives: 53.9 us -> 48 us
  starting transfers between devices: 2.61 us -> 7.74 us
    all_to_all x2, blocking collectives: 53.9 us -> 48 us  [exchange(): lax.all_to_all(parts, ('ctx', 'zh'), split_axis=0, concat_axis=0, tiled=T...]
    ppermute x0 -> x4, starting transfers between devices: none -> 3.94 us  [local(): other = [lax.ppermute(x, 'core', SWAP) for x in near]]
    ppermute x1, starting transfers between devices: 2.61 us -> 3.8 us  [local(): swapped = lax.ppermute(returned, 'core', SWAP)]
    pallas_call x2 -> x3, Pallas kernels: 4.94 us -> 4.8 us  [the longest x1 3.03 us: local(): pl.pallas_call(conv_kernel, out_shape=rows, scratch_shapes=[pltpu.VMEM((B...]
  transfers between devices with their start and end apart: 1 -> 5, of which waited for: 0 -> 1; matrix products, arithmetic and copies ran while one was open for 0% -> 0% of each run, Pallas kernels for 2% -> 4%
where the time goes in v5:
time: 64.4 us; the launch traced here: 64.2 us
  blocking collectives  48 us (75%)
  starting transfers between devices  7.74 us (12%)
  Pallas kernels  7.15 us (11%)
  between operations  0.84 us (1%)
    all_to_all x2, blocking collectives, exchange(): lax.all_to_all(parts, ('ctx', 'zh'), split_axis=0, concat_axis=0, tiled=T...  48 us
    ppermute x4, starting transfers between devices, local(): other = [lax.ppermute(x, 'core', SWAP) for x in near]  3.94 us
    ppermute x1, starting transfers between devices, local(): swapped = lax.ppermute(returned, 'core', SWAP)  3.8 us
    pallas_call x1, Pallas kernels, local(): pl.pallas_call(conv_kernel, out_shape=rows, scratch_shapes=[pltpu.VMEM((B...  3.03 us
  transfers between devices with their start and end apart: 5, of which 1 were waited for; matrix products, arithmetic and copies ran while one was open for 0% of the time, Pallas kernels for 4%

profile of v5, /device:TPU:1, one launch (start us, length us, event | category | flops | bytes accessed | tf_op | source)
XLA Modules:
  0.0 64.2 jit_solution(17679458982466346262)
XLA Ops:
  0.6 0.0 copy-start.2
  0.6 3.3 %collective-permute-start = (bf16[1,128,512]{2,1,0:T(8,128)(2,1)}, bf16[1,128,512]{2,1,0:T(8,128)(2,1)S(1)}, u32[]{:S(2)}, u32[]{:S(2)}) collective-permute-start(bf16[1,128,512]{2,1,0:T(8,128)(2,1)} %q_ref.3), channel_id=1, source_target_pairs={{0,1},{1,0},{2,3},{3,2},{4,5},{5,4},{6,7},{7,6},{8,9},{9,8},{10,11... | collective-permute-start | bytes 393224 | tf_op jit(solution)/shard_map/ppermute | solution.py:280
  4.0 0.1 collective-permute-start.1
  4.1 0.4 collective-permute-start.2
  4.5 0.1 collective-permute-start.3
  4.6 1.2 %gate.1 = (bf16[2,128,512]{2,1,0:T(8,128)(2,1)S(1)}, bf16[640,640]{1,0:T(8,128)(2,1)S(1)}) custom-call(bf16[1,128,512]{2,1,0:T(8,128)(2,1)} %q_ref.3, bf16[1,128,512]{2,1,0:T(8,128)(2,1)} %k_ref.3, bf16[1,128,512]{2,1,0:T(8,128)(2,1)} %v_ref.3, bf16[1,128,512]{2,1,0:T(8,128)(2,1)} %g_ref.3), custom_call_target="tpu_custom_call" | custom-call | flops 1000000000 | bytes 2000000 | tf_op jit(solution)/shard_map/gate/pallas_call | solution.py:282
  5.8 0.0 collective-permute-done.q_ref
  5.8 0.0 collective-permute-done.1.k_ref
  5.8 0.0 collective-permute-done.2.v_ref
  5.8 0.3 collective-permute-done.3.g_ref
  6.0 0.0 copy-done.2
  6.1 0.0 copy-start.6
  6.1 0.0 copy-start.7
  6.1 0.0 copy-start.8
  6.1 0.6 pack.1
  6.7 0.0 copy-start
  6.7 0.0 copy-start.3
  6.7 28.5 %all_to_all.10 = bf16[640,2,128]{2,1,0:T(2,128)(2,1)S(1)} all-to-all(bf16[640,2,128]{2,1,0:T(2,128)(2,1)S(1)} %bitcast.6), channel_id=1, replica_groups=mesh['ctx'=64,'zh'=2,'core'=2] {'ctx','zh'}, dimensions={0} | all-to-all | bytes 655360 | tf_op jit(solution)/shard_map/all_to_all | solution.py:271
  35.3 0.0 copy-done.1
  35.3 0.0 copy-done.4
  35.3 0.0 copy-start.13
  35.4 3.0 %conv.1 = bf16[1280,128]{1,0:T(8,128)(2,1)S(1)} custom-call(bf16[1280,128]{1,0:T(8,128)(2,1)S(1)} %bitcast.4, bf16[320,320]{1,0:T(8,128)(2,1)S(1)} %copy-done.4, bf16[320,320]{1,0:T(8,128)(2,1)S(1)} %copy-done.3, bf16[128,128]{1,0:T(8,128)(2,1)S(1)} %copy-done.8, bf16[128,192]{1,0:T(8,128)(2,1)S(1)} %copy-done.6, f32[128,128]{1,0:T(8,128)S(1)} %copy-done.5, ...), custom_call_target="tpu_custom_call" | custom-call | tf_op jit(solution)/shard_map/conv/pallas_call | solution.py:297
  38.4 0.0 copy-start.9
  38.4 0.0 copy-start.10
  38.4 0.0 copy-start.11
  38.4 0.0 copy-start.12
  38.4 19.5 %all_to_all.11 = bf16[640,2,128]{2,1,0:T(2,128)(2,1)S(1)} all-to-all(bf16[640,2,128]{2,1,0:T(2,128)(2,1)S(1)} %bitcast.5), channel_id=1, replica_groups=mesh['ctx'=64,'zh'=2,'core'=2] {'ctx','zh'}, dimensions={0} | all-to-all | bytes 655360 | tf_op jit(solution)/shard_map/all_to_all | solution.py:271
  57.9 3.8 %collective-permute-start.4 = (bf16[1280,128]{1,0:T(8,128)(2,1)S(1)}, bf16[1280,128]{1,0:T(8,128)(2,1)S(1)}, u32[]{:S(2)}, u32[]{:S(2)}) collective-permute-start(bf16[1280,128]{1,0:T(8,128)(2,1)S(1)} %bitcast.7), channel_id=1, source_target_pairs={{0,1},{1,0},{2,3},{3,2},{4,5},{5,4},{6,7},{7,6},{8,9},{9,8},{10,11... | collective-permute-start | bytes 983048 | tf_op jit(solution)/shard_map/ppermute | solution.py:310
  61.7 0.0 copy-done.11
  61.8 1.2 %unpack_own.1 = (bf16[1,128,512]{2,1,0:T(8,128)(2,1)}, bf16[1,128,512]{2,1,0:T(8,128)(2,1)}, bf16[1,128,512]{2,1,0:T(8,128)(2,1)}, bf16[1,128,512]{2,1,0:T(8,128)(2,1)}, f32[128,512]{1,0:T(8,128)}) custom-call(bf16[1,128,512]{2,1,0:T(8,128)(2,1)S(1)} %copy-done.9, bf16[1,128,512]{2,1,0:T(8,128)(2,1)S(1)} %copy-done.10, bf16[1,128,512]{2,1,0:T(8,128)(2,1)S(1)} %copy-done.11, ...), custom_call_target="tpu_custom_call" | custom-call | flops 1000000000 | bytes 2000000 | tf_op jit(solution)/shard_map/unpack_own/pallas_call | solution.py:324
  62.9 0.0 collective-permute-done.4.got_ref
  63.0 1.2 %unpack_other.1 = (bf16[1,128,512]{2,1,0:T(8,128)(2,1)}, bf16[1,128,512]{2,1,0:T(8,128)(2,1)}, bf16[1,128,512]{2,1,0:T(8,128)(2,1)}, bf16[1,128,512]{2,1,0:T(8,128)(2,1)}, f32[128,512]{1,0:T(8,128)}) custom-call(bf16[1,128,512]{2,1,0:T(8,128)(2,1)S(1)} %copy-done.9, ...), custom_call_target="tpu_custom_call", output_to_operand_aliasing={{0}: (6, {}), {1}: (7, {}), {2}: (8, {}), {3}: (9, {}), {4}... | custom-call | flops 1000000000 | bytes 2000000 | tf_op jit(solution)/shard_map/unpack_other/pallas_call | solution.py:326
  (13 shorter events, 0.0 us)
Async XLA Ops:
  0.6 5.4 %copy-start.2 = (f32[128,512]{1,0:T(8,128)S(1)}, f32[128,512]{1,0:T(8,128)}, u32[]{:S(2)}) copy-start(f32[128,512]{1,0:T(8,128)} %f_ref.1) | copy-start | bytes 786436
  0.6 5.1 %collective-permute-start = (bf16[1,128,512]{2,1,0:T(8,128)(2,1)}, bf16[1,128,512]{2,1,0:T(8,128)(2,1)S(1)}, u32[]{:S(2)}, u32[]{:S(2)}) collective-permute-start(bf16[1,128,512]{2,1,0:T(8,128)(2,1)} %q_ref.3), channel_id=1, source_target_pairs={{0,1},{1,0},{2,3},{3,2},{4,5},{5,4},{6,7},{7,6},{8,9},{9,8},{10,11... | collective-permute-start | bytes 393224 | tf_op jit(solution)/shard_map/ppermute | solution.py:280
  4.0 1.8 %collective-permute-start.1 = (bf16[1,128,512]{2,1,0:T(8,128)(2,1)}, bf16[1,128,512]{2,1,0:T(8,128)(2,1)S(1)}, u32[]{:S(2)}, u32[]{:S(2)}) collective-permute-start(bf16[1,128,512]{2,1,0:T(8,128)(2,1)} %k_ref.3), channel_id=1, source_target_pairs={{0,1},{1,0},{2,3},{3,2},{4,5},{5,4},{6,7},{7,6},{8,9},{9,8},{10,11... | collective-permute-start | bytes 393224 | tf_op jit(solution)/shard_map/ppermute | solution.py:280
  4.1 1.7 %collective-permute-start.2 = (bf16[1,128,512]{2,1,0:T(8,128)(2,1)}, bf16[1,128,512]{2,1,0:T(8,128)(2,1)S(1)}, u32[]{:S(2)}, u32[]{:S(2)}) collective-permute-start(bf16[1,128,512]{2,1,0:T(8,128)(2,1)} %v_ref.3), channel_id=1, source_target_pairs={{0,1},{1,0},{2,3},{3,2},{4,5},{5,4},{6,7},{7,6},{8,9},{9,8},{10,11... | collective-permute-start | bytes 393224 | tf_op jit(solution)/shard_map/ppermute | solution.py:280
  4.5 1.6 %collective-permute-start.3 = (bf16[1,128,512]{2,1,0:T(8,128)(2,1)}, bf16[1,128,512]{2,1,0:T(8,128)(2,1)S(1)}, u32[]{:S(2)}, u32[]{:S(2)}) collective-permute-start(bf16[1,128,512]{2,1,0:T(8,128)(2,1)} %g_ref.3), channel_id=1, source_target_pairs={{0,1},{1,0},{2,3},{3,2},{4,5},{5,4},{6,7},{7,6},{8,9},{9,8},{10,11... | collective-permute-start | bytes 393224 | tf_op jit(solution)/shard_map/ppermute | solution.py:280
  6.0 29.2 %copy-start.1 = (bf16[768,256]{1,0:T(8,128)(2,1)S(1)}, bf16[768,256]{1,0:T(8,128)(2,1)}, u32[]{:S(2)}) copy-start(bf16[768,256]{1,0:T(8,128)(2,1)} %constant.23.clone.sec_ref) | copy-start | bytes 1179652
  6.0 29.2 %copy-start.4 = (bf16[320,320]{1,0:T(8,128)(2,1)S(1)}, bf16[320,320]{1,0:T(8,128)(2,1)}, u32[]{:S(2)}) copy-start(bf16[320,320]{1,0:T(8,128)(2,1)} %constant.18.clone.order_ref) | copy-start | bytes 614404
  6.0 29.2 %copy-start.5 = (f32[128,128]{1,0:T(8,128)S(1)}, f32[128,128]{1,0:T(8,128)}, u32[]{:S(2)}) copy-start(f32[128,128]{1,0:T(8,128)} %constant.22.clone.tw_ref) | copy-start | bytes 196612
  6.1 29.2 %copy-start.6 = (bf16[128,192]{1,0:T(8,128)(2,1)S(1)}, bf16[128,192]{1,0:T(8,128)(2,1)}, u32[]{:S(2)}) copy-start(bf16[128,192]{1,0:T(8,128)(2,1)} %constant.21.clone.ff_ref) | copy-start | bytes 147460
  6.1 29.2 %copy-start.7 = (bf16[64,384]{1,0:T(8,128)(2,1)S(1)}, bf16[64,384]{1,0:T(8,128)(2,1)}, u32[]{:S(2)}) copy-start(bf16[64,384]{1,0:T(8,128)(2,1)} %constant.25.clone.last_ref) | copy-start | bytes 147460
  6.1 29.2 %copy-start.8 = (bf16[128,128]{1,0:T(8,128)(2,1)S(1)}, bf16[128,128]{1,0:T(8,128)(2,1)}, u32[]{:S(2)}) copy-start(bf16[128,128]{1,0:T(8,128)(2,1)} %constant.20.clone.fs_ref) | copy-start | bytes 98308
  6.7 28.6 %copy-start = (bf16[768,256]{1,0:T(8,128)(2,1)S(1)}, bf16[768,256]{1,0:T(8,128)(2,1)}, u32[]{:S(2)}) copy-start(bf16[768,256]{1,0:T(8,128)(2,1)} %constant.24.clone.secb_ref) | copy-start | bytes 1179652
  6.7 28.6 %copy-start.3 = (bf16[320,320]{1,0:T(8,128)(2,1)S(1)}, bf16[320,320]{1,0:T(8,128)(2,1)}, u32[]{:S(2)}) copy-start(bf16[320,320]{1,0:T(8,128)(2,1)} %constant.19.clone.back_ref) | copy-start | bytes 614404
  35.3 26.4 %copy-start.13 = (bf16[2,640,384]{2,1,0:T(8,128)(2,1)S(1)}, bf16[2,640,384]{2,1,0:T(8,128)(2,1)}, u32[]{:S(2)}) copy-start(bf16[2,640,384]{2,1,0:T(8,128)(2,1)} %constant.26.clone.sort_ref) | copy-start | bytes 2949124
  38.4 23.4 %copy-start.9 = (bf16[1,128,512]{2,1,0:T(8,128)(2,1)S(1)}, bf16[1,128,512]{2,1,0:T(8,128)(2,1)}, u32[]{:S(2)}) copy-start(bf16[1,128,512]{2,1,0:T(8,128)(2,1)} %q_ref.3) | copy-start | bytes 393220
  38.4 23.3 %copy-start.10 = (bf16[1,128,512]{2,1,0:T(8,128)(2,1)S(1)}, bf16[1,128,512]{2,1,0:T(8,128)(2,1)}, u32[]{:S(2)}) copy-start(bf16[1,128,512]{2,1,0:T(8,128)(2,1)} %k_ref.3) | copy-start | bytes 393220
  38.4 23.3 %copy-start.11 = (bf16[1,128,512]{2,1,0:T(8,128)(2,1)S(1)}, bf16[1,128,512]{2,1,0:T(8,128)(2,1)}, u32[]{:S(2)}) copy-start(bf16[1,128,512]{2,1,0:T(8,128)(2,1)} %v_ref.3) | copy-start | bytes 393220
  38.4 23.3 %copy-start.12 = (bf16[1,128,512]{2,1,0:T(8,128)(2,1)S(1)}, bf16[1,128,512]{2,1,0:T(8,128)(2,1)}, u32[]{:S(2)}) copy-start(bf16[1,128,512]{2,1,0:T(8,128)(2,1)} %g_ref.3) | copy-start | bytes 393220
  57.9 5.1 %collective-permute-start.4 = (bf16[1280,128]{1,0:T(8,128)(2,1)S(1)}, bf16[1280,128]{1,0:T(8,128)(2,1)S(1)}, u32[]{:S(2)}, u32[]{:S(2)}) collective-permute-start(bf16[1280,128]{1,0:T(8,128)(2,1)S(1)} %bitcast.7), channel_id=1, source_target_pairs={{0,1},{1,0},{2,3},{3,2},{4,5},{5,4},{6,7},{7,6},{8,9},{9,8},{10,11... | collective-permute-start | bytes 983048 | tf_op jit(solution)/shard_map/ppermute | solution.py:310

commit v6 on v5

v6 whole, which is shorter than its diff:
```python
import functools

import jax
import jax.numpy as jnp
import ml_dtypes
import numpy as np
from jax import lax
from jax.experimental import pallas as pl
from jax.experimental.pallas import tpu as pltpu
from jax.sharding import PartitionSpec as P

BF16 = jnp.bfloat16
F32 = jnp.float32

BLOCKS = 64
LANES = 128
ROWS = 128
HALF = 64
SEQS = 4
C = 512
CORES = 2
HALVES = 2
KINDS = 3
OWNERS = 128
OWNED = C // CORES // OWNERS
GROUP = 16
PARTS = 5
CHUNK = PARTS * OWNED
TILE = GROUP * HALVES * CHUNK
SETS = 2 * OWNED * HALVES
SWAP = ((0, 1), (1, 0))


def two_terms(table):
    high = table.astype(ml_dtypes.bfloat16)
    low = (table - high.astype(np.float64)).astype(ml_dtypes.bfloat16)
    return high, low


def tables():
    k1 = np.arange(HALF)[:, None] + 0.5
    angle1 = 2.0 * np.pi * k1 * np.arange(BLOCKS)[None, :] / ROWS
    first = np.concatenate([np.cos(angle1), -np.sin(angle1)], axis=0)
    first_high, first_low = two_terms(first)
    first_signal = np.concatenate([first_high, first_low], axis=1)
    first_filter = np.concatenate([first_high, first_low, first_high], axis=1)
    angle_t = 2.0 * np.pi * k1 * np.arange(LANES)[None, :] / (ROWS * LANES)
    twist = np.concatenate([np.cos(angle_t), -np.sin(angle_t)], axis=0).astype(np.float32)
    index = np.arange(LANES)
    angle2 = 2.0 * np.pi * ((index[:, None] * index[None, :]) % LANES) / LANES
    cos2, sin2 = np.cos(angle2), np.sin(angle2)
    second = np.block([[cos2, -sin2], [sin2, cos2]])
    second_back = np.block([[cos2, sin2], [-sin2, cos2]])
    last = np.concatenate([np.cos(angle1.T), -np.sin(angle1.T)], axis=1) * (2.0 / (ROWS * LANES))
    last_high, last_low = two_terms(last)
    last_stack = np.concatenate([last_high, last_high, last_low], axis=1)
    line = np.arange(TILE)
    block = line // (HALVES * CHUNK)
    half = line % (HALVES * CHUNK) // CHUNK
    part = line % CHUNK // OWNED
    own = line % OWNED
    slot = ((part % 2 * OWNED + own) * HALVES + half) * GROUP + block
    last_slot = (own * HALVES + half) * GROUP + block
    order_own = np.zeros((SETS * GROUP + OWNED * HALVES * GROUP, TILE))
    order_other = np.zeros((SETS * GROUP, TILE))
    order_own[slot[part < 2], line[part < 2]] = 1.0
    order_own[SETS * GROUP + last_slot[part == 4], line[part == 4]] = 1.0
    chosen = (part == 2) | (part == 3)
    order_other[slot[chosen], line[chosen]] = 1.0
    back = np.zeros((TILE, TILE))
    back[line, np.where(part == 4, 2 * SETS * GROUP + last_slot, part // 2 * SETS * GROUP + slot)] = 1.0
    row = np.arange(CHUNK * HALF)
    own = OWNED * (row // CHUNK) + row % OWNED
    part = row % CHUNK // OWNED
    sort = np.zeros((CORES, CHUNK * HALF, KINDS * LANES))
    for whose in range(CORES):
        for kind, wanted in enumerate((2 * whose, 2 * whose + 1, 4)):
            sort[whose, row[part == wanted], kind * LANES + own[part == wanted]] = 1.0
    high, low = two_terms(second)
    back_high, back_low = two_terms(second_back)
    return (
        sort.astype(ml_dtypes.bfloat16),
        order_own.astype(ml_dtypes.bfloat16),
        order_other.astype(ml_dtypes.bfloat16),
        back.astype(ml_dtypes.bfloat16),
        first_signal,
        first_filter,
        twist,
        np.concatenate([high, high, low], axis=0),
        np.concatenate([back_high, back_high, back_low], axis=0),
        last_stack,
    )


def mm(a, b, dims=((1,), (0,))):
    return lax.dot_general(a, b, (dims, ((), ())), preferred_element_type=F32)


def columns(core, b):
    return pl.ds(pl.multiple_of(core * (C // CORES) + b * LANES, LANES), LANES)


def pack_kernel(q_hbm, k_hbm, v_hbm, f_hbm, g_hbm, out_ref, in_ref, f_ref, pick_ref, sems):
    copies = [pltpu.make_async_copy(src.at[0], in_ref.at[i], sems.at[i]) for i, src in enumerate((k_hbm, v_hbm, g_hbm, q_hbm))]
    copies.append(pltpu.make_async_copy(f_hbm, f_ref, sems.at[4]))
    for copy in copies:
        copy.start()
    core = lax.axis_index("core")
    term = lax.axis_index("zh")
    row = lax.broadcasted_iota(jnp.int32, (CHUNK * HALF, LANES), 0)
    lane = lax.broadcasted_iota(jnp.int32, (CHUNK * HALF, LANES), 1)
    first = (lane >> 1) * CHUNK + (lane & 1)
    for part in range(PARTS):
        chosen = jnp.where(row == first + OWNED * part, 1.0, 0.0)
        pick_ref[:, part * LANES : (part + 1) * LANES] = chosen.astype(BF16)
    for copy in copies:
        copy.wait()
    for b in range(C // CORES // LANES):
        data = []
        for owners in (core, 1 - core):
            cols = columns(owners, b)
            for i in (0, 2):
                data.append((in_ref[i, :, cols].astype(F32) * in_ref[i + 1, :, cols].astype(F32)).astype(BF16))
        taps = f_ref[:, columns(core, b)]
        high = taps.astype(BF16).astype(F32)
        data.append(jnp.where(term == 0, high, taps - high).astype(BF16))
        rows = mm(pick_ref[...], jnp.concatenate(data, axis=1), ((1,), (1,)))
        out_ref[b * CHUNK * HALF : (b + 1) * CHUNK * HALF, :] = rows.astype(BF16)


def unpack_kernel(own, q_ref, k_ref, v_ref, g_ref, got_ref, sort_ref, *refs):
    o_hbm, gq_hbm, gk_hbm, gv_hbm, gf_hbm, rows_ref, taps_ref, sems = refs[-8:]
    core = lax.axis_index("core")
    owners = core if own else 1 - core
    copies = []
    for b in range(C // CORES // LANES):
        cols = columns(owners, b)
        got = got_ref[b * CHUNK * HALF : (b + 1) * CHUNK * HALF, :]
        data = mm(got, sort_ref[0 if own else 1], ((0,), (0,)))
        mixed, back = data[:, :LANES], data[:, LANES : 2 * LANES]
        taps_ref[b] = data[:, 2 * LANES :]
        rows_ref[0, b] = (q_ref[0, :, cols].astype(F32) * mixed).astype(BF16)
        rows_ref[1, b] = (g_ref[0, :, cols].astype(F32) * mixed).astype(BF16)
        rows_ref[2, b] = (back * v_ref[0, :, cols].astype(F32)).astype(BF16)
        rows_ref[3, b] = (back * k_ref[0, :, cols].astype(F32)).astype(BF16)
        for j, out in enumerate((o_hbm, gq_hbm, gk_hbm, gv_hbm)):
            copies.append(pltpu.make_async_copy(rows_ref.at[j, b], out.at[0, :, cols], sems.at[j, b]))
        copies.append(pltpu.make_async_copy(taps_ref.at[b], gf_hbm.at[:, cols], sems.at[4, b]))
        for copy in copies[-5:]:
            copy.start()
    for copy in copies:
        copy.wait()


def split(x):
    high = x.astype(BF16)
    low = (x - high.astype(F32)).astype(BF16)
    return high, low


def three(x):
    high, low = split(x)
    return jnp.concatenate([high, low, high], axis=1)


def sort_signals(got_ref, order_ref, sig_ref):
    order = order_ref[...]
    for h in range(2):
        lo = 2 * h * TILE
        data = jnp.concatenate([got_ref[lo : lo + TILE, :], got_ref[lo + TILE : lo + 2 * TILE, :]], axis=1)
        sorted_rows = mm(order, data).astype(BF16)
        for s in range(order.shape[0] // GROUP):
            for u in range(2):
                at = (2 * h + u) * GROUP
                sig_ref[at : at + GROUP, s * LANES : (s + 1) * LANES] = sorted_rows[
                    s * GROUP : (s + 1) * GROUP, u * LANES : (u + 1) * LANES
                ]


def turned(first, tw_ref):
    wr, wi = tw_ref[:HALF, :], tw_ref[HALF:, :]
    halves = []
    for u in range(2):
        ar = first[:HALF, u * LANES : (u + 1) * LANES]
        ai = first[HALF:, u * LANES : (u + 1) * LANES]
        halves.append(jnp.concatenate([ar * wr - ai * wi, ar * wi + ai * wr], axis=1))
    return three(jnp.concatenate(halves, axis=0))


def forward_lines(sig_ref, fs_ref, tw_ref):
    lines = []
    for p in range(SETS // 2):
        data = sig_ref[:, 2 * p * LANES : 2 * (p + 1) * LANES]
        lines.append(turned(mm(fs_ref[...], jnp.concatenate([data, data], axis=0)), tw_ref))
    return lines


def multiplied(spec_ref, filter_ref, at, sums):
    lines = []
    for own in range(OWNED):
        hr = filter_ref[at + own * HALF : at + (own + 1) * HALF, :LANES]
        hi = filter_ref[at + own * HALF : at + (own + 1) * HALF, LANES:]
        mixed_pair, back_pair = [], []
        qr, qi = sums[own]
        for half in range(HALVES):
            s = own * HALVES + half
            z = OWNED * HALVES + s
            pr = spec_ref[s * HALF : (s + 1) * HALF, :LANES]
            pi = spec_ref[s * HALF : (s + 1) * HALF, LANES:]
            gr = spec_ref[z * HALF : (z + 1) * HALF, :LANES]
            gi = spec_ref[z * HALF : (z + 1) * HALF, LANES:]
            mixed_pair.append(jnp.concatenate([hr * pr - hi * pi, hr * pi + hi * pr], axis=1))
            back_pair.append(jnp.concatenate([gr * hr + gi * hi, gi * hr - gr * hi], axis=1))
            qr = qr + (gr * pr + gi * pi)
            qi = qi + (gi * pr - gr * pi)
        sums[own] = (qr, qi)
        lines.append((own, three(jnp.concatenate(mixed_pair, axis=0))))
        lines.append((OWNED + own, three(jnp.concatenate(back_pair, axis=0))))
    return [line for _, line in sorted(lines, key=lambda entry: entry[0])]


def inverse(full, tw_ref, last_ref):
    wr, wi = tw_ref[:HALF, :], tw_ref[HALF:, :]
    cols = []
    for u in range(2):
        br = full[u * HALF : (u + 1) * HALF, :LANES]
        bi = full[u * HALF : (u + 1) * HALF, LANES:]
        cols.append(jnp.concatenate([br * wr + bi * wi, bi * wr - br * wi], axis=0))
    high, low = split(jnp.concatenate(cols, axis=1))
    return mm(last_ref[...], jnp.concatenate([high, low, high], axis=0))


def keep(fin_ref, s, values):
    values = values.astype(BF16)
    for b in range(BLOCKS // GROUP):
        fin_ref[b // 2, s * GROUP : (s + 1) * GROUP, (b % 2) * LANES : (b % 2 + 1) * LANES] = values[
            b * GROUP : (b + 1) * GROUP, :
        ]


def conv_own_kernel(
    got_ref, order_ref, fs_ref, ff_ref, tw_ref, sec_ref, secb_ref, last_ref, filter_ref, sum_ref, fin_ref, sig_ref, spec_ref, inv_ref
):
    sort_signals(got_ref, order_ref, sig_ref)
    lines = forward_lines(sig_ref, fs_ref, tw_ref)
    terms = []
    for term in range(HALVES):
        places = [SETS * LANES + (own * HALVES + term) * LANES for own in range(OWNED)]
        terms.append(jnp.concatenate([sig_ref[:, at : at + LANES] for at in places], axis=1))
    lines.append(turned(mm(ff_ref[...], jnp.concatenate([terms[0], terms[0], terms[1]], axis=0)), tw_ref))
    spec_ref[...] = mm(jnp.concatenate(lines, axis=0), sec_ref[...])
    filter_ref[...] = spec_ref[SETS * HALF :, :]
    zero = jnp.zeros((HALF, LANES), F32)
    sums = [(zero, zero) for _ in range(OWNED)]
    lines = multiplied(spec_ref, spec_ref, SETS * HALF, sums)
    for own in range(OWNED):
        sum_ref[own * HALF : (own + 1) * HALF, :] = jnp.concatenate(sums[own], axis=1)
    inv_ref[...] = mm(jnp.concatenate(lines, axis=0), secb_ref[...])
    for p in range(SETS // 2):
        res = inverse(inv_ref[2 * p * HALF : 2 * (p + 1) * HALF, :], tw_ref, last_ref)
        for u in range(2):
            keep(fin_ref, 2 * p + u, res[:, u * LANES : (u + 1) * LANES])


def conv_other_kernel(
    got_ref,
    filter_ref,
    sum_ref,
    done_ref,
    order_ref,
    back_ref,
    fs_ref,
    tw_ref,
    sec_ref,
    secb_ref,
    last_ref,
    out_ref,
    sig_ref,
    spec_ref,
    inv_ref,
    fin_ref,
):
    sort_signals(got_ref, order_ref, sig_ref)
    spec_ref[...] = mm(jnp.concatenate(forward_lines(sig_ref, fs_ref, tw_ref), axis=0), sec_ref[...])
    sums = []
    for own in range(OWNED):
        found = sum_ref[own * HALF : (own + 1) * HALF, :]
        sums.append((found[:, :LANES], found[:, LANES:]))
    lines = multiplied(spec_ref, filter_ref, 0, sums)
    lines.append(three(jnp.concatenate([jnp.concatenate(pair, axis=1) for pair in sums], axis=0)))
    inv_ref[...] = mm(jnp.concatenate(lines, axis=0), secb_ref[...])
    for p in range(SETS // 2 + 1):
        res = inverse(inv_ref[2 * p * HALF : 2 * (p + 1) * HALF, :], tw_ref, last_ref)
        for u in range(2):
            slots = [2 * p + u] if p < SETS // 2 else [SETS + u * HALVES + half for half in range(HALVES)]
            for s in slots:
                keep(fin_ref, s, res[:, u * LANES : (u + 1) * LANES])
    back = back_ref[...]
    for h in range(2):
        rows = mm(back, jnp.concatenate([done_ref[h], fin_ref[h]], axis=0)).astype(BF16)
        lo = 2 * h * TILE
        out_ref[lo : lo + TILE, :] = rows[:, :LANES]
        out_ref[lo + TILE : lo + 2 * TILE, :] = rows[:, LANES:]


def exchange(rows):
    parts = rows.reshape(rows.shape[0] // OWNED, OWNED, LANES)
    parts = lax.all_to_all(parts, ("ctx", "zh"), split_axis=0, concat_axis=0, tiled=True)
    return parts.reshape(rows.shape)


def local(query, key_input, value_input, filter_taps, grad_output):
    sort, order_own, order_other, back, first_signal, first_filter, twist, second, second_back, last = tables()
    limit = pltpu.CompilerParams(vmem_limit_bytes=32 * 1024 * 1024)
    hbm = pl.BlockSpec(memory_space=pltpu.HBM)
    near = (query, key_input, value_input, grad_output)
    inputs = (query, key_input, value_input, filter_taps, grad_output)
    rows = jax.ShapeDtypeStruct((OWNERS * CHUNK, LANES), BF16)
    sent = pl.pallas_call(
        pack_kernel,
        out_shape=rows,
        in_specs=[hbm] * 5,
        scratch_shapes=[
            pltpu.VMEM((4,) + query.shape[1:], BF16),
            pltpu.VMEM(filter_taps.shape, F32),
            pltpu.VMEM((CHUNK * HALF, PARTS * LANES), BF16),
            pltpu.SemaphoreType.DMA((5,)),
        ],
        compiler_params=limit,
        name="pack",
    )(*[pltpu.with_memory_space_constraint(x, pltpu.HBM) for x in inputs])
    got = exchange(sent)
    other = lax.ppermute(got, "core", SWAP)
    extra = OWNED * HALVES
    pair = jax.ShapeDtypeStruct((OWNED * HALF, 2 * LANES), F32)
    filter_spec, sums, done = pl.pallas_call(
        conv_own_kernel,
        out_shape=(pair, pair, jax.ShapeDtypeStruct((2, SETS * GROUP, 2 * LANES), BF16)),
        scratch_shapes=[
            pltpu.VMEM((BLOCKS, (SETS + extra) * LANES), BF16),
            pltpu.VMEM(((SETS + OWNED) * HALF, 2 * LANES), F32),
            pltpu.VMEM((SETS * HALF, 2 * LANES), F32),
        ],
        compiler_params=limit,
        cost_estimate=pl.CostEstimate(flops=2 * 10**9, bytes_accessed=4 * 10**6, transcendentals=0),
        name="conv_own",
    )(got, order_own, first_signal, first_filter, twist, second, second_back, last)
    results = pl.pallas_call(
        conv_other_kernel,
        out_shape=rows,
        scratch_shapes=[
            pltpu.VMEM((BLOCKS, SETS * LANES), BF16),
            pltpu.VMEM((SETS * HALF, 2 * LANES), F32),
            pltpu.VMEM(((SETS + OWNED) * HALF, 2 * LANES), F32),
            pltpu.VMEM((2, (SETS + extra) * GROUP, 2 * LANES), BF16),
        ],
        compiler_params=limit,
        name="conv_other",
    )(other, filter_spec, sums, done, order_other, back, first_signal, twist, second, second_back, last)
    returned = exchange(results)
    swapped = lax.ppermute(returned, "core", SWAP)
    like = jax.ShapeDtypeStruct(query.shape, BF16)
    unpack = functools.partial(
        pl.pallas_call,
        out_shape=(like, like, like, like, jax.ShapeDtypeStruct(filter_taps.shape, F32)),
        out_specs=[hbm] * 5,
        scratch_shapes=[
            pltpu.VMEM((4, C // CORES // LANES, LANES, LANES), BF16),
            pltpu.VMEM((C // CORES // LANES, LANES, LANES), F32),
            pltpu.SemaphoreType.DMA((5, C // CORES // LANES)),
        ],
        compiler_params=limit,
        cost_estimate=pl.CostEstimate(flops=10**9, bytes_accessed=2 * 10**6, transcendentals=0),
    )
    half = unpack(functools.partial(unpack_kernel, True), name="unpack_own")(*near, returned, sort)
    block = pl.BlockSpec(memory_space=pltpu.VMEM)
    return unpack(
        functools.partial(unpack_kernel, False),
        in_specs=[block] * 6 + [hbm] * 5,
        input_output_aliases={6 + i: i for i in range(5)},
        name="unpack_other",
    )(*near, swapped, sort, *half)


def solution(mesh):
    split = jax.sharding.Mesh(mesh.devices.reshape(BLOCKS, HALVES, CORES), ("ctx", "zh", "core"))
    shared = P(("zh", "core"), "ctx", None)
    taps = P("ctx", None)
    return jax.shard_map(
        local,
        mesh=split,
        in_specs=(shared, shared, shared, taps, shared),
        out_specs=(shared, shared, shared, shared, taps),
        check_vma=False,
    )
```

time: 64.4 us -> 64.9 us (level)
  blocking collectives: 48 us -> 51.4 us
  starting transfers between devices: 7.74 us -> 4.53 us
  Pallas kernels: 7.15 us -> 7.84 us
    all_to_all x2, blocking collectives: 48 us -> 51.4 us  [exchange(): lax.all_to_all(parts, ('ctx', 'zh'), split_axis=0, concat_axis=0, tiled=T...]
    ppermute x1, starting transfers between devices: 3.8 us -> 1.96 us  [local(): swapped = lax.ppermute(returned, 'core', SWAP)]
    ppermute x4 -> x1, starting transfers between devices: 3.94 us -> 2.57 us  [local(): other = lax.ppermute(got, 'core', SWAP)]
    pallas_call x3, Pallas kernels: 4.8 us -> 5.49 us  [the longest x1 1.91 us: local(): pl.pallas_call(pack_kernel, out_shape=rows, in_specs=[hbm] * 5, scratch_s...]
  transfers between devices with their start and end apart: 5 -> 2, of which waited for: 1 -> 0; matrix products, arithmetic and copies ran while one was open for 0% -> 0% of each run, Pallas kernels for 4% -> 4%
where the time goes in v6:
time: 64.9 us; the launch traced here: 64.7 us
  blocking collectives  51.4 us (79%)
  Pallas kernels  7.84 us (12%)
  starting transfers between devices  4.53 us (7%)
  between operations  0.83 us (1%)
    all_to_all x2, blocking collectives, exchange(): lax.all_to_all(parts, ('ctx', 'zh'), split_axis=0, concat_axis=0, tiled=T...  51.4 us
    ppermute x1, starting transfers between devices, local(): other = lax.ppermute(got, 'core', SWAP)  2.57 us
    ppermute x1, starting transfers between devices, local(): swapped = lax.ppermute(returned, 'core', SWAP)  1.96 us
    pallas_call x1, Pallas kernels, local(): pl.pallas_call(pack_kernel, out_shape=rows, in_specs=[hbm] * 5, scratch_s...  1.91 us
    pallas_call x1, Pallas kernels, local(): pl.pallas_call(conv_other_kernel, out_shape=rows, scratch_shapes=[pltpu.V...  1.87 us
    pallas_call x1, Pallas kernels, local(): pl.pallas_call(conv_own_kernel, out_shape=(pair, pair, jax.ShapeDtypeStru...  1.71 us
  transfers between devices with their start and end apart: 2, of which 0 were waited for; matrix products, arithmetic and copies ran while one was open for 0% of the time, Pallas kernels for 4%

profile of v6, /device:TPU:1, one launch (start us, length us, event | category | flops | bytes accessed | tf_op | source)
XLA Modules:
  0.0 64.7 jit_solution(4104906923263214596)
XLA Ops:
  0.6 0.0 copy-start.1
  0.6 0.0 copy-start.12
  0.7 1.9 %pack.1 = bf16[1280,128]{1,0:T(8,128)(2,1)S(1)} custom-call(bf16[1,128,512]{2,1,0:T(8,128)(2,1)} %q_ref.3, bf16[1,128,512]{2,1,0:T(8,128)(2,1)} %k_ref.3, bf16[1,128,512]{2,1,0:T(8,128)(2,1)} %v_ref.3, f32[128,512]{1,0:T(8,128)} %f_hbm.1, bf16[1,128,512]{2,1,0:T(8,128)(2,1)} %g_ref.3), custom_call_target="tpu_custom_call" | custom-call | tf_op jit(solution)/shard_map/pack/pallas_call | solution.py:319
  2.6 0.0 copy-start
  2.6 0.0 copy-start.8
  2.6 0.0 copy-start.9
  2.6 0.0 copy-start.10
  2.6 0.0 copy-start.13
  2.6 30.7 %all_to_all.10 = bf16[640,2,128]{2,1,0:T(2,128)(2,1)S(1)} all-to-all(bf16[640,2,128]{2,1,0:T(2,128)(2,1)S(1)} %bitcast.5), channel_id=1, replica_groups=mesh['ctx'=64,'zh'=2,'core'=2] {'ctx','zh'}, dimensions={0} | all-to-all | bytes 655360 | tf_op jit(solution)/shard_map/all_to_all | solution.py:308
  33.4 2.6 %collective-permute-start = (bf16[1280,128]{1,0:T(8,128)(2,1)S(1)}, bf16[1280,128]{1,0:T(8,128)(2,1)S(1)}, u32[]{:S(2)}, u32[]{:S(2)}) collective-permute-start(bf16[1280,128]{1,0:T(8,128)(2,1)S(1)} %bitcast.6), channel_id=1, source_target_pairs={{0,1},{1,0},{2,3},{3,2},{4,5},{5,4},{6,7},{7,6},{8,9},{9,8},{10,11... | collective-permute-start | bytes 983048 | tf_op jit(solution)/shard_map/ppermute | solution.py:333
  35.9 0.0 copy-done.1
  35.9 0.0 copy-done.12
  35.9 0.0 copy-done
  35.9 0.0 copy-done.8
  35.9 0.0 copy-done.9
  35.9 0.0 copy-done.10
  36.0 1.7 %conv_own.1 = (f32[128,256]{1,0:T(8,128)S(1)}, f32[128,256]{1,0:T(8,128)S(1)}, bf16[2,128,256]{2,1,0:T(8,128)(2,1)S(1)}) custom-call(bf16[1280,128]{1,0:T(8,128)(2,1)S(1)} %bitcast.7, bf16[192,320]{1,0:T(8,128)(2,1)S(1)} %copy-done.12, bf16[128,128]{1,0:T(8,128)(2,1)S(1)} %copy-done.10, bf16[128,192]{1,0:T(8,128)(2,1)S(1)} %copy-done.13, ...), custom_call_target="tpu_custom_call" | custom-call | flops 2000000000 | bytes 4000000 | tf_op jit(solution)/shard_map/conv_own/pallas_call | solution.py:336
  37.7 0.0 collective-permute-done.got_ref
  37.7 0.0 copy-done.2
  37.7 0.0 copy-done.7
  37.7 0.0 copy-start.11
  37.7 1.9 %conv_other.1 = bf16[1280,128]{1,0:T(8,128)(2,1)S(1)} custom-call(bf16[1280,128]{1,0:T(8,128)(2,1)S(1)} %collective-permute-done.got_ref, f32[128,256]{1,0:T(8,128)S(1)} %get-tuple-element.13.filter_ref, f32[128,256]{1,0:T(8,128)S(1)} %get-tuple-element.14.sum_ref, bf16[2,128,256]{2,1,0:T(8,128)(2,1)S(1)} %get-tuple-element.15.done_ref, ...), custom_call_target="tpu_custom_call" | custom-call | tf_op jit(solution)/shard_map/conv_other/pallas_call | solution.py:348
  39.6 0.0 copy-start.3
  39.6 0.0 copy-start.4
  39.6 0.0 copy-start.5
  39.6 0.0 copy-start.6
  39.7 20.7 %all_to_all.11 = bf16[640,2,128]{2,1,0:T(2,128)(2,1)S(1)} all-to-all(bf16[640,2,128]{2,1,0:T(2,128)(2,1)S(1)} %bitcast.4), channel_id=1, replica_groups=mesh['ctx'=64,'zh'=2,'core'=2] {'ctx','zh'}, dimensions={0} | all-to-all | bytes 655360 | tf_op jit(solution)/shard_map/all_to_all | solution.py:308
  60.4 2.0 %collective-permute-start.1 = (bf16[1280,128]{1,0:T(8,128)(2,1)S(1)}, bf16[1280,128]{1,0:T(8,128)(2,1)S(1)}, u32[]{:S(2)}, u32[]{:S(2)}) collective-permute-start(bf16[1280,128]{1,0:T(8,128)(2,1)S(1)} %bitcast.8), channel_id=1, source_target_pairs={{0,1},{1,0},{2,3},{3,2},{4,5},{5,4},{6,7},{7,6},{8,9},{9,8},{10,11... | collective-permute-start | bytes 983048 | tf_op jit(solution)/shard_map/ppermute | solution.py:361
  62.3 0.0 copy-done.4
  62.3 1.2 %unpack_own.1 = (bf16[1,128,512]{2,1,0:T(8,128)(2,1)}, bf16[1,128,512]{2,1,0:T(8,128)(2,1)}, bf16[1,128,512]{2,1,0:T(8,128)(2,1)}, bf16[1,128,512]{2,1,0:T(8,128)(2,1)}, f32[128,512]{1,0:T(8,128)}) custom-call(bf16[1,128,512]{2,1,0:T(8,128)(2,1)S(1)} %copy-done.3, bf16[1,128,512]{2,1,0:T(8,128)(2,1)S(1)} %copy-done.4, bf16[1,128,512]{2,1,0:T(8,128)(2,1)S(1)} %copy-done.5, ...), custom_call_target="tpu_custom_call" | custom-call | flops 1000000000 | bytes 2000000 | tf_op jit(solution)/shard_map/unpack_own/pallas_call | solution.py:375
  63.5 0.0 collective-permute-done.1.got_ref
  63.6 1.2 %unpack_other.1 = (bf16[1,128,512]{2,1,0:T(8,128)(2,1)}, bf16[1,128,512]{2,1,0:T(8,128)(2,1)}, bf16[1,128,512]{2,1,0:T(8,128)(2,1)}, bf16[1,128,512]{2,1,0:T(8,128)(2,1)}, f32[128,512]{1,0:T(8,128)}) custom-call(bf16[1,128,512]{2,1,0:T(8,128)(2,1)S(1)} %copy-done.3, ...), custom_call_target="tpu_custom_call", output_to_operand_aliasing={{0}: (6, {}), {1}: (7, {}), {2}: (8, {}), {3}: (9, {}), {4}... | custom-call | flops 1000000000 | bytes 2000000 | tf_op jit(solution)/shard_map/unpack_other/pallas_call | solution.py:377
  (7 shorter events, 0.0 us)
Async XLA Ops:
  0.6 35.3 %copy-start.1 = (bf16[768,256]{1,0:T(8,128)(2,1)S(1)}, bf16[768,256]{1,0:T(8,128)(2,1)}, u32[]{:S(2)}) copy-start(bf16[768,256]{1,0:T(8,128)(2,1)} %constant.24.clone.sec_ref) | copy-start | bytes 1179652
  0.6 35.3 %copy-start.12 = (bf16[192,320]{1,0:T(8,128)(2,1)S(1)}, bf16[192,320]{1,0:T(8,128)(2,1)}, u32[]{:S(2)}) copy-start(bf16[192,320]{1,0:T(8,128)(2,1)} %constant.20.clone.order_ref) | copy-start | bytes 368644
  2.6 33.4 %copy-start = (bf16[768,256]{1,0:T(8,128)(2,1)S(1)}, bf16[768,256]{1,0:T(8,128)(2,1)}, u32[]{:S(2)}) copy-start(bf16[768,256]{1,0:T(8,128)(2,1)} %constant.25.clone.secb_ref) | copy-start | bytes 1179652
  2.6 33.3 %copy-start.8 = (f32[128,128]{1,0:T(8,128)S(1)}, f32[128,128]{1,0:T(8,128)}, u32[]{:S(2)}) copy-start(f32[128,128]{1,0:T(8,128)} %constant.23.clone.tw_ref) | copy-start | bytes 196612
  2.6 33.3 %copy-start.9 = (bf16[64,384]{1,0:T(8,128)(2,1)S(1)}, bf16[64,384]{1,0:T(8,128)(2,1)}, u32[]{:S(2)}) copy-start(bf16[64,384]{1,0:T(8,128)(2,1)} %constant.26.clone.last_ref) | copy-start | bytes 147460
  2.6 33.3 %copy-start.10 = (bf16[128,128]{1,0:T(8,128)(2,1)S(1)}, bf16[128,128]{1,0:T(8,128)(2,1)}, u32[]{:S(2)}) copy-start(bf16[128,128]{1,0:T(8,128)(2,1)} %constant.21.clone.fs_ref) | copy-start | bytes 98308
  2.6 33.3 %copy-start.13 = (bf16[128,192]{1,0:T(8,128)(2,1)S(1)}, bf16[128,192]{1,0:T(8,128)(2,1)}, u32[]{:S(2)}) copy-start(bf16[128,192]{1,0:T(8,128)(2,1)} %constant.22.clone.ff_ref) | copy-start | bytes 147460
  33.3 4.4 %copy-start.2 = (bf16[320,320]{1,0:T(8,128)(2,1)S(1)}, bf16[320,320]{1,0:T(8,128)(2,1)}, u32[]{:S(2)}) copy-start(bf16[320,320]{1,0:T(8,128)(2,1)} %constant.28.clone.back_ref) | copy-start | bytes 614404
  33.3 4.4 %copy-start.7 = (bf16[128,320]{1,0:T(8,128)(2,1)S(1)}, bf16[128,320]{1,0:T(8,128)(2,1)}, u32[]{:S(2)}) copy-start(bf16[128,320]{1,0:T(8,128)(2,1)} %constant.27.clone.order_ref) | copy-start | bytes 245764
  33.4 4.3 %collective-permute-start = (bf16[1280,128]{1,0:T(8,128)(2,1)S(1)}, bf16[1280,128]{1,0:T(8,128)(2,1)S(1)}, u32[]{:S(2)}, u32[]{:S(2)}) collective-permute-start(bf16[1280,128]{1,0:T(8,128)(2,1)S(1)} %bitcast.6), channel_id=1, source_target_pairs={{0,1},{1,0},{2,3},{3,2},{4,5},{5,4},{6,7},{7,6},{8,9},{9,8},{10,11... | collective-permute-start | bytes 983048 | tf_op jit(solution)/shard_map/ppermute | solution.py:333
  37.7 24.6 %copy-start.11 = (bf16[2,640,384]{2,1,0:T(8,128)(2,1)S(1)}, bf16[2,640,384]{2,1,0:T(8,128)(2,1)}, u32[]{:S(2)}) copy-start(bf16[2,640,384]{2,1,0:T(8,128)(2,1)} %constant.29.clone.sort_ref) | copy-start | bytes 2949124
  39.6 22.7 %copy-start.3 = (bf16[1,128,512]{2,1,0:T(8,128)(2,1)S(1)}, bf16[1,128,512]{2,1,0:T(8,128)(2,1)}, u32[]{:S(2)}) copy-start(bf16[1,128,512]{2,1,0:T(8,128)(2,1)} %q_ref.3) | copy-start | bytes 393220
  39.6 22.7 %copy-start.4 = (bf16[1,128,512]{2,1,0:T(8,128)(2,1)S(1)}, bf16[1,128,512]{2,1,0:T(8,128)(2,1)}, u32[]{:S(2)}) copy-start(bf16[1,128,512]{2,1,0:T(8,128)(2,1)} %k_ref.3) | copy-start | bytes 393220
  39.6 22.7 %copy-start.5 = (bf16[1,128,512]{2,1,0:T(8,128)(2,1)S(1)}, bf16[1,128,512]{2,1,0:T(8,128)(2,1)}, u32[]{:S(2)}) copy-start(bf16[1,128,512]{2,1,0:T(8,128)(2,1)} %v_ref.3) | copy-start | bytes 393220
  39.6 22.7 %copy-start.6 = (bf16[1,128,512]{2,1,0:T(8,128)(2,1)S(1)}, bf16[1,128,512]{2,1,0:T(8,128)(2,1)}, u32[]{:S(2)}) copy-start(bf16[1,128,512]{2,1,0:T(8,128)(2,1)} %g_ref.3) | copy-start | bytes 393220
  60.4 3.2 %collective-permute-start.1 = (bf16[1280,128]{1,0:T(8,128)(2,1)S(1)}, bf16[1280,128]{1,0:T(8,128)(2,1)S(1)}, u32[]{:S(2)}, u32[]{:S(2)}) collective-permute-start(bf16[1280,128]{1,0:T(8,128)(2,1)S(1)} %bitcast.8), channel_id=1, source_target_pairs={{0,1},{1,0},{2,3},{3,2},{4,5},{5,4},{6,7},{7,6},{8,9},{9,8},{10,11... | collective-permute-start | bytes 983048 | tf_op jit(solution)/shard_map/ppermute | solution.py:361

commit v7 on v5

--- a/solution.py
+++ b/solution.py
@@ -28,6 +28,8 @@
 CHUNK = PARTS * OWNED
 TILE = GROUP * HALVES * CHUNK
 SWAP = ((0, 1), (1, 0))
+FORWARD_PAIRS = 4
+INVERSE_PAIRS = 5
 
 
 def two_terms(table):
@@ -153,6 +155,12 @@
     return high, low
 
 
+def multiply(lines, size, table_ref, to_ref):
+    for at in range(0, len(lines), size):
+        part = lines[at : at + size]
+        to_ref[2 * at * HALF : 2 * (at + len(part)) * HALF, :] = mm(jnp.concatenate(part, axis=0), table_ref[...])
+
+
 def conv_kernel(
     got_ref,
     order_ref,
@@ -206,7 +214,7 @@
         lines.append(turned(mm(fs_ref[...], jnp.concatenate([data, data], axis=0))))
     terms = [jnp.concatenate([sig(base + own * HALVES + term) for own in range(OWNED)], axis=1) for term in range(2)]
     lines.append(turned(mm(ff_ref[...], jnp.concatenate([terms[0], terms[0], terms[1]], axis=0))))
-    spec_ref[...] = mm(jnp.concatenate(lines, axis=0), sec_ref[...])
+    multiply(lines, FORWARD_PAIRS, sec_ref, spec_ref)
 
     def inverse(full):
         cols = []
@@ -251,7 +259,7 @@
         taps.append(jnp.concatenate([qr, qi], axis=1))
     lines.append(three(jnp.concatenate(taps, axis=0)))
     places.append([[base + own * HALVES + half for half in range(HALVES)] for own in range(OWNED)])
-    inv_ref[...] = mm(jnp.concatenate(lines, axis=0), secb_ref[...])
+    multiply(lines, INVERSE_PAIRS, secb_ref, inv_ref)
     for p, pair in enumerate(places):
         res = inverse(inv_ref[2 * p * HALF : 2 * (p + 1) * HALF, :])
         for u in range(2):

time: 64.4 us -> 63.6 us (0.988)
  Pallas kernels: 7.15 us -> 6.42 us
    pallas_call x1, Pallas kernels: 3.03 us -> 2.3 us  [local(): pl.pallas_call(conv_kernel, out_shape=rows, scratch_shapes=[pltpu.VMEM((B...]
where the time goes in v7:
time: 63.6 us; the launch traced here: 63.4 us
  blocking collectives  48 us (75%)
  starting transfers between devices  7.74 us (12%)
  Pallas kernels  6.42 us (10%)
  between operations  0.84 us (1%)
    all_to_all x2, blocking collectives, exchange(): lax.all_to_all(parts, ('ctx', 'zh'), split_axis=0, concat_axis=0, tiled=T...  48 us
    ppermute x4, starting transfers between devices, local(): other = [lax.ppermute(x, 'core', SWAP) for x in near]  3.94 us
    ppermute x1, starting transfers between devices, local(): swapped = lax.ppermute(returned, 'core', SWAP)  3.8 us
    pallas_call x1, Pallas kernels, local(): pl.pallas_call(conv_kernel, out_shape=rows, scratch_shapes=[pltpu.VMEM((B...  2.3 us
  transfers between devices with their start and end apart: 5, of which 1 were waited for; matrix products, arithmetic and copies ran while one was open for 0% of the time, Pallas kernels for 4%

profile of v7, /device:TPU:1, one launch (start us, length us, event | category | flops | bytes accessed | tf_op | source)
XLA Modules:
  0.0 63.4 jit_solution(480572315501977013)
XLA Ops:
  0.6 0.0 copy-start.2
  0.6 3.3 %collective-permute-start = (bf16[1,128,512]{2,1,0:T(8,128)(2,1)}, bf16[1,128,512]{2,1,0:T(8,128)(2,1)S(1)}, u32[]{:S(2)}, u32[]{:S(2)}) collective-permute-start(bf16[1,128,512]{2,1,0:T(8,128)(2,1)} %q_ref.3), channel_id=1, source_target_pairs={{0,1},{1,0},{2,3},{3,2},{4,5},{5,4},{6,7},{7,6},{8,9},{9,8},{10,11... | collective-permute-start | bytes 393224 | tf_op jit(solution)/shard_map/ppermute | solution.py:288
  4.0 0.1 collective-permute-start.1
  4.1 0.4 collective-permute-start.2
  4.5 0.1 collective-permute-start.3
  4.6 1.2 %gate.1 = (bf16[2,128,512]{2,1,0:T(8,128)(2,1)S(1)}, bf16[640,640]{1,0:T(8,128)(2,1)S(1)}) custom-call(bf16[1,128,512]{2,1,0:T(8,128)(2,1)} %q_ref.3, bf16[1,128,512]{2,1,0:T(8,128)(2,1)} %k_ref.3, bf16[1,128,512]{2,1,0:T(8,128)(2,1)} %v_ref.3, bf16[1,128,512]{2,1,0:T(8,128)(2,1)} %g_ref.3), custom_call_target="tpu_custom_call" | custom-call | flops 1000000000 | bytes 2000000 | tf_op jit(solution)/shard_map/gate/pallas_call | solution.py:290
  5.8 0.0 collective-permute-done.q_ref
  5.8 0.0 collective-permute-done.1.k_ref
  5.8 0.0 collective-permute-done.2.v_ref
  5.8 0.3 collective-permute-done.3.g_ref
  6.0 0.0 copy-done.2
  6.1 0.0 copy-start.6
  6.1 0.0 copy-start.7
  6.1 0.0 copy-start.8
  6.1 0.6 pack.1
  6.7 0.0 copy-start
  6.7 0.0 copy-start.3
  6.7 28.5 %all_to_all.10 = bf16[640,2,128]{2,1,0:T(2,128)(2,1)S(1)} all-to-all(bf16[640,2,128]{2,1,0:T(2,128)(2,1)S(1)} %bitcast.6), channel_id=1, replica_groups=mesh['ctx'=64,'zh'=2,'core'=2] {'ctx','zh'}, dimensions={0} | all-to-all | bytes 655360 | tf_op jit(solution)/shard_map/all_to_all | solution.py:279
  35.3 0.0 copy-done.1
  35.3 0.0 copy-done.4
  35.3 0.0 copy-start.13
  35.4 2.3 %conv.1 = bf16[1280,128]{1,0:T(8,128)(2,1)S(1)} custom-call(bf16[1280,128]{1,0:T(8,128)(2,1)S(1)} %bitcast.4, bf16[320,320]{1,0:T(8,128)(2,1)S(1)} %copy-done.4, bf16[320,320]{1,0:T(8,128)(2,1)S(1)} %copy-done.3, bf16[128,128]{1,0:T(8,128)(2,1)S(1)} %copy-done.8, bf16[128,192]{1,0:T(8,128)(2,1)S(1)} %copy-done.6, f32[128,128]{1,0:T(8,128)S(1)} %copy-done.5, ...), custom_call_target="tpu_custom_call" | custom-call | tf_op jit(solution)/shard_map/conv/pallas_call | solution.py:305
  37.7 0.0 copy-start.9
  37.7 0.0 copy-start.10
  37.7 0.0 copy-start.11
  37.7 0.0 copy-start.12
  37.7 19.5 %all_to_all.11 = bf16[640,2,128]{2,1,0:T(2,128)(2,1)S(1)} all-to-all(bf16[640,2,128]{2,1,0:T(2,128)(2,1)S(1)} %bitcast.5), channel_id=1, replica_groups=mesh['ctx'=64,'zh'=2,'core'=2] {'ctx','zh'}, dimensions={0} | all-to-all | bytes 655360 | tf_op jit(solution)/shard_map/all_to_all | solution.py:279
  57.2 3.8 %collective-permute-start.4 = (bf16[1280,128]{1,0:T(8,128)(2,1)S(1)}, bf16[1280,128]{1,0:T(8,128)(2,1)S(1)}, u32[]{:S(2)}, u32[]{:S(2)}) collective-permute-start(bf16[1280,128]{1,0:T(8,128)(2,1)S(1)} %bitcast.7), channel_id=1, source_target_pairs={{0,1},{1,0},{2,3},{3,2},{4,5},{5,4},{6,7},{7,6},{8,9},{9,8},{10,11... | collective-permute-start | bytes 983048 | tf_op jit(solution)/shard_map/ppermute | solution.py:318
  61.0 0.0 copy-done.10
  61.0 1.2 %unpack_own.1 = (bf16[1,128,512]{2,1,0:T(8,128)(2,1)}, bf16[1,128,512]{2,1,0:T(8,128)(2,1)}, bf16[1,128,512]{2,1,0:T(8,128)(2,1)}, bf16[1,128,512]{2,1,0:T(8,128)(2,1)}, f32[128,512]{1,0:T(8,128)}) custom-call(bf16[1,128,512]{2,1,0:T(8,128)(2,1)S(1)} %copy-done.9, bf16[1,128,512]{2,1,0:T(8,128)(2,1)S(1)} %copy-done.10, bf16[1,128,512]{2,1,0:T(8,128)(2,1)S(1)} %copy-done.11, ...), custom_call_target="tpu_custom_call" | custom-call | flops 1000000000 | bytes 2000000 | tf_op jit(solution)/shard_map/unpack_own/pallas_call | solution.py:332
  62.2 0.0 collective-permute-done.4.got_ref
  62.3 1.2 %unpack_other.1 = (bf16[1,128,512]{2,1,0:T(8,128)(2,1)}, bf16[1,128,512]{2,1,0:T(8,128)(2,1)}, bf16[1,128,512]{2,1,0:T(8,128)(2,1)}, bf16[1,128,512]{2,1,0:T(8,128)(2,1)}, f32[128,512]{1,0:T(8,128)}) custom-call(bf16[1,128,512]{2,1,0:T(8,128)(2,1)S(1)} %copy-done.9, ...), custom_call_target="tpu_custom_call", output_to_operand_aliasing={{0}: (6, {}), {1}: (7, {}), {2}: (8, {}), {3}: (9, {}), {4}... | custom-call | flops 1000000000 | bytes 2000000 | tf_op jit(solution)/shard_map/unpack_other/pallas_call | solution.py:334
  (13 shorter events, 0.0 us)
Async XLA Ops:
  0.6 5.4 %copy-start.2 = (f32[128,512]{1,0:T(8,128)S(1)}, f32[128,512]{1,0:T(8,128)}, u32[]{:S(2)}) copy-start(f32[128,512]{1,0:T(8,128)} %f_ref.1) | copy-start | bytes 786436
  0.6 5.1 %collective-permute-start = (bf16[1,128,512]{2,1,0:T(8,128)(2,1)}, bf16[1,128,512]{2,1,0:T(8,128)(2,1)S(1)}, u32[]{:S(2)}, u32[]{:S(2)}) collective-permute-start(bf16[1,128,512]{2,1,0:T(8,128)(2,1)} %q_ref.3), channel_id=1, source_target_pairs={{0,1},{1,0},{2,3},{3,2},{4,5},{5,4},{6,7},{7,6},{8,9},{9,8},{10,11... | collective-permute-start | bytes 393224 | tf_op jit(solution)/shard_map/ppermute | solution.py:288
  4.0 1.8 %collective-permute-start.1 = (bf16[1,128,512]{2,1,0:T(8,128)(2,1)}, bf16[1,128,512]{2,1,0:T(8,128)(2,1)S(1)}, u32[]{:S(2)}, u32[]{:S(2)}) collective-permute-start(bf16[1,128,512]{2,1,0:T(8,128)(2,1)} %k_ref.3), channel_id=1, source_target_pairs={{0,1},{1,0},{2,3},{3,2},{4,5},{5,4},{6,7},{7,6},{8,9},{9,8},{10,11... | collective-permute-start | bytes 393224 | tf_op jit(solution)/shard_map/ppermute | solution.py:288
  4.1 1.7 %collective-permute-start.2 = (bf16[1,128,512]{2,1,0:T(8,128)(2,1)}, bf16[1,128,512]{2,1,0:T(8,128)(2,1)S(1)}, u32[]{:S(2)}, u32[]{:S(2)}) collective-permute-start(bf16[1,128,512]{2,1,0:T(8,128)(2,1)} %v_ref.3), channel_id=1, source_target_pairs={{0,1},{1,0},{2,3},{3,2},{4,5},{5,4},{6,7},{7,6},{8,9},{9,8},{10,11... | collective-permute-start | bytes 393224 | tf_op jit(solution)/shard_map/ppermute | solution.py:288
  4.5 1.6 %collective-permute-start.3 = (bf16[1,128,512]{2,1,0:T(8,128)(2,1)}, bf16[1,128,512]{2,1,0:T(8,128)(2,1)S(1)}, u32[]{:S(2)}, u32[]{:S(2)}) collective-permute-start(bf16[1,128,512]{2,1,0:T(8,128)(2,1)} %g_ref.3), channel_id=1, source_target_pairs={{0,1},{1,0},{2,3},{3,2},{4,5},{5,4},{6,7},{7,6},{8,9},{9,8},{10,11... | collective-permute-start | bytes 393224 | tf_op jit(solution)/shard_map/ppermute | solution.py:288
  6.0 29.2 %copy-start.1 = (bf16[768,256]{1,0:T(8,128)(2,1)S(1)}, bf16[768,256]{1,0:T(8,128)(2,1)}, u32[]{:S(2)}) copy-start(bf16[768,256]{1,0:T(8,128)(2,1)} %constant.23.clone.sec_ref) | copy-start | bytes 1179652
  6.0 29.2 %copy-start.4 = (bf16[320,320]{1,0:T(8,128)(2,1)S(1)}, bf16[320,320]{1,0:T(8,128)(2,1)}, u32[]{:S(2)}) copy-start(bf16[320,320]{1,0:T(8,128)(2,1)} %constant.18.clone.order_ref) | copy-start | bytes 614404
  6.0 29.2 %copy-start.5 = (f32[128,128]{1,0:T(8,128)S(1)}, f32[128,128]{1,0:T(8,128)}, u32[]{:S(2)}) copy-start(f32[128,128]{1,0:T(8,128)} %constant.22.clone.tw_ref) | copy-start | bytes 196612
  6.1 29.2 %copy-start.6 = (bf16[128,192]{1,0:T(8,128)(2,1)S(1)}, bf16[128,192]{1,0:T(8,128)(2,1)}, u32[]{:S(2)}) copy-start(bf16[128,192]{1,0:T(8,128)(2,1)} %constant.21.clone.ff_ref) | copy-start | bytes 147460
  6.1 29.2 %copy-start.7 = (bf16[64,384]{1,0:T(8,128)(2,1)S(1)}, bf16[64,384]{1,0:T(8,128)(2,1)}, u32[]{:S(2)}) copy-start(bf16[64,384]{1,0:T(8,128)(2,1)} %constant.25.clone.last_ref) | copy-start | bytes 147460
  6.1 29.2 %copy-start.8 = (bf16[128,128]{1,0:T(8,128)(2,1)S(1)}, bf16[128,128]{1,0:T(8,128)(2,1)}, u32[]{:S(2)}) copy-start(bf16[128,128]{1,0:T(8,128)(2,1)} %constant.20.clone.fs_ref) | copy-start | bytes 98308
  6.7 28.6 %copy-start = (bf16[768,256]{1,0:T(8,128)(2,1)S(1)}, bf16[768,256]{1,0:T(8,128)(2,1)}, u32[]{:S(2)}) copy-start(bf16[768,256]{1,0:T(8,128)(2,1)} %constant.24.clone.secb_ref) | copy-start | bytes 1179652
  6.7 28.6 %copy-start.3 = (bf16[320,320]{1,0:T(8,128)(2,1)S(1)}, bf16[320,320]{1,0:T(8,128)(2,1)}, u32[]{:S(2)}) copy-start(bf16[320,320]{1,0:T(8,128)(2,1)} %constant.19.clone.back_ref) | copy-start | bytes 614404
  35.3 25.7 %copy-start.13 = (bf16[2,640,384]{2,1,0:T(8,128)(2,1)S(1)}, bf16[2,640,384]{2,1,0:T(8,128)(2,1)}, u32[]{:S(2)}) copy-start(bf16[2,640,384]{2,1,0:T(8,128)(2,1)} %constant.26.clone.sort_ref) | copy-start | bytes 2949124
  37.7 23.4 %copy-start.9 = (bf16[1,128,512]{2,1,0:T(8,128)(2,1)S(1)}, bf16[1,128,512]{2,1,0:T(8,128)(2,1)}, u32[]{:S(2)}) copy-start(bf16[1,128,512]{2,1,0:T(8,128)(2,1)} %q_ref.3) | copy-start | bytes 393220
  37.7 23.3 %copy-start.10 = (bf16[1,128,512]{2,1,0:T(8,128)(2,1)S(1)}, bf16[1,128,512]{2,1,0:T(8,128)(2,1)}, u32[]{:S(2)}) copy-start(bf16[1,128,512]{2,1,0:T(8,128)(2,1)} %k_ref.3) | copy-start | bytes 393220
  37.7 23.3 %copy-start.11 = (bf16[1,128,512]{2,1,0:T(8,128)(2,1)S(1)}, bf16[1,128,512]{2,1,0:T(8,128)(2,1)}, u32[]{:S(2)}) copy-start(bf16[1,128,512]{2,1,0:T(8,128)(2,1)} %v_ref.3) | copy-start | bytes 393220
  37.7 23.3 %copy-start.12 = (bf16[1,128,512]{2,1,0:T(8,128)(2,1)S(1)}, bf16[1,128,512]{2,1,0:T(8,128)(2,1)}, u32[]{:S(2)}) copy-start(bf16[1,128,512]{2,1,0:T(8,128)(2,1)} %g_ref.3) | copy-start | bytes 393220
  57.2 5.1 %collective-permute-start.4 = (bf16[1280,128]{1,0:T(8,128)(2,1)S(1)}, bf16[1280,128]{1,0:T(8,128)(2,1)S(1)}, u32[]{:S(2)}, u32[]{:S(2)}) collective-permute-start(bf16[1280,128]{1,0:T(8,128)(2,1)S(1)} %bitcast.7), channel_id=1, source_target_pairs={{0,1},{1,0},{2,3},{3,2},{4,5},{5,4},{6,7},{7,6},{8,9},{9,8},{10,11... | collective-permute-start | bytes 983048 | tf_op jit(solution)/shard_map/ppermute | solution.py:318

commit v8 on v6

--- a/solution.py
+++ b/solution.py
@@ -163,6 +163,12 @@
     return jnp.concatenate([high, low, high], axis=1)
 
 
+def multiply(lines, size, table_ref, to_ref):
+    for at in range(0, len(lines), size):
+        part = lines[at : at + size]
+        to_ref[2 * at * HALF : 2 * (at + len(part)) * HALF, :] = mm(jnp.concatenate(part, axis=0), table_ref[...])
+
+
 def sort_signals(got_ref, order_ref, sig_ref):
     order = order_ref[...]
     for h in range(2):
@@ -248,14 +254,14 @@
         places = [SETS * LANES + (own * HALVES + term) * LANES for own in range(OWNED)]
         terms.append(jnp.concatenate([sig_ref[:, at : at + LANES] for at in places], axis=1))
     lines.append(turned(mm(ff_ref[...], jnp.concatenate([terms[0], terms[0], terms[1]], axis=0)), tw_ref))
-    spec_ref[...] = mm(jnp.concatenate(lines, axis=0), sec_ref[...])
+    multiply(lines, 3, sec_ref, spec_ref)
     filter_ref[...] = spec_ref[SETS * HALF :, :]
     zero = jnp.zeros((HALF, LANES), F32)
     sums = [(zero, zero) for _ in range(OWNED)]
     lines = multiplied(spec_ref, spec_ref, SETS * HALF, sums)
     for own in range(OWNED):
         sum_ref[own * HALF : (own + 1) * HALF, :] = jnp.concatenate(sums[own], axis=1)
-    inv_ref[...] = mm(jnp.concatenate(lines, axis=0), secb_ref[...])
+    multiply(lines, 2, secb_ref, inv_ref)
     for p in range(SETS // 2):
         res = inverse(inv_ref[2 * p * HALF : 2 * (p + 1) * HALF, :], tw_ref, last_ref)
         for u in range(2):
@@ -281,14 +287,14 @@
     fin_ref,
 ):
     sort_signals(got_ref, order_ref, sig_ref)
-    spec_ref[...] = mm(jnp.concatenate(forward_lines(sig_ref, fs_ref, tw_ref), axis=0), sec_ref[...])
+    multiply(forward_lines(sig_ref, fs_ref, tw_ref), 2, sec_ref, spec_ref)
     sums = []
     for own in range(OWNED):
         found = sum_ref[own * HALF : (own + 1) * HALF, :]
         sums.append((found[:, :LANES], found[:, LANES:]))
     lines = multiplied(spec_ref, filter_ref, 0, sums)
     lines.append(three(jnp.concatenate([jnp.concatenate(pair, axis=1) for pair in sums], axis=0)))
-    inv_ref[...] = mm(jnp.concatenate(lines, axis=0), secb_ref[...])
+    multiply(lines, 3, secb_ref, inv_ref)
     for p in range(SETS // 2 + 1):
         res = inverse(inv_ref[2 * p * HALF : 2 * (p + 1) * HALF, :], tw_ref, last_ref)
         for u in range(2):

time: 64.9 us -> 64.4 us (level)
  transfers between devices with their start and end apart: 2 -> 2, of which waited for: 0 -> 1; matrix products, arithmetic and copies ran while one was open for 0% -> 0% of each run, Pallas kernels for 4% -> 4%
where the time goes in v8:
time: 64.4 us; the launch traced here: 64.2 us
  blocking collectives  51.2 us (80%)
  Pallas kernels  7.26 us (11%)
  starting transfers between devices  4.72 us (7%)
  between operations  0.83 us (1%)
    all_to_all x2, blocking collectives, exchange(): lax.all_to_all(parts, ('ctx', 'zh'), split_axis=0, concat_axis=0, tiled=T...  51.2 us
    ppermute x1, starting transfers between devices, local(): other = lax.ppermute(got, 'core', SWAP)  2.57 us
    ppermute x1, starting transfers between devices, local(): swapped = lax.ppermute(returned, 'core', SWAP)  2.15 us
    pallas_call x1, Pallas kernels, local(): pl.pallas_call(pack_kernel, out_shape=rows, in_specs=[hbm] * 5, scratch_s...  1.91 us
    pallas_call x1, Pallas kernels, local(): pl.pallas_call(conv_other_kernel, out_shape=rows, scratch_shapes=[pltpu.V...  1.65 us
    pallas_call x1, Pallas kernels, local(): pl.pallas_call(conv_own_kernel, out_shape=(pair, pair, jax.ShapeDtypeStru...  1.36 us
  transfers between devices with their start and end apart: 2, of which 1 were waited for; matrix products, arithmetic and copies ran while one was open for 0% of the time, Pallas kernels for 4%

profile of v8, /device:TPU:1, one launch (start us, length us, event | category | flops | bytes accessed | tf_op | source)
XLA Modules:
  0.0 64.2 jit_solution(12343531894655832924)
XLA Ops:
  0.6 0.0 copy-start.1
  0.6 0.0 copy-start.12
  0.7 1.9 %pack.1 = bf16[1280,128]{1,0:T(8,128)(2,1)S(1)} custom-call(bf16[1,128,512]{2,1,0:T(8,128)(2,1)} %q_ref.3, bf16[1,128,512]{2,1,0:T(8,128)(2,1)} %k_ref.3, bf16[1,128,512]{2,1,0:T(8,128)(2,1)} %v_ref.3, f32[128,512]{1,0:T(8,128)} %f_hbm.1, bf16[1,128,512]{2,1,0:T(8,128)(2,1)} %g_ref.3), custom_call_target="tpu_custom_call" | custom-call | tf_op jit(solution)/shard_map/pack/pallas_call | solution.py:325
  2.6 0.0 copy-start
  2.6 0.0 copy-start.8
  2.6 0.0 copy-start.9
  2.6 0.0 copy-start.10
  2.6 0.0 copy-start.13
  2.6 30.7 %all_to_all.10 = bf16[640,2,128]{2,1,0:T(2,128)(2,1)S(1)} all-to-all(bf16[640,2,128]{2,1,0:T(2,128)(2,1)S(1)} %bitcast.5), channel_id=1, replica_groups=mesh['ctx'=64,'zh'=2,'core'=2] {'ctx','zh'}, dimensions={0} | all-to-all | bytes 655360 | tf_op jit(solution)/shard_map/all_to_all | solution.py:314
  33.4 2.6 %collective-permute-start = (bf16[1280,128]{1,0:T(8,128)(2,1)S(1)}, bf16[1280,128]{1,0:T(8,128)(2,1)S(1)}, u32[]{:S(2)}, u32[]{:S(2)}) collective-permute-start(bf16[1280,128]{1,0:T(8,128)(2,1)S(1)} %bitcast.6), channel_id=1, source_target_pairs={{0,1},{1,0},{2,3},{3,2},{4,5},{5,4},{6,7},{7,6},{8,9},{9,8},{10,11... | collective-permute-start | bytes 983048 | tf_op jit(solution)/shard_map/ppermute | solution.py:339
  35.9 0.0 copy-done.1
  35.9 0.0 copy-done.12
  35.9 0.0 copy-done
  35.9 0.0 copy-done.8
  35.9 0.0 copy-done.9
  35.9 0.0 copy-done.10
  36.0 1.4 %conv_own.1 = (f32[128,256]{1,0:T(8,128)S(1)}, f32[128,256]{1,0:T(8,128)S(1)}, bf16[2,128,256]{2,1,0:T(8,128)(2,1)S(1)}) custom-call(bf16[1280,128]{1,0:T(8,128)(2,1)S(1)} %bitcast.7, bf16[192,320]{1,0:T(8,128)(2,1)S(1)} %copy-done.12, bf16[128,128]{1,0:T(8,128)(2,1)S(1)} %copy-done.10, bf16[128,192]{1,0:T(8,128)(2,1)S(1)} %copy-done.13, ...), custom_call_target="tpu_custom_call" | custom-call | flops 2000000000 | bytes 4000000 | tf_op jit(solution)/shard_map/conv_own/pallas_call | solution.py:342
  37.3 0.0 collective-permute-done.got_ref
  37.3 0.0 copy-done.2
  37.4 0.0 copy-done.7
  37.4 0.0 copy-start.11
  37.4 1.7 %conv_other.1 = bf16[1280,128]{1,0:T(8,128)(2,1)S(1)} custom-call(bf16[1280,128]{1,0:T(8,128)(2,1)S(1)} %collective-permute-done.got_ref, f32[128,256]{1,0:T(8,128)S(1)} %get-tuple-element.13.filter_ref, f32[128,256]{1,0:T(8,128)S(1)} %get-tuple-element.14.sum_ref, bf16[2,128,256]{2,1,0:T(8,128)(2,1)S(1)} %get-tuple-element.15.done_ref, ...), custom_call_target="tpu_custom_call" | custom-call | tf_op jit(solution)/shard_map/conv_other/pallas_call | solution.py:354
  39.0 0.0 copy-start.3
  39.0 0.0 copy-start.4
  39.1 0.0 copy-start.5
  39.1 0.0 copy-start.6
  39.1 20.5 %all_to_all.11 = bf16[640,2,128]{2,1,0:T(2,128)(2,1)S(1)} all-to-all(bf16[640,2,128]{2,1,0:T(2,128)(2,1)S(1)} %bitcast.4), channel_id=1, replica_groups=mesh['ctx'=64,'zh'=2,'core'=2] {'ctx','zh'}, dimensions={0} | all-to-all | bytes 655360 | tf_op jit(solution)/shard_map/all_to_all | solution.py:314
  59.6 2.1 %collective-permute-start.1 = (bf16[1280,128]{1,0:T(8,128)(2,1)S(1)}, bf16[1280,128]{1,0:T(8,128)(2,1)S(1)}, u32[]{:S(2)}, u32[]{:S(2)}) collective-permute-start(bf16[1280,128]{1,0:T(8,128)(2,1)S(1)} %bitcast.8), channel_id=1, source_target_pairs={{0,1},{1,0},{2,3},{3,2},{4,5},{5,4},{6,7},{7,6},{8,9},{9,8},{10,11... | collective-permute-start | bytes 983048 | tf_op jit(solution)/shard_map/ppermute | solution.py:367
  61.7 0.0 copy-done.4
  61.8 1.2 %unpack_own.1 = (bf16[1,128,512]{2,1,0:T(8,128)(2,1)}, bf16[1,128,512]{2,1,0:T(8,128)(2,1)}, bf16[1,128,512]{2,1,0:T(8,128)(2,1)}, bf16[1,128,512]{2,1,0:T(8,128)(2,1)}, f32[128,512]{1,0:T(8,128)}) custom-call(bf16[1,128,512]{2,1,0:T(8,128)(2,1)S(1)} %copy-done.3, bf16[1,128,512]{2,1,0:T(8,128)(2,1)S(1)} %copy-done.4, bf16[1,128,512]{2,1,0:T(8,128)(2,1)S(1)} %copy-done.5, ...), custom_call_target="tpu_custom_call" | custom-call | flops 1000000000 | bytes 2000000 | tf_op jit(solution)/shard_map/unpack_own/pallas_call | solution.py:381
  62.9 0.1 collective-permute-done.1.got_ref
  63.0 1.2 %unpack_other.1 = (bf16[1,128,512]{2,1,0:T(8,128)(2,1)}, bf16[1,128,512]{2,1,0:T(8,128)(2,1)}, bf16[1,128,512]{2,1,0:T(8,128)(2,1)}, bf16[1,128,512]{2,1,0:T(8,128)(2,1)}, f32[128,512]{1,0:T(8,128)}) custom-call(bf16[1,128,512]{2,1,0:T(8,128)(2,1)S(1)} %copy-done.3, ...), custom_call_target="tpu_custom_call", output_to_operand_aliasing={{0}: (6, {}), {1}: (7, {}), {2}: (8, {}), {3}: (9, {}), {4}... | custom-call | flops 1000000000 | bytes 2000000 | tf_op jit(solution)/shard_map/unpack_other/pallas_call | solution.py:383
  (7 shorter events, 0.0 us)
Async XLA Ops:
  0.6 35.3 %copy-start.1 = (bf16[768,256]{1,0:T(8,128)(2,1)S(1)}, bf16[768,256]{1,0:T(8,128)(2,1)}, u32[]{:S(2)}) copy-start(bf16[768,256]{1,0:T(8,128)(2,1)} %constant.24.clone.sec_ref) | copy-start | bytes 1179652
  0.6 35.3 %copy-start.12 = (bf16[192,320]{1,0:T(8,128)(2,1)S(1)}, bf16[192,320]{1,0:T(8,128)(2,1)}, u32[]{:S(2)}) copy-start(bf16[192,320]{1,0:T(8,128)(2,1)} %constant.20.clone.order_ref) | copy-start | bytes 368644
  2.6 33.4 %copy-start = (bf16[768,256]{1,0:T(8,128)(2,1)S(1)}, bf16[768,256]{1,0:T(8,128)(2,1)}, u32[]{:S(2)}) copy-start(bf16[768,256]{1,0:T(8,128)(2,1)} %constant.25.clone.secb_ref) | copy-start | bytes 1179652
  2.6 33.3 %copy-start.8 = (f32[128,128]{1,0:T(8,128)S(1)}, f32[128,128]{1,0:T(8,128)}, u32[]{:S(2)}) copy-start(f32[128,128]{1,0:T(8,128)} %constant.23.clone.tw_ref) | copy-start | bytes 196612
  2.6 33.3 %copy-start.9 = (bf16[64,384]{1,0:T(8,128)(2,1)S(1)}, bf16[64,384]{1,0:T(8,128)(2,1)}, u32[]{:S(2)}) copy-start(bf16[64,384]{1,0:T(8,128)(2,1)} %constant.26.clone.last_ref) | copy-start | bytes 147460
  2.6 33.3 %copy-start.10 = (bf16[128,128]{1,0:T(8,128)(2,1)S(1)}, bf16[128,128]{1,0:T(8,128)(2,1)}, u32[]{:S(2)}) copy-start(bf16[128,128]{1,0:T(8,128)(2,1)} %constant.21.clone.fs_ref) | copy-start | bytes 98308
  2.6 33.3 %copy-start.13 = (bf16[128,192]{1,0:T(8,128)(2,1)S(1)}, bf16[128,192]{1,0:T(8,128)(2,1)}, u32[]{:S(2)}) copy-start(bf16[128,192]{1,0:T(8,128)(2,1)} %constant.22.clone.ff_ref) | copy-start | bytes 147460
  33.3 4.0 %copy-start.2 = (bf16[320,320]{1,0:T(8,128)(2,1)S(1)}, bf16[320,320]{1,0:T(8,128)(2,1)}, u32[]{:S(2)}) copy-start(bf16[320,320]{1,0:T(8,128)(2,1)} %constant.28.clone.back_ref) | copy-start | bytes 614404
  33.3 4.0 %copy-start.7 = (bf16[128,320]{1,0:T(8,128)(2,1)S(1)}, bf16[128,320]{1,0:T(8,128)(2,1)}, u32[]{:S(2)}) copy-start(bf16[128,320]{1,0:T(8,128)(2,1)} %constant.27.clone.order_ref) | copy-start | bytes 245764
  33.4 4.0 %collective-permute-start = (bf16[1280,128]{1,0:T(8,128)(2,1)S(1)}, bf16[1280,128]{1,0:T(8,128)(2,1)S(1)}, u32[]{:S(2)}, u32[]{:S(2)}) collective-permute-start(bf16[1280,128]{1,0:T(8,128)(2,1)S(1)} %bitcast.6), channel_id=1, source_target_pairs={{0,1},{1,0},{2,3},{3,2},{4,5},{5,4},{6,7},{7,6},{8,9},{9,8},{10,11... | collective-permute-start | bytes 983048 | tf_op jit(solution)/shard_map/ppermute | solution.py:339
  37.4 24.4 %copy-start.11 = (bf16[2,640,384]{2,1,0:T(8,128)(2,1)S(1)}, bf16[2,640,384]{2,1,0:T(8,128)(2,1)}, u32[]{:S(2)}) copy-start(bf16[2,640,384]{2,1,0:T(8,128)(2,1)} %constant.29.clone.sort_ref) | copy-start | bytes 2949124
  39.0 22.7 %copy-start.3 = (bf16[1,128,512]{2,1,0:T(8,128)(2,1)S(1)}, bf16[1,128,512]{2,1,0:T(8,128)(2,1)}, u32[]{:S(2)}) copy-start(bf16[1,128,512]{2,1,0:T(8,128)(2,1)} %q_ref.3) | copy-start | bytes 393220
  39.0 22.7 %copy-start.4 = (bf16[1,128,512]{2,1,0:T(8,128)(2,1)S(1)}, bf16[1,128,512]{2,1,0:T(8,128)(2,1)}, u32[]{:S(2)}) copy-start(bf16[1,128,512]{2,1,0:T(8,128)(2,1)} %k_ref.3) | copy-start | bytes 393220
  39.1 22.7 %copy-start.5 = (bf16[1,128,512]{2,1,0:T(8,128)(2,1)S(1)}, bf16[1,128,512]{2,1,0:T(8,128)(2,1)}, u32[]{:S(2)}) copy-start(bf16[1,128,512]{2,1,0:T(8,128)(2,1)} %v_ref.3) | copy-start | bytes 393220
  39.1 22.7 %copy-start.6 = (bf16[1,128,512]{2,1,0:T(8,128)(2,1)S(1)}, bf16[1,128,512]{2,1,0:T(8,128)(2,1)}, u32[]{:S(2)}) copy-start(bf16[1,128,512]{2,1,0:T(8,128)(2,1)} %g_ref.3) | copy-start | bytes 393220
  59.6 3.4 %collective-permute-start.1 = (bf16[1280,128]{1,0:T(8,128)(2,1)S(1)}, bf16[1280,128]{1,0:T(8,128)(2,1)S(1)}, u32[]{:S(2)}, u32[]{:S(2)}) collective-permute-start(bf16[1280,128]{1,0:T(8,128)(2,1)S(1)} %bitcast.8), channel_id=1, source_target_pairs={{0,1},{1,0},{2,3},{3,2},{4,5},{5,4},{6,7},{7,6},{8,9},{9,8},{10,11... | collective-permute-start | bytes 983048 | tf_op jit(solution)/shard_map/ppermute | solution.py:367
